TPU v7x, 256 devices: a whole 4x4x8 slice. The times are simulated.
256 devices in a mesh: row: 32 (over x, z), col: 8 (over y, core).
Axes of the slice: x: 4, y: 4, z: 8, core: 2. Of those that a mesh axis runs over, the one named last changes fastest.
Arguments:
- front_tiles: bfloat16 [4, 8192, 2, 2048], P(None, 'row', None, 'col'), may hold values from -6 to 6
- fill_pattern: int32 [4, 32, 2, 8], P(None, 'row', None, 'col'), may hold values from 0 to 1
- w_inverse: bfloat16 [2, 256, 256], replicated, may hold values from -0.015625 to 0.015625
- samples: bfloat16 [4, 8192, 512], P(None, 'row'), may hold values from -6 to 6
Outputs:
- factor_slab: bfloat16 [4, 8192, 2, 2048], P(None, 'row', None, 'col')
- solved_rows: bfloat16 [4, 8192, 512], P(None, 'row')
All inputs are finite; a program needn't handle non-finite values.
Results may differ from a plain program's by a relative error of at most 0.0062.
Values may be sent and summed in bfloat16 or wider, within the bound.
No kernel may reach another device: no remote copies, remote signals or barrier semaphores. Data moves between devices by JAX's collectives and lax.ppermute only.
A program may use at most 64 MiB of HBM per device.

v0:
```python
import jax
import jax.numpy as jnp
from jax import lax
from jax.experimental import pallas as pl
from jax.experimental.pallas import tpu as pltpu
from jax.sharding import Mesh, PartitionSpec as P


X, Z, Y, K = 4, 8, 4, 2
T = 256
TR = 4
TC = 2
Q = X * Y
RB = T // Q
F32, BF16 = jnp.float32, jnp.bfloat16


def swap(v):
    return lax.ppermute(v, "core", [(0, 1), (1, 0)])


def mm(a, b):
    return lax.dot_general(a, b, (((1,), (0,)), ((), ())), preferred_element_type=F32)


def mmt(a, b):
    return lax.dot_general(a, b, (((1,), (1,)), ((), ())), preferred_element_type=F32)


def keep(cond, value):
    return jnp.where(cond, value, jnp.zeros_like(value))


def finish(k, place, fill, f0, f1, g0, g1, w, wt, m, samples, slab, solved, lrow, lcol, ys, obuf, sem):
    row_pos = place[0]
    col_pos = place[1]

    def tile(ref, at):
        return ref[:, at * RB : (at + 1) * RB, :].reshape(T, T)

    l0_one = mm(tile(g0, 4), w[0]).astype(BF16)

    for half, g in enumerate((g0, g1)):
        y0 = mm(wt[0], tile(g, 5)).astype(BF16)
        r1 = (tile(g, 6).astype(F32) - mm(l0_one, y0)).astype(BF16)
        y1 = mm(wt[1], r1).astype(BF16)
        ys[0:T, half * T : (half + 1) * T] = y0
        ys[T : 2 * T, half * T : (half + 1) * T] = y1

    for a in range(TR):
        index = a * X * Z + row_pos
        first = mm(f0[a], w[0]).astype(BF16)
        if a == 0:
            first = keep(index >= 1, first)
        second = (f1[a].astype(F32) - mmt(first, l0_one)).astype(BF16)
        third = mm(second, w[1]).astype(BF16)
        if a == 0:
            third = keep(index >= 2, third)
        lrow[a * T : (a + 1) * T, 0:T] = first
        lrow[a * T : (a + 1) * T, T : 2 * T] = third
        if a == 0:
            slab[0, 0] = second

    for a in range(TR):
        rest = samples[a].astype(F32) - mm(lrow[a * T : (a + 1) * T, :], ys[...])
        obuf[a] = rest.astype(BF16)
        if a == 0:

            @pl.when(row_pos == 0)
            def _():
                obuf[0] = ys[0:T, :]

            @pl.when(row_pos == 1)
            def _():
                obuf[0] = ys[T : 2 * T, :]

        pltpu.make_async_copy(obuf.at[a], solved.at[a], sem.at[a]).start()

    for b in range(TC):
        index = b * Y * K + col_pos
        first = mm(tile(g0, 2 * k + b), w[0]).astype(BF16)
        if b == 0:
            first = keep(index >= 1, first)
        second = (tile(g1, 2 * k + b).astype(F32) - mmt(first, l0_one)).astype(BF16)
        third = mm(second, w[1]).astype(BF16)
        if b == 0:
            third = keep(index >= 2, third)
        lcol[b * T : (b + 1) * T, 0:T] = first
        lcol[b * T : (b + 1) * T, T : 2 * T] = third

    for a in range(TR):
        index = a * X * Z + row_pos
        rows = lrow[a * T : (a + 1) * T, :]
        for b in range(TC):
            if b == 0:

                @pl.when(col_pos == 0)
                def _():
                    slab[0, a] = rows[:, 0:T]

                    if a == 0:

                        @pl.when(index < 1)
                        def _():
                            slab[0, a] = f0[a]

                @pl.when(col_pos == 1)
                def _():
                    if a == 0:

                        @pl.when(index >= 2)
                        def _():
                            slab[0, a] = rows[:, T : 2 * T]

                    else:
                        slab[0, a] = rows[:, T : 2 * T]

                @pl.when(col_pos >= 2)
                def _():
                    rest = m[0, a].astype(F32) - mmt(rows, lcol[0:T, :])
                    slab[0, a] = keep(fill[2 * a] != 0, rest.astype(BF16))

            else:
                rest = m[b, a].astype(F32) - mmt(rows, lcol[b * T : (b + 1) * T, :])
                slab[b, a] = keep(fill[2 * a + b] != 0, rest.astype(BF16))

    for a in range(TR):
        pltpu.make_async_copy(obuf.at[a], solved.at[a], sem.at[a]).wait()


def finish_kernel(place, fill, own, other, got, got_o, w, wt, m, samples, *rest):
    @pl.when(place[2] == 0)
    def _():
        finish(0, place, fill, own, other, got, got_o, w, wt, m, samples, *rest)

    @pl.when(place[2] == 1)
    def _():
        finish(1, place, fill, other, own, got_o, got, w, wt, m, samples, *rest)


def body(front, fill, w, samples):
    x = lax.axis_index("x")
    z = lax.axis_index("z")
    y = lax.axis_index("y")
    k = lax.axis_index("core")
    masked = front * fill.astype(BF16)
    panel = masked[:, :, 0, :]

    piece = lax.dynamic_slice_in_dim(samples[0], k * T, T, 1)
    send = jnp.concatenate([panel[0].reshape(Q, RB, T), piece.reshape(Q, RB, T)], axis=1)
    got = lax.all_to_all(send, ("x", "y"), 0, 0)

    moved = []
    for to in (1, 2, 3):
        moved.append(lax.ppermute(panel, "y", [(0, to)]))

    send = jnp.concatenate([got[0, :RB], got[Y, :RB], got[0, RB:]], axis=0)
    got = lax.all_to_all(jnp.broadcast_to(send[None], (Z,) + send.shape), "z", 0, 0)

    pairs = got.reshape(Y, 2, 3 * RB, T)[:, :, : 2 * RB, :].reshape(Y, 4 * RB, T)
    common = jnp.concatenate([got[1, :RB], got[0, 2 * RB :], got[1, 2 * RB :]], axis=0)
    send = jnp.concatenate([pairs, jnp.broadcast_to(common[None], (Y,) + common.shape)], axis=1)
    send = jnp.broadcast_to(send[None], (X,) + send.shape).reshape(Q, 7 * RB, T)
    got = lax.all_to_all(send, ("x", "y"), 0, 0)

    own = lax.select(y == 0, panel, moved[0] + moved[1] + moved[2])
    other = swap(own)
    got_o = swap(got)

    place = jnp.stack([x * Z + z, y * K + k, k]).astype(jnp.int32)
    vmem = pl.BlockSpec(memory_space=pltpu.VMEM)
    smem = pl.BlockSpec(memory_space=pltpu.SMEM)
    slab, solved = pl.pallas_call(
        finish_kernel,
        in_specs=[smem, smem] + [vmem] * 8,
        out_specs=[vmem, pl.BlockSpec(memory_space=pl.ANY)],
        out_shape=[
            jax.ShapeDtypeStruct((TC, TR, T, T), BF16),
            jax.ShapeDtypeStruct((TR, T, 2 * T), BF16),
        ],
        scratch_shapes=[
            pltpu.VMEM((TR * T, 2 * T), BF16),
            pltpu.VMEM((TC * T, 2 * T), BF16),
            pltpu.VMEM((2 * T, 2 * T), BF16),
            pltpu.VMEM((TR, T, 2 * T), BF16),
            pltpu.SemaphoreType.DMA((TR,)),
        ],
        compiler_params=pltpu.CompilerParams(vmem_limit_bytes=20 * 1024 * 1024),
        name="finish",
    )(
        place,
        fill.reshape(TR * TC),
        own,
        other,
        got,
        got_o,
        w,
        w.transpose(0, 2, 1),
        masked.transpose(2, 0, 1, 3),
        samples,
    )
    return slab.transpose(1, 2, 0, 3), solved


def solution(mesh):
    fine = Mesh(mesh.devices.reshape(X, Z, Y, K), ("x", "z", "y", "core"))
    row, col = ("x", "z"), ("y", "core")
    in_specs = (P(None, row, None, col), P(None, row, None, col), P(), P(None, row))
    out_specs = (P(None, row, None, col), P(None, row))
    return jax.shard_map(body, mesh=fine, in_specs=in_specs, out_specs=out_specs, check_vma=False)
```

profile of v0, /device:TPU:8, one launch (start us, length us, event | category | flops | bytes accessed | tf_op | source)
XLA Modules:
  0.0 86.6 jit_solution(11460693613724614714)
XLA Ops:
  0.6 0.7 copy-done.3
  1.3 1.4 %copy_multiply_fusion = bf16[4,256,2,256]{3,1,0,2:T(8,128)(2,1)S(1)} fusion(bf16[4,256,2,256]{3,2,1,0:T(2,128)(2,1)} %param.4, bf16[4,2]{0,1:T(2,128)(2,1)S(1)} %bitcast.40), kind=kLoop, calls=%fused_computation | loop fusion | flops 524288 | bytes 2097168 | tf_op jit(solution)/shard_map/mul | solution.py:146
  2.7 0.0 copy-start.2
  2.7 0.0 slice-start
  2.8 1.1 %slice-done = bf16[1,256,512]{2,1,0:T(8,128)(2,1)S(1)} async-done(((bf16[4,256,512]{2,1,0:T(8,128)(2,1)}), bf16[1,256,512]{2,1,0:T(8,128)(2,1)S(1)}, s32[]{:S(2)}) %slice-start) | async-done | bytes 262168 | tf_op jit(solution)/shard_map/slice | solution.py:149
  3.9 14.3 %all_to_all.15 = bf16[16,32,256]{2,1,0:T(8,128)(2,1)S(1)} all-to-all(bf16[16,32,256]{2,1,0:T(8,128)(2,1)S(1)} %pad_maximum_fusion), channel_id=1, replica_groups=mesh['x'=4,'z'=8,'y'=4,'core'=2] {'x','y'}, dimensions={0} | all-to-all | bytes 524288 | tf_op jit(solution)/shard_map/all_to_all | solution.py:151
  18.2 18.0 %all_to_all.16 = bf16[8,48,256]{2,1,0:T(8,128)(2,1)S(1)} all-to-all(bf16[8,48,256]{2,1,0:T(8,128)(2,1)S(1)} %broadcast_in_dim.6), channel_id=1, replica_groups=mesh['x'=4,'z'=8,'y'=4,'core'=2] {'z'}, dimensions={0} | all-to-all | bytes 393216 | tf_op jit(solution)/shard_map/all_to_all | solution.py:158
  36.3 1.0 %broadcast_in_dim.8 = bf16[4,4,112,256]{3,2,1,0:T(8,128)(2,1)} broadcast(bf16[4,112,256]{2,1,0:T(8,128)(2,1)S(1)} %pad_maximum_fusion.1), dimensions={1,2,3} | broadcast | bytes 1146880 | tf_op jit(solution)/shard_map/broadcast_in_dim | solution.py:163
  37.3 5.1 %all-to-all-start.2 = ((bf16[16,112,256]{2,1,0:T(8,128)(2,1)}), bf16[16,112,256]{2,1,0:T(8,128)(2,1)S(1)}, u32[]{:S(2)}, u32[]{:S(2)}) async-start(bf16[16,112,256]{2,1,0:T(8,128)(2,1)} %bitcast.35), calls=%async_computation.2 | async-start | bytes 1835008 | tf_op jit(solution)/shard_map/all_to_all | solution.py:164
  42.4 0.7 collective-permute-start.2
  43.1 1.5 %collective-permute-start.1 = (bf16[4,256,256]{2,1,0:T(8,128)(2,1)S(1)}, bf16[4,256,256]{2,1,0:T(8,128)(2,1)}, u32[]{:S(2)}, u32[]{:S(2)}) collective-permute-start(bf16[4,256,256]{2,1,0:T(8,128)(2,1)S(1)} %slice_bitcast_fusion), channel_id=1, source_target_pairs={{0,4},{1,5},{8,12},{9,13},{16,20},{17,21},{24,28},{25,29},{32,36},... | collective-permute-start | bytes 1572872 | tf_op jit(solution)/shard_map/ppermute | solution.py:155
  44.6 1.3 %collective-permute-start = (bf16[4,256,256]{2,1,0:T(8,128)(2,1)S(1)}, bf16[4,256,256]{2,1,0:T(8,128)(2,1)}, u32[]{:S(2)}, u32[]{:S(2)}) collective-permute-start(bf16[4,256,256]{2,1,0:T(8,128)(2,1)S(1)} %slice_bitcast_fusion), channel_id=1, source_target_pairs={{0,2},{1,3},{8,10},{9,11},{16,18},{17,19},{24,26},{25,27},{32,34},... | collective-permute-start | bytes 1572872 | tf_op jit(solution)/shard_map/ppermute | solution.py:155
  45.9 8.4 %all-to-all-done.2.got = bf16[16,112,256]{2,1,0:T(8,128)(2,1)S(1)} async-done(((bf16[16,112,256]{2,1,0:T(8,128)(2,1)}), bf16[16,112,256]{2,1,0:T(8,128)(2,1)S(1)}, u32[]{:S(2)}, u32[]{:S(2)}) %all-to-all-start.2) | async-done | bytes 917536 | tf_op jit(solution)/shard_map/all_to_all | solution.py:164
  54.4 21.0 %collective-permute-done = bf16[4,256,256]{2,1,0:T(8,128)(2,1)} collective-permute-done((bf16[4,256,256]{2,1,0:T(8,128)(2,1)S(1)}, bf16[4,256,256]{2,1,0:T(8,128)(2,1)}, u32[]{:S(2)}, u32[]{:S(2)}) %collective-permute-start) | collective-permute-done | bytes 524320 | tf_op jit(solution)/shard_map/ppermute | solution.py:155
  75.4 1.5 %add_select_fusion.own = bf16[4,256,256]{2,1,0:T(8,128)(2,1)S(1)} fusion(bf16[4,256,256]{2,1,0:T(8,128)(2,1)S(1)} %collective-permute-done.2, bf16[4,256,256]{2,1,0:T(8,128)(2,1)} %collective-permute-done, bf16[4,256,256]{2,1,0:T(8,128)(2,1)} %collective-permute-done.1, pred[]{:T(512)S(6)} %eq.3, bf16[4,256,2,256]{3,1,0,2:T(8,128)(2,1)} %copy-done.2), kind=kLoop, calls=%fused_computation.2 | loop fusion | flops 786432 | bytes 2621441 | tf_op jit(solution)/shard_map/select_n | solution.py:166
  76.8 0.1 collective-permute-start.3
  76.9 0.1 copy.10
  77.0 0.1 reshape.26.fill
  77.1 0.1 copy.12
  77.3 0.1 pad_add_fusion.place
  77.4 1.5 %fusion.m = bf16[2,4,256,256]{3,2,1,0:T(8,128)(2,1)S(1)} fusion(bf16[4,2]{0,1:T(2,128)(2,1)S(1)} %bitcast.41, bf16[4,256,2,256]{3,2,1,0:T(2,128)(2,1)} %param.4), kind=kLoop, calls=%fused_computation.16 | loop fusion | flops 524288 | bytes 2097168 | tf_op jit(solution)/shard_map/transpose | solution.py:199
  78.9 0.0 copy-done
  78.9 5.6 %finish.1 = (bf16[2,4,256,256]{3,2,1,0:T(8,128)(2,1)S(1)}, bf16[4,256,512]{2,1,0:T(8,128)(2,1)}) custom-call(s32[3]{0:T(128)S(1)} %pad_add_fusion.place, s32[8]{0:T(128)S(1)} %reshape.26.fill, bf16[4,256,256]{2,1,0:T(8,128)(2,1)S(1)} %add_select_fusion.own, bf16[4,256,256]{2,1,0:T(8,128)(2,1)S(1)} %collective-permute-done.3.other, ...), custom_call_target="tpu_custom_call" | custom-call | tf_op jit(solution)/shard_map/finish/pallas_call | solution.py:173
  84.5 2.0 %copy.13 = bf16[4,256,2,256]{3,2,1,0:T(2,128)(2,1)} copy(bf16[4,256,2,256]{3,1,0,2:T(8,128)(2,1)S(1)} %bitcast.34) | data formatting | bytes 2097152
  (24 shorter events, 0.2 us)
Async XLA Ops:
  0.6 0.7 copy-start.3
  2.7 39.7 %copy-start.2 = (bf16[4,256,2,256]{3,1,0,2:T(8,128)(2,1)}, bf16[4,256,2,256]{3,1,0,2:T(8,128)(2,1)S(1)}, u32[]{:S(2)}) copy-start(bf16[4,256,2,256]{3,1,0,2:T(8,128)(2,1)S(1)} %copy_multiply_fusion) | copy-start | bytes 3145732
  2.7 1.1 %slice-start = ((bf16[4,256,512]{2,1,0:T(8,128)(2,1)}), bf16[1,256,512]{2,1,0:T(8,128)(2,1)S(1)}, s32[]{:S(2)}) async-start(bf16[4,256,512]{2,1,0:T(8,128)(2,1)} %samples.1), calls=%async_computation.3 | async-start | bytes 524288 | tf_op jit(solution)/shard_map/slice | solution.py:149
  37.3 17.0 %all-to-all-start.2 = ((bf16[16,112,256]{2,1,0:T(8,128)(2,1)}), bf16[16,112,256]{2,1,0:T(8,128)(2,1)S(1)}, u32[]{:S(2)}, u32[]{:S(2)}) async-start(bf16[16,112,256]{2,1,0:T(8,128)(2,1)} %bitcast.35), calls=%async_computation.2 | async-start | bytes 1835008 | tf_op jit(solution)/shard_map/all_to_all | solution.py:164
  42.4 11.9 %collective-permute-start.2 = (bf16[4,256,256]{2,1,0:T(8,128)(2,1)S(1)}, bf16[4,256,256]{2,1,0:T(8,128)(2,1)S(1)}, u32[]{:S(2)}, u32[]{:S(2)}) collective-permute-start(bf16[4,256,256]{2,1,0:T(8,128)(2,1)S(1)} %slice_bitcast_fusion), channel_id=1, source_target_pairs={{0,6},{1,7},{8,14},{9,15},{16,22},{17,23},{24,30},{25,31},{32,38},... | collective-permute-start | bytes 1572872 | tf_op jit(solution)/shard_map/ppermute | solution.py:155
  43.1 11.2 %collective-permute-start.1 = (bf16[4,256,256]{2,1,0:T(8,128)(2,1)S(1)}, bf16[4,256,256]{2,1,0:T(8,128)(2,1)}, u32[]{:S(2)}, u32[]{:S(2)}) collective-permute-start(bf16[4,256,256]{2,1,0:T(8,128)(2,1)S(1)} %slice_bitcast_fusion), channel_id=1, source_target_pairs={{0,4},{1,5},{8,12},{9,13},{16,20},{17,21},{24,28},{25,29},{32,36},... | collective-permute-start | bytes 1572872 | tf_op jit(solution)/shard_map/ppermute | solution.py:155
  44.6 30.8 %collective-permute-start = (bf16[4,256,256]{2,1,0:T(8,128)(2,1)S(1)}, bf16[4,256,256]{2,1,0:T(8,128)(2,1)}, u32[]{:S(2)}, u32[]{:S(2)}) collective-permute-start(bf16[4,256,256]{2,1,0:T(8,128)(2,1)S(1)} %slice_bitcast_fusion), channel_id=1, source_target_pairs={{0,2},{1,3},{8,10},{9,11},{16,18},{17,19},{24,26},{25,27},{32,34},... | collective-permute-start | bytes 1572872 | tf_op jit(solution)/shard_map/ppermute | solution.py:155
  54.3 24.5 %collective-permute-start.4 = (bf16[16,112,256]{2,1,0:T(8,128)(2,1)S(1)}, bf16[16,112,256]{2,1,0:T(8,128)(2,1)S(1)}, u32[]{:S(2)}, u32[]{:S(2)}) collective-permute-start(bf16[16,112,256]{2,1,0:T(8,128)(2,1)S(1)} %all-to-all-done.2.got), channel_id=1, source_target_pairs={{0,1},{1,0},{2,3},{3,2},{4,5},{5,4},{6,7},{7,6},{8,9},{9,8},{10,11... | collective-permute-start | bytes 2752520 | tf_op jit(solution)/shard_map/ppermute | solution.py:19
  54.3 22.8 %copy-start.1 = (bf16[2,256,256]{2,1,0:T(8,128)(2,1)S(1)}, bf16[2,256,256]{2,1,0:T(8,128)(2,1)}, u32[]{:S(2)}) copy-start(bf16[2,256,256]{2,1,0:T(8,128)(2,1)} %w.1) | copy-start | bytes 786436
  76.8 2.0 %collective-permute-start.3 = (bf16[4,256,256]{2,1,0:T(8,128)(2,1)S(1)}, bf16[4,256,256]{2,1,0:T(8,128)(2,1)S(1)}, u32[]{:S(2)}, u32[]{:S(2)}) collective-permute-start(bf16[4,256,256]{2,1,0:T(8,128)(2,1)S(1)} %add_select_fusion.own), channel_id=1, source_target_pairs={{0,1},{1,0},{2,3},{3,2},{4,5},{5,4},{6,7},{7,6},{8,9},{9,8},{10,11... | collective-permute-start | bytes 1572872 | tf_op jit(solution)/shard_map/ppermute | solution.py:19
  77.4 1.5 %copy-start = (bf16[4,256,512]{2,1,0:T(8,128)(2,1)S(1)}, bf16[4,256,512]{2,1,0:T(8,128)(2,1)}, u32[]{:S(2)}) copy-start(bf16[4,256,512]{2,1,0:T(8,128)(2,1)} %samples.1) | copy-start | bytes 3145732
where the time goes:
time: 87.7 us; the launch traced here: 86.6 us
  blocking collectives  32.3 us (37%)
  waiting for transfers between devices  29.5 us (34%)
  starting transfers between devices  8.6 us (10%)
  Pallas kernels  5.59 us (6%)
  local copies, waits for them, and re-layouts  5.29 us (6%)
  other arithmetic  4.45 us (5%)
    ppermute x3, waiting for transfers between devices, body(): moved.append(lax.ppermute(panel, 'y', [(0, to)]))  21 us
    all_to_all x1, blocking collectives, body(): lax.all_to_all(jnp.broadcast_to(send[None], (Z,) + send.shape), 'z', 0, 0)  18 us
    all_to_all x1, blocking collectives, body(): got = lax.all_to_all(send, ('x', 'y'), 0, 0)  14.3 us
    all_to_all x1, waiting for transfers between devices, body(): got = lax.all_to_all(send, ('x', 'y'), 0, 0)  8.45 us
    pallas_call x1, Pallas kernels, body(): pl.pallas_call(finish_kernel, in_specs=[smem, smem] + [vmem] * 8, out_spe...  5.59 us
    all_to_all x1, starting transfers between devices, body(): got = lax.all_to_all(send, ('x', 'y'), 0, 0)  5.06 us
    ppermute x3, starting transfers between devices, body(): moved.append(lax.ppermute(panel, 'y', [(0, to)]))  3.44 us
    unnamed x12, local copies, waits for them, and re-layouts  3 us
  transfers between devices with their start and end apart: 6, of which 2 were waited for; matrix products, arithmetic and copies ran while one was open for 4% of the time, Pallas kernels for 0%

commit v1 on v0

v1 whole, which is shorter than its diff:
```python
import jax
import jax.numpy as jnp
from jax import lax
from jax.experimental import pallas as pl
from jax.experimental.pallas import tpu as pltpu
from jax.sharding import Mesh, PartitionSpec as P


X, Z, Y, K = 4, 8, 4, 2
T = 256
TR = 4
TC = 2
Q = X * Y
RB = T // Q
F32, BF16 = jnp.float32, jnp.bfloat16


def swap(v):
    return lax.ppermute(v, "core", [(0, 1), (1, 0)])


def mm(a, b):
    return lax.dot_general(a, b, (((1,), (0,)), ((), ())), preferred_element_type=F32)


def mmt(a, b):
    return lax.dot_general(a, b, (((1,), (1,)), ((), ())), preferred_element_type=F32)


def tmm(a, b):
    return lax.dot_general(a, b, (((0,), (0,)), ((), ())), preferred_element_type=F32)


def keep(cond, value):
    return jnp.where(cond, value, jnp.zeros_like(value))


def finish(k, place, f0, f1, g0, g1, wt, m, samples, slab, solved, lrow, lcol, ys, obuf, sem, arrival):
    row_pos = place[0]
    col_pos = place[1]

    def tile(ref, at):
        return ref[:, at * RB : (at + 1) * RB, :].reshape(T, T)

    def pair(ref, at):
        return jnp.concatenate([tile(ref, at), tile(ref, at + 1)], axis=0)

    l0_one = mm(tile(g0, 4), wt[0]).astype(BF16)

    lcol[:, 0:T] = mm(pair(g0, 2 * k), wt[0]).astype(BF16)

    @pl.when(col_pos == 0)
    def _():
        lcol[0:T, 0:T] = jnp.zeros((T, T), BF16)

    second = (pair(g1, 2 * k).astype(F32) - mmt(lcol[:, 0:T], l0_one)).astype(BF16)
    lcol[:, T : 2 * T] = mm(second, wt[1]).astype(BF16)

    y0 = tmm(wt[0], jnp.concatenate([tile(g0, 5), tile(g1, 5)], axis=1)).astype(BF16)
    r1 = jnp.concatenate([tile(g0, 6), tile(g1, 6)], axis=1).astype(F32) - mm(l0_one, y0)
    ys[0:T, :] = y0
    ys[T : 2 * T, :] = tmm(wt[1], r1.astype(BF16)).astype(BF16)

    arrival.wait()
    lrow[:, 0:T] = mm(f0[...].reshape(TR * T, T), wt[0]).astype(BF16)

    @pl.when(row_pos == 0)
    def _():
        lrow[0:T, 0:T] = jnp.zeros((T, T), BF16)

    second = (f1[...].reshape(TR * T, T).astype(F32) - mmt(lrow[:, 0:T], l0_one)).astype(BF16)
    lrow[:, T : 2 * T] = mm(second, wt[1]).astype(BF16)
    slab[0, 0] = second[0:T]

    @pl.when(row_pos <= 1)
    def _():
        lrow[0:T, T : 2 * T] = jnp.zeros((T, T), BF16)

    @pl.when(col_pos <= 1)
    def _():
        lcol[0:T, T : 2 * T] = jnp.zeros((T, T), BF16)

    for a in range(TR):
        rest = samples[a].astype(F32) - mm(lrow[a * T : (a + 1) * T, :], ys[...])
        obuf[a] = rest.astype(BF16)

    @pl.when(row_pos == 0)
    def _():
        obuf[0] = ys[0:T, :]

    @pl.when(row_pos == 1)
    def _():
        obuf[0] = ys[T : 2 * T, :]

    out = pltpu.make_async_copy(obuf, solved, sem)
    out.start()

    for a in range(TR):
        product = mmt(lrow[a * T : (a + 1) * T, :], lcol[...])
        for b in range(TC):
            rest = (m[b, a].astype(F32) - product[:, b * T : (b + 1) * T]).astype(BF16)
            rest = keep(place[3 + 2 * a + b] != 0, rest)
            if (a, b) == (0, 0):
                @pl.when(col_pos >= 2)
                def _():
                    slab[0, 0] = rest

            else:
                slab[b, a] = rest

    @pl.when(col_pos == 0)
    def _():
        for a in range(1, TR):
            slab[0, a] = lrow[a * T : (a + 1) * T, 0:T]

        @pl.when(row_pos == 0)
        def _():
            slab[0, 0] = f0[0]

        @pl.when(row_pos >= 1)
        def _():
            slab[0, 0] = lrow[0:T, 0:T]

    @pl.when(col_pos == 1)
    def _():
        for a in range(1, TR):
            slab[0, a] = lrow[a * T : (a + 1) * T, T : 2 * T]

        @pl.when(row_pos >= 2)
        def _():
            slab[0, 0] = lrow[0:T, T : 2 * T]

    out.wait()


def finish_kernel(place, own, other_hbm, got, got_o, wt, m, samples, *rest):
    *rest, other, other_sem = rest
    arrival = pltpu.make_async_copy(other_hbm, other, other_sem)
    arrival.start()
    rest = (*rest, arrival)

    @pl.when(place[2] == 0)
    def _():
        finish(0, place, own, other, got, got_o, wt, m, samples, *rest)

    @pl.when(place[2] == 1)
    def _():
        finish(1, place, other, own, got_o, got, wt, m, samples, *rest)


def body(front, fill, w, samples):
    x = lax.axis_index("x")
    z = lax.axis_index("z")
    y = lax.axis_index("y")
    k = lax.axis_index("core")
    tiles = front.transpose(2, 0, 1, 3)
    pattern = fill.astype(BF16)[:, :, 0, :]
    panel = tiles[0] * pattern

    piece = lax.dynamic_slice(samples, (0, 0, k * T), (1, T, T))
    send = jnp.concatenate([(tiles[0, 0] * pattern[0]).reshape(Q, RB, T), piece.reshape(Q, RB, T)], axis=1)
    got = lax.all_to_all(send, ("x", "y"), 0, 0)

    moved = []
    for to in (1, 2, 3):
        moved.append(lax.ppermute(panel, "y", [(0, to)]))

    send = jnp.concatenate([got[0, :RB], got[Y, :RB], got[0, RB:]], axis=0)
    got = lax.all_to_all(jnp.broadcast_to(send[None], (Z,) + send.shape), "z", 0, 0)

    pairs = got.reshape(Y, 2, 3 * RB, T)[:, :, : 2 * RB, :].reshape(Y, 4 * RB, T)
    common = jnp.concatenate([got[1, :RB], got[0, 2 * RB :], got[1, 2 * RB :]], axis=0)
    send = jnp.concatenate([pairs, jnp.broadcast_to(common[None], (Y,) + common.shape)], axis=1)
    send = jnp.broadcast_to(send[None], (X,) + send.shape).reshape(Q, 7 * RB, T)
    got = lax.all_to_all(send, ("x", "y"), 0, 0)

    wt = w * jnp.where(z >= 0, 1.0, 0.0).astype(BF16)
    place = jnp.stack([x * Z + z, y * K + k, k]).astype(jnp.int32)
    place = jnp.concatenate([place, fill.reshape(TR * TC)])

    own = lax.select(y == 0, panel, moved[0] + moved[1] + moved[2])
    other = swap(own)
    got_o = swap(got)

    vmem = pl.BlockSpec(memory_space=pltpu.VMEM)
    smem = pl.BlockSpec(memory_space=pltpu.SMEM)
    slab, solved = pl.pallas_call(
        finish_kernel,
        in_specs=[smem, vmem, pl.BlockSpec(memory_space=pl.ANY)] + [vmem] * 5,
        out_specs=[vmem, pl.BlockSpec(memory_space=pl.ANY)],
        out_shape=[
            jax.ShapeDtypeStruct((TC, TR, T, T), BF16),
            jax.ShapeDtypeStruct((TR, T, 2 * T), BF16),
        ],
        scratch_shapes=[
            pltpu.VMEM((TR * T, 2 * T), BF16),
            pltpu.VMEM((TC * T, 2 * T), BF16),
            pltpu.VMEM((2 * T, 2 * T), BF16),
            pltpu.VMEM((TR, T, 2 * T), BF16),
            pltpu.SemaphoreType.DMA,
            pltpu.VMEM((TR, T, T), BF16),
            pltpu.SemaphoreType.DMA,
        ],
        compiler_params=pltpu.CompilerParams(vmem_limit_bytes=20 * 1024 * 1024),
        name="finish",
    )(
        place,
        own,
        other,
        got,
        got_o,
        wt,
        tiles,
        samples,
    )
    return slab.transpose(1, 2, 0, 3), solved


def solution(mesh):
    fine = Mesh(mesh.devices.reshape(X, Z, Y, K), ("x", "z", "y", "core"))
    row, col = ("x", "z"), ("y", "core")
    in_specs = (P(None, row, None, col), P(None, row, None, col), P(), P(None, row))
    out_specs = (P(None, row, None, col), P(None, row))
    return jax.shard_map(body, mesh=fine, in_specs=in_specs, out_specs=out_specs, check_vma=False)
```

time: 87.7 us -> 87.3 us (level)
  local copies, waits for them, and re-layouts: 5.29 us -> 6.76 us
    unnamed x12 -> x9, local copies, waits for them, and re-layouts: 3 us -> 5.13 us
    transpose x1 -> x0, other arithmetic: 1.48 us -> none  [body(): masked.transpose(2, 0, 1, 3)]
    mul x1 -> x3, other arithmetic: 1.39 us -> 2.53 us  [the longest x1 0.97 us: body(): wt = w * jnp.where(z >= 0, 1.0, 0.0).astype(BF16)]
  transfers between devices with their start and end apart: 6 -> 6, of which waited for: 2 -> 3; matrix products, arithmetic and copies ran while one was open for 4% -> 4% of each run, Pallas kernels for 0% -> 0%
where the time goes in v1:
time: 87.3 us; the launch traced here: 86.5 us
  blocking collectives  32.3 us (37%)
  waiting for transfers between devices  28.8 us (33%)
  starting transfers between devices  8.58 us (10%)
  local copies, waits for them, and re-layouts  6.76 us (8%)
  Pallas kernels  5.11 us (6%)
  other arithmetic  4.17 us (5%)
    ppermute x3, waiting for transfers between devices, body(): moved.append(lax.ppermute(panel, 'y', [(0, to)]))  20.4 us
    all_to_all x1, blocking collectives, body(): lax.all_to_all(jnp.broadcast_to(send[None], (Z,) + send.shape), 'z', 0, 0)  18 us
    all_to_all x1, blocking collectives, body(): got = lax.all_to_all(send, ('x', 'y'), 0, 0)  14.3 us
    all_to_all x1, waiting for transfers between devices, body(): got = lax.all_to_all(send, ('x', 'y'), 0, 0)  7.61 us
    unnamed x9, local copies, waits for them, and re-layouts  5.13 us
    pallas_call x1, Pallas kernels, body(): pl.pallas_call(finish_kernel, in_specs=[smem, vmem, pl.BlockSpec(memory_s...  5.11 us
    all_to_all x1, starting transfers between devices, body(): got = lax.all_to_all(send, ('x', 'y'), 0, 0)  5.06 us
    ppermute x3, starting transfers between devices, body(): moved.append(lax.ppermute(panel, 'y', [(0, to)]))  3.42 us
  transfers between devices with their start and end apart: 6, of which 3 were waited for; matrix products, arithmetic and copies ran while one was open for 4% of the time, Pallas kernels for 0%

profile of v1, /device:TPU:8, one launch (start us, length us, event | category | flops | bytes accessed | tf_op | source)
XLA Modules:
  0.0 86.5 jit_solution(3357024945057082091)
XLA Ops:
  0.6 0.7 copy-done.2
  1.3 0.5 slice.49
  1.8 1.5 %copy.13 = bf16[4,256,2,256]{3,1,0,2:T(8,128)(2,1)S(1)} copy(bf16[4,256,2,256]{3,2,1,0:T(2,128)(2,1)} %param.4) | data formatting | bytes 2097152 | tf_op args[0]
  3.4 0.7 slice_multiply_fusion
  4.1 14.3 %all_to_all.15 = bf16[16,32,256]{2,1,0:T(8,128)(2,1)S(1)} all-to-all(bf16[16,32,256]{2,1,0:T(8,128)(2,1)S(1)} %pad_maximum_fusion), channel_id=1, replica_groups=mesh['x'=4,'z'=8,'y'=4,'core'=2] {'x','y'}, dimensions={0} | all-to-all | bytes 524288 | tf_op jit(solution)/shard_map/all_to_all | solution.py:162
  18.4 18.0 %all_to_all.16 = bf16[8,48,256]{2,1,0:T(8,128)(2,1)S(1)} all-to-all(bf16[8,48,256]{2,1,0:T(8,128)(2,1)S(1)} %broadcast_in_dim.6), channel_id=1, replica_groups=mesh['x'=4,'z'=8,'y'=4,'core'=2] {'z'}, dimensions={0} | all-to-all | bytes 393216 | tf_op jit(solution)/shard_map/all_to_all | solution.py:169
  36.5 1.0 %broadcast_in_dim.8 = bf16[4,4,112,256]{3,2,1,0:T(8,128)(2,1)} broadcast(bf16[4,112,256]{2,1,0:T(8,128)(2,1)S(1)} %pad_maximum_fusion.1), dimensions={1,2,3} | broadcast | bytes 1146880 | tf_op jit(solution)/shard_map/broadcast_in_dim | solution.py:174
  37.5 5.1 %all-to-all-start.2 = ((bf16[16,112,256]{2,1,0:T(8,128)(2,1)}), bf16[16,112,256]{2,1,0:T(8,128)(2,1)S(1)}, u32[]{:S(2)}, u32[]{:S(2)}) async-start(bf16[16,112,256]{2,1,0:T(8,128)(2,1)} %bitcast.40), calls=%async_computation.2 | async-start | bytes 1835008 | tf_op jit(solution)/shard_map/all_to_all | solution.py:175
  42.6 0.9 %fusion = bf16[4,256,256]{2,1,0:T(8,128)(2,1)} fusion(bf16[2,4,256,256]{3,2,1,0:T(8,128)(2,1)S(1)} %bitcast.36, bf16[4]{0:T(256)(128)(2,1)S(1)} %slice_bitcast_fusion.7), kind=kLoop, calls=%fused_computation.2 | loop fusion | flops 262144 | bytes 1048584 | tf_op jit(solution)/shard_map/mul | solution.py:158
  43.5 0.7 collective-permute-start.2
  44.1 1.5 %collective-permute-start.1 = (bf16[4,256,256]{2,1,0:T(8,128)(2,1)}, bf16[4,256,256]{2,1,0:T(8,128)(2,1)}, u32[]{:S(2)}, u32[]{:S(2)}) collective-permute-start(bf16[4,256,256]{2,1,0:T(8,128)(2,1)} %fusion), channel_id=1, source_target_pairs={{0,4},{1,5},{8,12},{9,13},{16,20},{17,21},{24,28},{25,29},{32,36},... | collective-permute-start | bytes 1572872 | tf_op jit(solution)/shard_map/ppermute | solution.py:166
  45.6 1.3 %collective-permute-start = (bf16[4,256,256]{2,1,0:T(8,128)(2,1)}, bf16[4,256,256]{2,1,0:T(8,128)(2,1)}, u32[]{:S(2)}, u32[]{:S(2)}) collective-permute-start(bf16[4,256,256]{2,1,0:T(8,128)(2,1)} %fusion), channel_id=1, source_target_pairs={{0,2},{1,3},{8,10},{9,11},{16,18},{17,19},{24,26},{25,27},{32,34},... | collective-permute-start | bytes 1572872 | tf_op jit(solution)/shard_map/ppermute | solution.py:166
  46.9 7.6 %all-to-all-done.2.got = bf16[16,112,256]{2,1,0:T(8,128)(2,1)S(1)} async-done(((bf16[16,112,256]{2,1,0:T(8,128)(2,1)}), bf16[16,112,256]{2,1,0:T(8,128)(2,1)S(1)}, u32[]{:S(2)}, u32[]{:S(2)}) %all-to-all-start.2) | async-done | bytes 917536 | tf_op jit(solution)/shard_map/all_to_all | solution.py:175
  54.5 0.8 copy-done.1
  55.3 20.4 %collective-permute-done = bf16[4,256,256]{2,1,0:T(8,128)(2,1)} collective-permute-done((bf16[4,256,256]{2,1,0:T(8,128)(2,1)}, bf16[4,256,256]{2,1,0:T(8,128)(2,1)}, u32[]{:S(2)}, u32[]{:S(2)}) %collective-permute-start) | collective-permute-done | bytes 524320 | tf_op jit(solution)/shard_map/ppermute | solution.py:166
  75.7 1.5 %add_select_fusion.own = bf16[4,256,256]{2,1,0:T(8,128)(2,1)S(1)} fusion(bf16[4,256,256]{2,1,0:T(8,128)(2,1)} %copy-done.1, bf16[4,256,256]{2,1,0:T(8,128)(2,1)} %collective-permute-done, bf16[4,256,256]{2,1,0:T(8,128)(2,1)} %collective-permute-done.1, pred[]{:T(512)S(6)} %eq.3, bf16[4]{0:T(256)(128)(2,1)S(1)} %slice_bitcast_fusion.7, ...), kind=kLoop, calls=%fused_computation.3 | loop fusion | flops 1048576 | bytes 2621449 | tf_op jit(solution)/shard_map/select_n | solution.py:181
  77.2 0.1 collective-permute-start.3
  77.3 0.1 copy.9
  77.4 0.1 reshape.30
  77.5 0.1 pad_add_fusion.place
  77.6 1.0 %broadcast_multiply_fusion.wt = bf16[2,256,256]{2,1,0:T(8,128)(2,1)S(1)} fusion(bf16[2,256,256]{2,1,0:T(8,128)(2,1)} %param.6, bf16[]{:T(256)S(6)} %select_n.16), kind=kLoop, calls=%fused_computation.7 | loop fusion | flops 131072 | bytes 524290 | tf_op jit(solution)/shard_map/mul | solution.py:177
  78.5 0.8 collective-permute-done.3.other_hbm
  79.3 5.1 %finish.1 = (bf16[2,4,256,256]{3,2,1,0:T(8,128)(2,1)S(1)}, bf16[4,256,512]{2,1,0:T(8,128)(2,1)}) custom-call(s32[11]{0:T(128)S(1)} %pad_add_fusion.place, bf16[4,256,256]{2,1,0:T(8,128)(2,1)S(1)} %add_select_fusion.own, bf16[4,256,256]{2,1,0:T(8,128)(2,1)} %collective-permute-done.3.other_hbm, bf16[16,112,256]{2,1,0:T(8,128)(2,1)S(1)} %all-to-all-done.2.got, ...), custom_call_target="tpu_custom_call" | custom-call | tf_op jit(solution)/shard_map/finish/pallas_call | solution.py:187
  84.5 2.0 %copy.11 = bf16[4,256,2,256]{3,2,1,0:T(2,128)(2,1)} copy(bf16[4,256,2,256]{3,1,0,2:T(8,128)(2,1)S(1)} %bitcast.39) | data formatting | bytes 2097152
  (20 shorter events, 0.2 us)
Async XLA Ops:
  0.6 0.7 copy-start.2
  1.8 1.5 %copy-start = (bf16[4,256,512]{2,1,0:T(8,128)(2,1)S(1)}, bf16[4,256,512]{2,1,0:T(8,128)(2,1)}, u32[]{:S(2)}) copy-start(bf16[4,256,512]{2,1,0:T(8,128)(2,1)} %samples.1) | copy-start | bytes 3145732
  37.5 17.0 %all-to-all-start.2 = ((bf16[16,112,256]{2,1,0:T(8,128)(2,1)}), bf16[16,112,256]{2,1,0:T(8,128)(2,1)S(1)}, u32[]{:S(2)}, u32[]{:S(2)}) async-start(bf16[16,112,256]{2,1,0:T(8,128)(2,1)} %bitcast.40), calls=%async_computation.2 | async-start | bytes 1835008 | tf_op jit(solution)/shard_map/all_to_all | solution.py:175
  43.5 11.1 %collective-permute-start.2 = (bf16[4,256,256]{2,1,0:T(8,128)(2,1)}, bf16[4,256,256]{2,1,0:T(8,128)(2,1)S(1)}, u32[]{:S(2)}, u32[]{:S(2)}) collective-permute-start(bf16[4,256,256]{2,1,0:T(8,128)(2,1)} %fusion), channel_id=1, source_target_pairs={{0,6},{1,7},{8,14},{9,15},{16,22},{17,23},{24,30},{25,31},{32,38},... | collective-permute-start | bytes 1572872 | tf_op jit(solution)/shard_map/ppermute | solution.py:166
  44.1 10.4 %collective-permute-start.1 = (bf16[4,256,256]{2,1,0:T(8,128)(2,1)}, bf16[4,256,256]{2,1,0:T(8,128)(2,1)}, u32[]{:S(2)}, u32[]{:S(2)}) collective-permute-start(bf16[4,256,256]{2,1,0:T(8,128)(2,1)} %fusion), channel_id=1, source_target_pairs={{0,4},{1,5},{8,12},{9,13},{16,20},{17,21},{24,28},{25,29},{32,36},... | collective-permute-start | bytes 1572872 | tf_op jit(solution)/shard_map/ppermute | solution.py:166
  45.6 30.1 %collective-permute-start = (bf16[4,256,256]{2,1,0:T(8,128)(2,1)}, bf16[4,256,256]{2,1,0:T(8,128)(2,1)}, u32[]{:S(2)}, u32[]{:S(2)}) collective-permute-start(bf16[4,256,256]{2,1,0:T(8,128)(2,1)} %fusion), channel_id=1, source_target_pairs={{0,2},{1,3},{8,10},{9,11},{16,18},{17,19},{24,26},{25,27},{32,34},... | collective-permute-start | bytes 1572872 | tf_op jit(solution)/shard_map/ppermute | solution.py:166
  54.5 24.8 %collective-permute-start.4 = (bf16[16,112,256]{2,1,0:T(8,128)(2,1)S(1)}, bf16[16,112,256]{2,1,0:T(8,128)(2,1)}, u32[]{:S(2)}, u32[]{:S(2)}) collective-permute-start(bf16[16,112,256]{2,1,0:T(8,128)(2,1)S(1)} %all-to-all-done.2.got), channel_id=1, source_target_pairs={{0,1},{1,0},{2,3},{3,2},{4,5},{5,4},{6,7},{7,6},{8,9},{9,8},{10,11... | collective-permute-start | bytes 2752520 | tf_op jit(solution)/shard_map/ppermute | solution.py:19
  54.5 0.8 copy-start.1
  77.2 2.1 %collective-permute-start.3 = (bf16[4,256,256]{2,1,0:T(8,128)(2,1)S(1)}, bf16[4,256,256]{2,1,0:T(8,128)(2,1)}, u32[]{:S(2)}, u32[]{:S(2)}) collective-permute-start(bf16[4,256,256]{2,1,0:T(8,128)(2,1)S(1)} %add_select_fusion.own), channel_id=1, source_target_pairs={{0,1},{1,0},{2,3},{3,2},{4,5},{5,4},{6,7},{7,6},{8,9},{9,8},{10,11... | collective-permute-start | bytes 1572872 | tf_op jit(solution)/shard_map/ppermute | solution.py:19

commit v2 on v1

--- a/solution.py
+++ b/solution.py
@@ -35,54 +35,45 @@
     return jnp.where(cond, value, jnp.zeros_like(value))
 
 
-def finish(k, place, f0, f1, g0, g1, wt, m, samples, slab, solved, lrow, lcol, ys, obuf, sem, arrival):
+def finish(k, place, f0, f1, g0, g1, w, m, samples, slab, solved, lrow, lcol, ys, obuf, sem, arrival):
     row_pos = place[0]
     col_pos = place[1]
 
     def tile(ref, at):
         return ref[:, at * RB : (at + 1) * RB, :].reshape(T, T)
 
-    def pair(ref, at):
-        return jnp.concatenate([tile(ref, at), tile(ref, at + 1)], axis=0)
-
-    l0_one = mm(tile(g0, 4), wt[0]).astype(BF16)
-
-    lcol[:, 0:T] = mm(pair(g0, 2 * k), wt[0]).astype(BF16)
-
-    @pl.when(col_pos == 0)
-    def _():
-        lcol[0:T, 0:T] = jnp.zeros((T, T), BF16)
-
-    second = (pair(g1, 2 * k).astype(F32) - mmt(lcol[:, 0:T], l0_one)).astype(BF16)
-    lcol[:, T : 2 * T] = mm(second, wt[1]).astype(BF16)
-
-    y0 = tmm(wt[0], jnp.concatenate([tile(g0, 5), tile(g1, 5)], axis=1)).astype(BF16)
+    def from_second(tile_second, first):
+        return (tile_second.astype(F32) - mmt(first, l0_one)).astype(BF16)
+
+    l0_one = mm(tile(g0, 4), w[0]).astype(BF16)
+    first_col = [mm(tile(g0, 2 * k + b), w[0]).astype(BF16) for b in range(TC)]
+    first_col[0] = keep(col_pos >= 1, first_col[0])
+    y0 = tmm(w[0], jnp.concatenate([tile(g0, 5), tile(g1, 5)], axis=1)).astype(BF16)
+    arrival.wait()
+    first_row = mm(f0[...].reshape(TR * T, T), w[0]).astype(BF16)
+    first_row = [first_row[a * T : (a + 1) * T] for a in range(TR)]
+    first_row[0] = keep(row_pos >= 1, first_row[0])
+    ys[0:T, :] = y0
+    for b in range(TC):
+        lcol[b * T : (b + 1) * T, 0:T] = first_col[b]
+    for a in range(TR):
+        lrow[a * T : (a + 1) * T, 0:T] = first_row[a]
+
+    second_col = [from_second(tile(g1, 2 * k + b), first_col[b]) for b in range(TC)]
+    second_row = [from_second(f1[a], first_row[a]) for a in range(TR)]
     r1 = jnp.concatenate([tile(g0, 6), tile(g1, 6)], axis=1).astype(F32) - mm(l0_one, y0)
-    ys[0:T, :] = y0
-    ys[T : 2 * T, :] = tmm(wt[1], r1.astype(BF16)).astype(BF16)
-
-    arrival.wait()
-    lrow[:, 0:T] = mm(f0[...].reshape(TR * T, T), wt[0]).astype(BF16)
-
-    @pl.when(row_pos == 0)
-    def _():
-        lrow[0:T, 0:T] = jnp.zeros((T, T), BF16)
-
-    second = (f1[...].reshape(TR * T, T).astype(F32) - mmt(lrow[:, 0:T], l0_one)).astype(BF16)
-    lrow[:, T : 2 * T] = mm(second, wt[1]).astype(BF16)
-    slab[0, 0] = second[0:T]
-
-    @pl.when(row_pos <= 1)
-    def _():
-        lrow[0:T, T : 2 * T] = jnp.zeros((T, T), BF16)
-
-    @pl.when(col_pos <= 1)
-    def _():
-        lcol[0:T, T : 2 * T] = jnp.zeros((T, T), BF16)
-
-    for a in range(TR):
-        rest = samples[a].astype(F32) - mm(lrow[a * T : (a + 1) * T, :], ys[...])
-        obuf[a] = rest.astype(BF16)
+    slab[0, 0] = second_row[0]
+    for b in range(TC):
+        third = mm(second_col[b], w[1]).astype(BF16)
+        lcol[b * T : (b + 1) * T, T : 2 * T] = keep(col_pos >= 2, third) if b == 0 else third
+    for a in range(TR):
+        third = mm(second_row[a], w[1]).astype(BF16)
+        lrow[a * T : (a + 1) * T, T : 2 * T] = keep(row_pos >= 2, third) if a == 0 else third
+    ys[T : 2 * T, :] = tmm(w[1], r1.astype(BF16)).astype(BF16)
+
+    for a in range(TR):
+        rows = lrow[a * T : (a + 1) * T, :]
+        obuf[a] = (samples[a].astype(F32) - mm(rows, ys[...])).astype(BF16)
 
     @pl.when(row_pos == 0)
     def _():
@@ -100,13 +91,7 @@
         for b in range(TC):
             rest = (m[b, a].astype(F32) - product[:, b * T : (b + 1) * T]).astype(BF16)
             rest = keep(place[3 + 2 * a + b] != 0, rest)
-            if (a, b) == (0, 0):
-                @pl.when(col_pos >= 2)
-                def _():
-                    slab[0, 0] = rest
-
-            else:
-                slab[b, a] = rest
+            slab[b, a] = lax.select(col_pos >= 2, rest, slab[0, 0]) if (a, b) == (0, 0) else rest
 
     @pl.when(col_pos == 0)
     def _():
@@ -153,17 +138,18 @@
     z = lax.axis_index("z")
     y = lax.axis_index("y")
     k = lax.axis_index("core")
-    tiles = front.transpose(2, 0, 1, 3)
-    pattern = fill.astype(BF16)[:, :, 0, :]
-    panel = tiles[0] * pattern
+    tiles = front.transpose(2, 0, 1, 3) * fill.astype(BF16).transpose(2, 0, 1, 3)
+    tiles = lax.optimization_barrier(tiles)
+    panel = tiles[0]
 
     piece = lax.dynamic_slice(samples, (0, 0, k * T), (1, T, T))
-    send = jnp.concatenate([(tiles[0, 0] * pattern[0]).reshape(Q, RB, T), piece.reshape(Q, RB, T)], axis=1)
+    send = jnp.concatenate([panel[0].reshape(Q, RB, T), piece.reshape(Q, RB, T)], axis=1)
     got = lax.all_to_all(send, ("x", "y"), 0, 0)
 
-    moved = []
-    for to in (1, 2, 3):
-        moved.append(lax.ppermute(panel, "y", [(0, to)]))
+    right = lax.ppermute(panel, "y", [(0, 1)])
+    left = lax.ppermute(panel, "y", [(0, 3)])
+    lower = lax.ppermute(right[: TR // 2], "y", [(1, 2)])
+    upper = lax.ppermute(left[TR // 2 :], "y", [(3, 2)])
 
     send = jnp.concatenate([got[0, :RB], got[Y, :RB], got[0, RB:]], axis=0)
     got = lax.all_to_all(jnp.broadcast_to(send[None], (Z,) + send.shape), "z", 0, 0)
@@ -178,7 +164,7 @@
     place = jnp.stack([x * Z + z, y * K + k, k]).astype(jnp.int32)
     place = jnp.concatenate([place, fill.reshape(TR * TC)])
 
-    own = lax.select(y == 0, panel, moved[0] + moved[1] + moved[2])
+    own = lax.select(y == 0, panel, right + left + jnp.concatenate([lower, upper]))
     other = swap(own)
     got_o = swap(got)
 

time: 87.3 us -> 83 us (0.951)
  the two profiles are of different devices: /device:TPU:8 before, /device:TPU:17 now
where the time goes in v2:
time: 83 us; the launch traced here: 82.5 us
  blocking collectives  29.1 us (35%)
  waiting for transfers between devices  23.7 us (29%)
  starting transfers between devices  15 us (18%)
  Pallas kernels  4.97 us (6%)
  local copies, waits for them, and re-layouts  4.82 us (6%)
  other arithmetic  4.06 us (5%)
    ppermute x1, waiting for transfers between devices, body(): upper = lax.ppermute(left[TR // 2:], 'y', [(3, 2)])  17.6 us
    all_to_all x1, blocking collectives, body(): lax.all_to_all(jnp.broadcast_to(send[None], (Z,) + send.shape), 'z', 0, 0)  16.7 us
    all_to_all x1, blocking collectives, body(): got = lax.all_to_all(send, ('x', 'y'), 0, 0)  12.5 us
    ppermute x2, starting transfers between devices, swap(): return lax.ppermute(v, 'core', [(0, 1), (1, 0)])  5.93 us
    all_to_all x1, waiting for transfers between devices, body(): got = lax.all_to_all(send, ('x', 'y'), 0, 0)  5.62 us
    all_to_all x1, starting transfers between devices, body(): got = lax.all_to_all(send, ('x', 'y'), 0, 0)  5.09 us
    pallas_call x1, Pallas kernels, body(): pl.pallas_call(finish_kernel, in_specs=[smem, vmem, pl.BlockSpec(memory_s...  4.97 us
    unnamed x11, local copies, waits for them, and re-layouts  3.62 us
  transfers between devices with their start and end apart: 7, of which 3 were waited for; matrix products, arithmetic and copies ran while one was open for 3% of the time, Pallas kernels for 0%

profile of v2, /device:TPU:17, one launch (start us, length us, event | category | flops | bytes accessed | tf_op | source)
XLA Modules:
  0.0 82.5 jit_solution(16938189182557985624)
XLA Ops:
  0.6 0.7 copy-done.3
  1.3 1.5 %bitcast_multiply_fusion.m = bf16[2,4,256,256]{3,2,1,0:T(8,128)(2,1)S(1)} fusion(bf16[4,256,2,256]{3,2,1,0:T(2,128)(2,1)} %param.4, bf16[2,4]{1,0:T(2,128)(2,1)S(1)} %bitcast.40), kind=kLoop, calls=%fused_computation | loop fusion | flops 524288 | bytes 2097168 | tf_op jit(solution)/shard_map/mul | solution.py:141
  2.8 0.0 copy-done
  2.9 12.5 %all_to_all.15 = bf16[16,32,256]{2,1,0:T(8,128)(2,1)S(1)} all-to-all(bf16[16,32,256]{2,1,0:T(8,128)(2,1)S(1)} %pad_maximum_fusion), channel_id=1, replica_groups=mesh['x'=4,'z'=8,'y'=4,'core'=2] {'x','y'}, dimensions={0} | all-to-all | bytes 524288 | tf_op jit(solution)/shard_map/all_to_all | solution.py:147
  15.4 16.7 %all_to_all.16 = bf16[8,48,256]{2,1,0:T(8,128)(2,1)S(1)} all-to-all(bf16[8,48,256]{2,1,0:T(8,128)(2,1)S(1)} %broadcast_in_dim.6), channel_id=1, replica_groups=mesh['x'=4,'z'=8,'y'=4,'core'=2] {'z'}, dimensions={0} | all-to-all | bytes 393216 | tf_op jit(solution)/shard_map/all_to_all | solution.py:155
  32.2 1.0 %broadcast_in_dim.8 = bf16[4,4,112,256]{3,2,1,0:T(8,128)(2,1)} broadcast(bf16[4,112,256]{2,1,0:T(8,128)(2,1)S(1)} %pad_maximum_fusion.1), dimensions={1,2,3} | broadcast | bytes 1146880 | tf_op jit(solution)/shard_map/broadcast_in_dim | solution.py:160
  33.1 5.1 %all-to-all-start.2 = ((bf16[16,112,256]{2,1,0:T(8,128)(2,1)}), bf16[16,112,256]{2,1,0:T(8,128)(2,1)S(1)}, u32[]{:S(2)}, u32[]{:S(2)}) async-start(bf16[16,112,256]{2,1,0:T(8,128)(2,1)} %bitcast.35), calls=%async_computation.2 | async-start | bytes 1835008 | tf_op jit(solution)/shard_map/all_to_all | solution.py:161
  38.3 0.7 collective-permute-start.1
  39.0 0.7 collective-permute-start
  39.7 1.3 %collective-permute-start.3 = (bf16[2,256,256]{2,1,0:T(8,128)(2,1)S(1)}, bf16[2,256,256]{2,1,0:T(8,128)(2,1)}, u32[]{:S(2)}, u32[]{:S(2)}) collective-permute-start(bf16[2,256,256]{2,1,0:T(8,128)(2,1)S(1)} %slice.48), channel_id=1, source_target_pairs={{6,4},{7,5},{14,12},{15,13},{22,20},{23,21},{30,28},{31,29},{38,36... | collective-permute-start | bytes 786440 | tf_op jit(solution)/shard_map/ppermute | solution.py:152
  41.1 0.7 copy-done.2
  41.8 1.3 %collective-permute-start.2 = (bf16[2,256,256]{2,1,0:T(8,128)(2,1)S(1)}, bf16[2,256,256]{2,1,0:T(8,128)(2,1)}, u32[]{:S(2)}, u32[]{:S(2)}) collective-permute-start(bf16[2,256,256]{2,1,0:T(8,128)(2,1)S(1)} %slice.47), channel_id=1, source_target_pairs={{2,4},{3,5},{10,12},{11,13},{18,20},{19,21},{26,28},{27,29},{34,36... | collective-permute-start | bytes 786440 | tf_op jit(solution)/shard_map/ppermute | solution.py:151
  43.1 5.6 %all-to-all-done.2.got = bf16[16,112,256]{2,1,0:T(8,128)(2,1)S(1)} async-done(((bf16[16,112,256]{2,1,0:T(8,128)(2,1)}), bf16[16,112,256]{2,1,0:T(8,128)(2,1)S(1)}, u32[]{:S(2)}, u32[]{:S(2)}) %all-to-all-start.2) | async-done | bytes 917536 | tf_op jit(solution)/shard_map/all_to_all | solution.py:161
  48.7 4.3 %collective-permute-start.5 = (bf16[16,112,256]{2,1,0:T(8,128)(2,1)S(1)}, bf16[16,112,256]{2,1,0:T(8,128)(2,1)}, u32[]{:S(2)}, u32[]{:S(2)}) collective-permute-start(bf16[16,112,256]{2,1,0:T(8,128)(2,1)S(1)} %all-to-all-done.2.got), channel_id=1, source_target_pairs={{0,1},{1,0},{2,3},{3,2},{4,5},{5,4},{6,7},{7,6},{8,9},{9,8},{10,11... | collective-permute-start | bytes 2752520 | tf_op jit(solution)/shard_map/ppermute | solution.py:19
  53.1 17.6 %collective-permute-done.3 = bf16[2,256,256]{2,1,0:T(8,128)(2,1)} collective-permute-done((bf16[2,256,256]{2,1,0:T(8,128)(2,1)S(1)}, bf16[2,256,256]{2,1,0:T(8,128)(2,1)}, u32[]{:S(2)}, u32[]{:S(2)}) %collective-permute-start.3) | collective-permute-done | bytes 262176 | tf_op jit(solution)/shard_map/ppermute | solution.py:152
  70.7 1.5 %fusion.own = bf16[4,256,256]{2,1,0:T(8,128)(2,1)S(1)} fusion(bf16[2,256,256]{2,1,0:T(8,128)(2,1)} %collective-permute-done.3, bf16[2,256,256]{2,1,0:T(8,128)(2,1)} %collective-permute-done.2, bf16[4,256,256]{2,1,0:T(8,128)(2,1)} %copy-done.2, bf16[4,256,256]{2,1,0:T(8,128)(2,1)} %copy-done.1, pred[]{:T(512)S(6)} %eq.3, ...), kind=kLoop, calls=%fused_computation.3 | loop fusion | flops 1048576 | bytes 2621441 | tf_op jit(solution)/shard_map/select_n | solution.py:167
  72.2 1.6 %collective-permute-start.4 = (bf16[4,256,256]{2,1,0:T(8,128)(2,1)S(1)}, bf16[4,256,256]{2,1,0:T(8,128)(2,1)}, u32[]{:S(2)}, u32[]{:S(2)}) collective-permute-start(bf16[4,256,256]{2,1,0:T(8,128)(2,1)S(1)} %fusion.own), channel_id=1, source_target_pairs={{0,1},{1,0},{2,3},{3,2},{4,5},{5,4},{6,7},{7,6},{8,9},{9,8},{10,11... | collective-permute-start | bytes 1572872 | tf_op jit(solution)/shard_map/ppermute | solution.py:19
  73.8 0.1 copy.9
  73.9 0.1 reshape.24
  74.0 0.1 pad_add_fusion.place
  74.0 1.0 %broadcast_multiply_fusion.wt = bf16[2,256,256]{2,1,0:T(8,128)(2,1)S(1)} fusion(bf16[2,256,256]{2,1,0:T(8,128)(2,1)} %param.6, bf16[]{:T(256)S(6)} %select_n.16), kind=kLoop, calls=%fused_computation.6 | loop fusion | flops 131072 | bytes 524290 | tf_op jit(solution)/shard_map/mul | solution.py:163
  75.0 0.4 collective-permute-done.4.other_hbm
  75.5 5.0 %finish.1 = (bf16[2,4,256,256]{3,2,1,0:T(8,128)(2,1)S(1)}, bf16[4,256,512]{2,1,0:T(8,128)(2,1)}) custom-call(s32[11]{0:T(128)S(1)} %pad_add_fusion.place, bf16[4,256,256]{2,1,0:T(8,128)(2,1)S(1)} %fusion.own, bf16[4,256,256]{2,1,0:T(8,128)(2,1)} %collective-permute-done.4.other_hbm, bf16[16,112,256]{2,1,0:T(8,128)(2,1)S(1)} %all-to-all-done.2.got, ...), custom_call_target="tpu_custom_call" | custom-call | tf_op jit(solution)/shard_map/finish/pallas_call | solution.py:173
  80.4 2.0 %copy.11 = bf16[4,256,2,256]{3,2,1,0:T(2,128)(2,1)} copy(bf16[4,256,2,256]{3,1,0,2:T(8,128)(2,1)S(1)} %bitcast.34) | data formatting | bytes 2097152
  (25 shorter events, 0.2 us)
Async XLA Ops:
  0.6 0.7 copy-start.3
  1.3 1.5 %copy-start = (bf16[4,256,512]{2,1,0:T(8,128)(2,1)S(1)}, bf16[4,256,512]{2,1,0:T(8,128)(2,1)}, u32[]{:S(2)}) copy-start(bf16[4,256,512]{2,1,0:T(8,128)(2,1)} %samples.1) | copy-start | bytes 3145732
  33.1 15.6 %all-to-all-start.2 = ((bf16[16,112,256]{2,1,0:T(8,128)(2,1)}), bf16[16,112,256]{2,1,0:T(8,128)(2,1)S(1)}, u32[]{:S(2)}, u32[]{:S(2)}) async-start(bf16[16,112,256]{2,1,0:T(8,128)(2,1)} %bitcast.35), calls=%async_computation.2 | async-start | bytes 1835008 | tf_op jit(solution)/shard_map/all_to_all | solution.py:161
  38.3 1.4 %collective-permute-start.1 = (bf16[4,256,256]{2,1,0:T(8,128)(2,1)S(1)}, bf16[4,256,256]{2,1,0:T(8,128)(2,1)S(1)}, u32[]{:S(2)}, u32[]{:S(2)}) collective-permute-start(bf16[4,256,256]{2,1,0:T(8,128)(2,1)S(1)} %slice_bitcast_fusion), channel_id=1, source_target_pairs={{0,6},{1,7},{8,14},{9,15},{16,22},{17,23},{24,30},{25,31},{32,38},... | collective-permute-start | bytes 1572872 | tf_op jit(solution)/shard_map/ppermute | solution.py:150
  39.0 2.1 %collective-permute-start = (bf16[4,256,256]{2,1,0:T(8,128)(2,1)S(1)}, bf16[4,256,256]{2,1,0:T(8,128)(2,1)S(1)}, u32[]{:S(2)}, u32[]{:S(2)}) collective-permute-start(bf16[4,256,256]{2,1,0:T(8,128)(2,1)S(1)} %slice_bitcast_fusion), channel_id=1, source_target_pairs={{0,2},{1,3},{8,10},{9,11},{16,18},{17,19},{24,26},{25,27},{32,34},... | collective-permute-start | bytes 1572872 | tf_op jit(solution)/shard_map/ppermute | solution.py:149
  39.7 1.4 %copy-start.1 = (bf16[4,256,256]{2,1,0:T(8,128)(2,1)}, bf16[4,256,256]{2,1,0:T(8,128)(2,1)S(1)}, u32[]{:S(2)}) copy-start(bf16[4,256,256]{2,1,0:T(8,128)(2,1)S(1)} %collective-permute-done.1) | copy-start | bytes 1572868
  39.7 31.0 %collective-permute-start.3 = (bf16[2,256,256]{2,1,0:T(8,128)(2,1)S(1)}, bf16[2,256,256]{2,1,0:T(8,128)(2,1)}, u32[]{:S(2)}, u32[]{:S(2)}) collective-permute-start(bf16[2,256,256]{2,1,0:T(8,128)(2,1)S(1)} %slice.48), channel_id=1, source_target_pairs={{6,4},{7,5},{14,12},{15,13},{22,20},{23,21},{30,28},{31,29},{38,36... | collective-permute-start | bytes 786440 | tf_op jit(solution)/shard_map/ppermute | solution.py:152
  41.0 0.8 copy-start.2
  41.8 28.9 %collective-permute-start.2 = (bf16[2,256,256]{2,1,0:T(8,128)(2,1)S(1)}, bf16[2,256,256]{2,1,0:T(8,128)(2,1)}, u32[]{:S(2)}, u32[]{:S(2)}) collective-permute-start(bf16[2,256,256]{2,1,0:T(8,128)(2,1)S(1)} %slice.47), channel_id=1, source_target_pairs={{2,4},{3,5},{10,12},{11,13},{18,20},{19,21},{26,28},{27,29},{34,36... | collective-permute-start | bytes 786440 | tf_op jit(solution)/shard_map/ppermute | solution.py:151
  48.7 26.7 %collective-permute-start.5 = (bf16[16,112,256]{2,1,0:T(8,128)(2,1)S(1)}, bf16[16,112,256]{2,1,0:T(8,128)(2,1)}, u32[]{:S(2)}, u32[]{:S(2)}) collective-permute-start(bf16[16,112,256]{2,1,0:T(8,128)(2,1)S(1)} %all-to-all-done.2.got), channel_id=1, source_target_pairs={{0,1},{1,0},{2,3},{3,2},{4,5},{5,4},{6,7},{7,6},{8,9},{9,8},{10,11... | collective-permute-start | bytes 2752520 | tf_op jit(solution)/shard_map/ppermute | solution.py:19
  72.2 3.3 %collective-permute-start.4 = (bf16[4,256,256]{2,1,0:T(8,128)(2,1)S(1)}, bf16[4,256,256]{2,1,0:T(8,128)(2,1)}, u32[]{:S(2)}, u32[]{:S(2)}) collective-permute-start(bf16[4,256,256]{2,1,0:T(8,128)(2,1)S(1)} %fusion.own), channel_id=1, source_target_pairs={{0,1},{1,0},{2,3},{3,2},{4,5},{5,4},{6,7},{7,6},{8,9},{9,8},{10,11... | collective-permute-start | bytes 1572872 | tf_op jit(solution)/shard_map/ppermute | solution.py:19

commit v3 on v2

--- a/solution.py
+++ b/solution.py
@@ -35,9 +35,11 @@
     return jnp.where(cond, value, jnp.zeros_like(value))
 
 
-def finish(k, place, f0, f1, g0, g1, w, m, samples, slab, solved, lrow, lcol, ys, obuf, sem, arrival):
+def finish(k, place, f0, f1, g0, g1, m0, m1, samples, slab, solved, lrow, lcol, ys, obuf, sem, arrival):
     row_pos = place[0]
     col_pos = place[1]
+    w = (f0[TR], f0[TR + 1])
+    m = (m0, m1)
 
     def tile(ref, at):
         return ref[:, at * RB : (at + 1) * RB, :].reshape(T, T)
@@ -49,8 +51,7 @@
     first_col = [mm(tile(g0, 2 * k + b), w[0]).astype(BF16) for b in range(TC)]
     first_col[0] = keep(col_pos >= 1, first_col[0])
     y0 = tmm(w[0], jnp.concatenate([tile(g0, 5), tile(g1, 5)], axis=1)).astype(BF16)
-    arrival.wait()
-    first_row = mm(f0[...].reshape(TR * T, T), w[0]).astype(BF16)
+    first_row = mm(f0[0:TR].reshape(TR * T, T), w[0]).astype(BF16)
     first_row = [first_row[a * T : (a + 1) * T] for a in range(TR)]
     first_row[0] = keep(row_pos >= 1, first_row[0])
     ys[0:T, :] = y0
@@ -71,6 +72,7 @@
         lrow[a * T : (a + 1) * T, T : 2 * T] = keep(row_pos >= 2, third) if a == 0 else third
     ys[T : 2 * T, :] = tmm(w[1], r1.astype(BF16)).astype(BF16)
 
+    arrival.wait()
     for a in range(TR):
         rows = lrow[a * T : (a + 1) * T, :]
         obuf[a] = (samples[a].astype(F32) - mm(rows, ys[...])).astype(BF16)
@@ -89,7 +91,7 @@
     for a in range(TR):
         product = mmt(lrow[a * T : (a + 1) * T, :], lcol[...])
         for b in range(TC):
-            rest = (m[b, a].astype(F32) - product[:, b * T : (b + 1) * T]).astype(BF16)
+            rest = (m[b][a].astype(F32) - product[:, b * T : (b + 1) * T]).astype(BF16)
             rest = keep(place[3 + 2 * a + b] != 0, rest)
             slab[b, a] = lax.select(col_pos >= 2, rest, slab[0, 0]) if (a, b) == (0, 0) else rest
 
@@ -118,19 +120,19 @@
     out.wait()
 
 
-def finish_kernel(place, own, other_hbm, got, got_o, wt, m, samples, *rest):
-    *rest, other, other_sem = rest
-    arrival = pltpu.make_async_copy(other_hbm, other, other_sem)
+def finish_kernel(place, rows0, rows1, got, got_o, m0, m1, samples_far, *rest):
+    *rest, samples, samples_sem = rest
+    arrival = pltpu.make_async_copy(samples_far, samples, samples_sem)
     arrival.start()
-    rest = (*rest, arrival)
+    rest = (m0, m1, samples, *rest, arrival)
 
     @pl.when(place[2] == 0)
     def _():
-        finish(0, place, own, other, got, got_o, wt, m, samples, *rest)
+        finish(0, place, rows0, rows1, got, got_o, *rest)
 
     @pl.when(place[2] == 1)
     def _():
-        finish(1, place, other, own, got_o, got, wt, m, samples, *rest)
+        finish(1, place, rows0, rows1, got_o, got, *rest)
 
 
 def body(front, fill, w, samples):
@@ -138,9 +140,8 @@
     z = lax.axis_index("z")
     y = lax.axis_index("y")
     k = lax.axis_index("core")
-    tiles = front.transpose(2, 0, 1, 3) * fill.astype(BF16).transpose(2, 0, 1, 3)
-    tiles = lax.optimization_barrier(tiles)
-    panel = tiles[0]
+    pattern = fill.astype(BF16)
+    panel = lax.optimization_barrier(front[:, :, 0, :] * pattern[:, :, 0, :])
 
     piece = lax.dynamic_slice(samples, (0, 0, k * T), (1, T, T))
     send = jnp.concatenate([panel[0].reshape(Q, RB, T), piece.reshape(Q, RB, T)], axis=1)
@@ -148,8 +149,7 @@
 
     right = lax.ppermute(panel, "y", [(0, 1)])
     left = lax.ppermute(panel, "y", [(0, 3)])
-    lower = lax.ppermute(right[: TR // 2], "y", [(1, 2)])
-    upper = lax.ppermute(left[TR // 2 :], "y", [(3, 2)])
+    far = lax.ppermute(right, "y", [(1, 2)])
 
     send = jnp.concatenate([got[0, :RB], got[Y, :RB], got[0, RB:]], axis=0)
     got = lax.all_to_all(jnp.broadcast_to(send[None], (Z,) + send.shape), "z", 0, 0)
@@ -160,19 +160,21 @@
     send = jnp.broadcast_to(send[None], (X,) + send.shape).reshape(Q, 7 * RB, T)
     got = lax.all_to_all(send, ("x", "y"), 0, 0)
 
-    wt = w * jnp.where(z >= 0, 1.0, 0.0).astype(BF16)
+    rest = lax.optimization_barrier(front[:, :, 1, :] * pattern[:, :, 1, :])
     place = jnp.stack([x * Z + z, y * K + k, k]).astype(jnp.int32)
     place = jnp.concatenate([place, fill.reshape(TR * TC)])
 
-    own = lax.select(y == 0, panel, right + left + jnp.concatenate([lower, upper]))
+    own = lax.select(y == 0, panel, right + left + far)
     other = swap(own)
+    rows0 = jnp.concatenate([lax.select(k == 0, own, other), w])
+    rows1 = lax.select(k == 0, other, own)
     got_o = swap(got)
 
     vmem = pl.BlockSpec(memory_space=pltpu.VMEM)
     smem = pl.BlockSpec(memory_space=pltpu.SMEM)
     slab, solved = pl.pallas_call(
         finish_kernel,
-        in_specs=[smem, vmem, pl.BlockSpec(memory_space=pl.ANY)] + [vmem] * 5,
+        in_specs=[smem] + [vmem] * 6 + [pl.BlockSpec(memory_space=pltpu.HBM)],
         out_specs=[vmem, pl.BlockSpec(memory_space=pl.ANY)],
         out_shape=[
             jax.ShapeDtypeStruct((TC, TR, T, T), BF16),
@@ -184,20 +186,20 @@
             pltpu.VMEM((2 * T, 2 * T), BF16),
             pltpu.VMEM((TR, T, 2 * T), BF16),
             pltpu.SemaphoreType.DMA,
-            pltpu.VMEM((TR, T, T), BF16),
+            pltpu.VMEM((TR, T, 2 * T), BF16),
             pltpu.SemaphoreType.DMA,
         ],
         compiler_params=pltpu.CompilerParams(vmem_limit_bytes=20 * 1024 * 1024),
         name="finish",
     )(
         place,
-        own,
-        other,
+        rows0,
+        rows1,
         got,
         got_o,
-        wt,
-        tiles,
-        samples,
+        panel,
+        rest,
+        pltpu.with_memory_space_constraint(samples, pltpu.HBM),
     )
     return slab.transpose(1, 2, 0, 3), solved
 

time: 83 us -> 78.5 us (0.946)
  the two profiles are of different devices: /device:TPU:17 before, /device:TPU:1 now
where the time goes in v3:
time: 78.5 us; the launch traced here: 78 us
  waiting for transfers between devices  24.1 us (31%)
  starting transfers between devices  21.1 us (27%)
  blocking collectives  14.8 us (19%)
  local copies, waits for them, and re-layouts  9.76 us (12%)
  other arithmetic  3.94 us (5%)
  Pallas kernels  3.49 us (4%)
  between operations  0.79 us (1%)
    ppermute x1, waiting for transfers between devices, body(): left = lax.ppermute(panel, 'y', [(0, 3)])  17.6 us
    all_to_all x1, blocking collectives, body(): got = lax.all_to_all(send, ('x', 'y'), 0, 0)  14.8 us
    all_to_all x1, starting transfers between devices, body(): lax.all_to_all(jnp.broadcast_to(send[None], (Z,) + send.shape), 'z', 0, 0)  8.19 us
    all_to_all x1, waiting for transfers between devices, body(): lax.all_to_all(jnp.broadcast_to(send[None], (Z,) + send.shape), 'z', 0, 0)  6.45 us
    ppermute x1, starting transfers between devices, body(): left = lax.ppermute(panel, 'y', [(0, 3)])  4.4 us
    slice x1, local copies, waits for them, and re-layouts, body(): rest = lax.optimization_barrier(front[:, :, 1, :] * pattern[:, :, 1, :])  4.22 us
    all_to_all x1, starting transfers between devices, body(): got = lax.all_to_all(send, ('x', 'y'), 0, 0)  3.63 us
    pallas_call x1, Pallas kernels, body(): pl.pallas_call(finish_kernel, in_specs=[smem] + [vmem] * 6 + [pl.BlockSpe...  3.49 us
  transfers between devices with their start and end apart: 7, of which 2 were waited for; matrix products, arithmetic and copies ran while one was open for 6% of the time, Pallas kernels for 0%

profile of v3, /device:TPU:1, one launch (start us, length us, event | category | flops | bytes accessed | tf_op | source)
XLA Modules:
  0.0 78.0 jit_solution(5888621299090494894)
XLA Ops:
  0.6 0.7 copy-done.1
  1.3 4.2 %fusion.2 = (bf16[4,256,1,256]{3,2,1,0:T(2,128)(2,1)}, bf16[4,256,1,256]{3,2,1,0:T(2,128)(2,1)S(1)}) fusion(bf16[4,256,2,256]{3,2,1,0:T(2,128)(2,1)} %param.4), kind=kLoop, calls=%fused_computation.22 | loop fusion | bytes 2097152 | tf_op jit(solution)/shard_map/slice | solution.py:163
  5.5 0.1 fusion.1.m0
  5.7 0.9 %constant_dynamic-slice_fusion = bf16[1,256,256]{2,1,0:T(8,128)(2,1)S(1)} fusion(bf16[4,256,512]{2,1,0:T(8,128)(2,1)} %samples_far.1, s32[]{:T(128)S(6)} %select_n.24), kind=kLoop, calls=%fused_computation.21 | loop fusion | bytes 262148 | tf_op jit(solution)/shard_map/dynamic_slice | solution.py:146
  6.6 14.8 %all_to_all.15 = bf16[16,32,256]{2,1,0:T(8,128)(2,1)S(1)} all-to-all(bf16[16,32,256]{2,1,0:T(8,128)(2,1)S(1)} %pad_maximum_fusion.1), channel_id=1, replica_groups=mesh['x'=4,'z'=8,'y'=4,'core'=2] {'x','y'}, dimensions={0} | all-to-all | bytes 524288 | tf_op jit(solution)/shard_map/all_to_all | solution.py:148
  21.5 0.7 broadcast_in_dim.6
  22.2 8.2 %all-to-all-start.1 = ((bf16[8,48,256]{2,1,0:T(8,128)(2,1)}), bf16[8,48,256]{2,1,0:T(8,128)(2,1)S(1)}, u32[]{:S(2)}, u32[]{:S(2)}) async-start(bf16[8,48,256]{2,1,0:T(8,128)(2,1)} %broadcast_in_dim.6), calls=%async_computation.1 | async-start | bytes 393216 | tf_op jit(solution)/shard_map/all_to_all | solution.py:155
  30.3 2.3 %collective-permute-start = (bf16[4,256,256]{2,1,0:T(8,128)(2,1)S(1)}, bf16[4,256,256]{2,1,0:T(8,128)(2,1)S(1)}, u32[]{:S(2)}, u32[]{:S(2)}) collective-permute-start(bf16[4,256,256]{2,1,0:T(8,128)(2,1)S(1)} %fusion.1.m0), channel_id=1, source_target_pairs={{0,2},{1,3},{8,10},{9,11},{16,18},{17,19},{24,26},{25,27},{32,34},... | collective-permute-start | bytes 1572872 | tf_op jit(solution)/shard_map/ppermute | solution.py:150
  32.6 6.5 %all-to-all-done.1 = bf16[8,48,256]{2,1,0:T(8,128)(2,1)S(1)} async-done(((bf16[8,48,256]{2,1,0:T(8,128)(2,1)}), bf16[8,48,256]{2,1,0:T(8,128)(2,1)S(1)}, u32[]{:S(2)}, u32[]{:S(2)}) %all-to-all-start.1) | async-done | bytes 196640 | tf_op jit(solution)/shard_map/all_to_all | solution.py:155
  39.2 1.0 %broadcast_in_dim.8 = bf16[4,4,112,256]{3,2,1,0:T(8,128)(2,1)} broadcast(bf16[4,112,256]{2,1,0:T(8,128)(2,1)S(1)} %pad_maximum_fusion.2), dimensions={1,2,3} | broadcast | bytes 1146880 | tf_op jit(solution)/shard_map/broadcast_in_dim | solution.py:160
  40.2 3.6 %all-to-all-start.2 = ((bf16[16,112,256]{2,1,0:T(8,128)(2,1)}), bf16[16,112,256]{2,1,0:T(8,128)(2,1)S(1)}, u32[]{:S(2)}, u32[]{:S(2)}) async-start(bf16[16,112,256]{2,1,0:T(8,128)(2,1)} %bitcast.15), calls=%async_computation.2 | async-start | bytes 1835008 | tf_op jit(solution)/shard_map/all_to_all | solution.py:161
  43.8 4.4 %collective-permute-start.1 = (bf16[4,256,256]{2,1,0:T(8,128)(2,1)S(1)}, bf16[4,256,256]{2,1,0:T(8,128)(2,1)S(1)}, u32[]{:S(2)}, u32[]{:S(2)}) collective-permute-start(bf16[4,256,256]{2,1,0:T(8,128)(2,1)S(1)} %fusion.1.m0), channel_id=1, source_target_pairs={{0,6},{1,7},{8,14},{9,15},{16,22},{17,23},{24,30},{25,31},{32,38},... | collective-permute-start | bytes 1572872 | tf_op jit(solution)/shard_map/ppermute | solution.py:151
  48.2 1.5 %collective-permute-start.2 = (bf16[4,256,256]{2,1,0:T(8,128)(2,1)S(1)}, bf16[4,256,256]{2,1,0:T(8,128)(2,1)}, u32[]{:S(2)}, u32[]{:S(2)}) collective-permute-start(bf16[4,256,256]{2,1,0:T(8,128)(2,1)S(1)} %collective-permute-done), channel_id=1, source_target_pairs={{2,4},{3,5},{10,12},{11,13},{18,20},{19,21},{26,28},{27,29},{34,36... | collective-permute-start | bytes 1572872 | tf_op jit(solution)/shard_map/ppermute | solution.py:152
  49.7 17.6 %collective-permute-done.1 = bf16[4,256,256]{2,1,0:T(8,128)(2,1)S(1)} collective-permute-done((bf16[4,256,256]{2,1,0:T(8,128)(2,1)S(1)}, bf16[4,256,256]{2,1,0:T(8,128)(2,1)S(1)}, u32[]{:S(2)}, u32[]{:S(2)}) %collective-permute-start.1) | collective-permute-done | bytes 524320 | tf_op jit(solution)/shard_map/ppermute | solution.py:151
  67.3 1.1 %add_select_fusion = bf16[4,256,256]{2,1,0:T(8,128)(2,1)S(1)} fusion(bf16[4,256,256]{2,1,0:T(8,128)(2,1)S(1)} %fusion.1.m0, bf16[4,256,256]{2,1,0:T(8,128)(2,1)} %collective-permute-done.2, bf16[4,256,256]{2,1,0:T(8,128)(2,1)S(1)} %collective-permute-done, bf16[4,256,256]{2,1,0:T(8,128)(2,1)S(1)} %collective-permute-done.1, pred[]{:T(512)S(6)} %eq.8), kind=kLoop, calls=%fused_computation.5 | loop fusion | flops 786432 | bytes 2621441 | tf_op jit(solution)/shard_map/select_n | solution.py:167
  68.4 1.0 %collective-permute-start.3 = (bf16[4,256,256]{2,1,0:T(8,128)(2,1)S(1)}, bf16[4,256,256]{2,1,0:T(8,128)(2,1)}, u32[]{:S(2)}, u32[]{:S(2)}) collective-permute-start(bf16[4,256,256]{2,1,0:T(8,128)(2,1)S(1)} %add_select_fusion), channel_id=1, source_target_pairs={{0,1},{1,0},{2,3},{3,2},{4,5},{5,4},{6,7},{7,6},{8,9},{9,8},{10,11... | collective-permute-start | bytes 1572872 | tf_op jit(solution)/shard_map/ppermute | solution.py:19
  69.4 0.1 collective-permute-start.4
  69.5 0.1 copy.10
  69.6 0.1 reshape.24
  69.7 1.3 %fusion.m1 = bf16[4,256,256]{2,1,0:T(8,128)(2,1)S(1)} fusion(bf16[4,256,1,256]{3,2,1,0:T(2,128)(2,1)} %get-tuple-element.10, bf16[4]{0:T(256)(128)(2,1)S(1)} %get-tuple-element.20), kind=kLoop, calls=%fused_computation.2 | loop fusion | flops 262144 | bytes 1048584 | tf_op jit(solution)/shard_map/mul | solution.py:163
  71.1 0.1 pad_add_fusion.place
  71.1 1.2 %broadcast_select_fusion = (bf16[4,256,256]{2,1,0:T(8,128)(2,1)S(1)}, bf16[4,256,256]{2,1,0:T(8,128)(2,1)S(1)}) fusion(bf16[4,256,256]{2,1,0:T(8,128)(2,1)} %collective-permute-done.3, bf16[4,256,256]{2,1,0:T(8,128)(2,1)S(1)} %add_select_fusion, pred[]{:T(512)S(6)} %eq.7), kind=kLoop, calls=%fused_computation.6 | loop fusion | flops 524288 | bytes 2097153 | tf_op jit(solution)/shard_map/select_n | solution.py:170
  72.4 3.5 %finish.1 = (bf16[2,4,256,256]{3,2,1,0:T(8,128)(2,1)S(1)}, bf16[4,256,512]{2,1,0:T(8,128)(2,1)}) custom-call(s32[11]{0:T(128)S(1)} %pad_add_fusion.place, bf16[6,256,256]{2,1,0:T(8,128)(2,1)S(1)} %pad_maximum_fusion.rows0, bf16[4,256,256]{2,1,0:T(8,128)(2,1)S(1)} %get-tuple-element.12.rows1, bf16[16,112,256]{2,1,0:T(8,128)(2,1)S(1)} %all-to-all-done.2.got, ...), custom_call_target="tpu_custom_call" | custom-call | tf_op jit(solution)/shard_map/finish/pallas_call | solution.py:175
  75.9 2.0 %copy.13 = bf16[4,256,2,256]{3,2,1,0:T(2,128)(2,1)} copy(bf16[4,256,2,256]{3,1,0,2:T(8,128)(2,1)S(1)} %bitcast.35) | data formatting | bytes 2097152
  (20 shorter events, 0.2 us)
Async XLA Ops:
  0.6 0.7 copy-start.1
  22.2 16.9 %all-to-all-start.1 = ((bf16[8,48,256]{2,1,0:T(8,128)(2,1)}), bf16[8,48,256]{2,1,0:T(8,128)(2,1)S(1)}, u32[]{:S(2)}, u32[]{:S(2)}) async-start(bf16[8,48,256]{2,1,0:T(8,128)(2,1)} %broadcast_in_dim.6), calls=%async_computation.1 | async-start | bytes 393216 | tf_op jit(solution)/shard_map/all_to_all | solution.py:155
  30.3 17.9 %collective-permute-start = (bf16[4,256,256]{2,1,0:T(8,128)(2,1)S(1)}, bf16[4,256,256]{2,1,0:T(8,128)(2,1)S(1)}, u32[]{:S(2)}, u32[]{:S(2)}) collective-permute-start(bf16[4,256,256]{2,1,0:T(8,128)(2,1)S(1)} %fusion.1.m0), channel_id=1, source_target_pairs={{0,2},{1,3},{8,10},{9,11},{16,18},{17,19},{24,26},{25,27},{32,34},... | collective-permute-start | bytes 1572872 | tf_op jit(solution)/shard_map/ppermute | solution.py:150
  40.2 29.3 %all-to-all-start.2 = ((bf16[16,112,256]{2,1,0:T(8,128)(2,1)}), bf16[16,112,256]{2,1,0:T(8,128)(2,1)S(1)}, u32[]{:S(2)}, u32[]{:S(2)}) async-start(bf16[16,112,256]{2,1,0:T(8,128)(2,1)} %bitcast.15), calls=%async_computation.2 | async-start | bytes 1835008 | tf_op jit(solution)/shard_map/all_to_all | solution.py:161
  43.8 23.5 %collective-permute-start.1 = (bf16[4,256,256]{2,1,0:T(8,128)(2,1)S(1)}, bf16[4,256,256]{2,1,0:T(8,128)(2,1)S(1)}, u32[]{:S(2)}, u32[]{:S(2)}) collective-permute-start(bf16[4,256,256]{2,1,0:T(8,128)(2,1)S(1)} %fusion.1.m0), channel_id=1, source_target_pairs={{0,6},{1,7},{8,14},{9,15},{16,22},{17,23},{24,30},{25,31},{32,38},... | collective-permute-start | bytes 1572872 | tf_op jit(solution)/shard_map/ppermute | solution.py:151
  48.2 19.1 %collective-permute-start.2 = (bf16[4,256,256]{2,1,0:T(8,128)(2,1)S(1)}, bf16[4,256,256]{2,1,0:T(8,128)(2,1)}, u32[]{:S(2)}, u32[]{:S(2)}) collective-permute-start(bf16[4,256,256]{2,1,0:T(8,128)(2,1)S(1)} %collective-permute-done), channel_id=1, source_target_pairs={{2,4},{3,5},{10,12},{11,13},{18,20},{19,21},{26,28},{27,29},{34,36... | collective-permute-start | bytes 1572872 | tf_op jit(solution)/shard_map/ppermute | solution.py:152
  68.4 2.7 %collective-permute-start.3 = (bf16[4,256,256]{2,1,0:T(8,128)(2,1)S(1)}, bf16[4,256,256]{2,1,0:T(8,128)(2,1)}, u32[]{:S(2)}, u32[]{:S(2)}) collective-permute-start(bf16[4,256,256]{2,1,0:T(8,128)(2,1)S(1)} %add_select_fusion), channel_id=1, source_target_pairs={{0,1},{1,0},{2,3},{3,2},{4,5},{5,4},{6,7},{7,6},{8,9},{9,8},{10,11... | collective-permute-start | bytes 1572872 | tf_op jit(solution)/shard_map/ppermute | solution.py:19
  69.4 3.0 %collective-permute-start.4 = (bf16[16,112,256]{2,1,0:T(8,128)(2,1)S(1)}, bf16[16,112,256]{2,1,0:T(8,128)(2,1)S(1)}, u32[]{:S(2)}, u32[]{:S(2)}) collective-permute-start(bf16[16,112,256]{2,1,0:T(8,128)(2,1)S(1)} %all-to-all-done.2.got), channel_id=1, source_target_pairs={{0,1},{1,0},{2,3},{3,2},{4,5},{5,4},{6,7},{7,6},{8,9},{9,8},{10,11... | collective-permute-start | bytes 2752520 | tf_op jit(solution)/shard_map/ppermute | solution.py:19
  71.1 1.2 %copy-start = (bf16[2,256,256]{2,1,0:T(8,128)(2,1)S(1)}, bf16[2,256,256]{2,1,0:T(8,128)(2,1)}, u32[]{:S(2)}) copy-start(bf16[2,256,256]{2,1,0:T(8,128)(2,1)} %param.6) | copy-start | bytes 786436

commit v4 on v3

--- a/solution.py
+++ b/solution.py
@@ -140,8 +140,10 @@
     z = lax.axis_index("z")
     y = lax.axis_index("y")
     k = lax.axis_index("core")
-    pattern = fill.astype(BF16)
-    panel = lax.optimization_barrier(front[:, :, 0, :] * pattern[:, :, 0, :])
+    tiles = front.transpose(2, 0, 1, 3) * fill.astype(BF16).transpose(2, 0, 1, 3)
+    tiles = lax.optimization_barrier(tiles)
+
+    panel = lax.optimization_barrier(tiles[0])
 
     piece = lax.dynamic_slice(samples, (0, 0, k * T), (1, T, T))
     send = jnp.concatenate([panel[0].reshape(Q, RB, T), piece.reshape(Q, RB, T)], axis=1)
@@ -160,7 +162,7 @@
     send = jnp.broadcast_to(send[None], (X,) + send.shape).reshape(Q, 7 * RB, T)
     got = lax.all_to_all(send, ("x", "y"), 0, 0)
 
-    rest = lax.optimization_barrier(front[:, :, 1, :] * pattern[:, :, 1, :])
+    rest = tiles[1]
     place = jnp.stack([x * Z + z, y * K + k, k]).astype(jnp.int32)
     place = jnp.concatenate([place, fill.reshape(TR * TC)])
 

time: 78.5 us -> 76.5 us (0.975)
  local copies, waits for them, and re-layouts: 9.76 us -> 6.4 us
  waiting for transfers between devices: 24.1 us -> 25.4 us
    slice x1 -> x0, local copies, waits for them, and re-layouts: 4.22 us -> none  [body(): rest = lax.optimization_barrier(front[:, :, 1, :] * pattern[:, :, 1, :])]
    ppermute x2, waiting for transfers between devices: 0.01 us -> 1.3 us  [swap(): return lax.ppermute(v, 'core', [(0, 1), (1, 0)])]
    unnamed x6 -> x9, local copies, waits for them, and re-layouts: 2.82 us -> 3.62 us
  transfers between devices with their start and end apart: 7 -> 7, of which waited for: 2 -> 3; matrix products, arithmetic and copies ran while one was open for 6% -> 5% of each run, Pallas kernels for 0% -> 0%
where the time goes in v4:
time: 76.5 us; the launch traced here: 76 us
  waiting for transfers between devices  25.4 us (33%)
  starting transfers between devices  21.1 us (28%)
  blocking collectives  14.8 us (19%)
  local copies, waits for them, and re-layouts  6.4 us (8%)
  other arithmetic  4 us (5%)
  Pallas kernels  3.49 us (5%)
  between operations  0.79 us (1%)
    ppermute x1, waiting for transfers between devices, body(): left = lax.ppermute(panel, 'y', [(0, 3)])  17.6 us
    all_to_all x1, blocking collectives, body(): got = lax.all_to_all(send, ('x', 'y'), 0, 0)  14.8 us
    all_to_all x1, starting transfers between devices, body(): lax.all_to_all(jnp.broadcast_to(send[None], (Z,) + send.shape), 'z', 0, 0)  8.19 us
    all_to_all x1, waiting for transfers between devices, body(): lax.all_to_all(jnp.broadcast_to(send[None], (Z,) + send.shape), 'z', 0, 0)  6.45 us
    ppermute x1, starting transfers between devices, body(): left = lax.ppermute(panel, 'y', [(0, 3)])  4.4 us
    all_to_all x1, starting transfers between devices, body(): got = lax.all_to_all(send, ('x', 'y'), 0, 0)  3.63 us
    unnamed x9, local copies, waits for them, and re-layouts  3.62 us
    pallas_call x1, Pallas kernels, body(): pl.pallas_call(finish_kernel, in_specs=[smem] + [vmem] * 6 + [pl.BlockSpe...  3.49 us
  transfers between devices with their start and end apart: 7, of which 3 were waited for; matrix products, arithmetic and copies ran while one was open for 5% of the time, Pallas kernels for 0%

profile of v4, /device:TPU:1, one launch (start us, length us, event | category | flops | bytes accessed | tf_op | source)
XLA Modules:
  0.0 76.0 jit_solution(10356018813605773029)
XLA Ops:
  0.6 0.7 copy-done.2
  1.3 1.4 %bitcast_multiply_fusion = bf16[2,4,256,256]{3,2,1,0:T(8,128)(2,1)S(1)} fusion(bf16[4,256,2,256]{3,2,1,0:T(2,128)(2,1)} %param.4, bf16[2,4]{1,0:T(2,128)(2,1)S(1)} %bitcast.39), kind=kLoop, calls=%fused_computation | loop fusion | flops 524288 | bytes 2097168 | tf_op jit(solution)/shard_map/mul | solution.py:143
  2.8 0.9 %constant_dynamic-slice_fusion = bf16[1,256,256]{2,1,0:T(8,128)(2,1)S(1)} fusion(bf16[4,256,512]{2,1,0:T(8,128)(2,1)} %samples_far.1, s32[]{:T(128)S(6)} %select_n.24), kind=kLoop, calls=%fused_computation.20 | loop fusion | bytes 262148 | tf_op jit(solution)/shard_map/dynamic_slice | solution.py:148
  3.8 14.8 %all_to_all.15 = bf16[16,32,256]{2,1,0:T(8,128)(2,1)S(1)} all-to-all(bf16[16,32,256]{2,1,0:T(8,128)(2,1)S(1)} %pad_maximum_fusion.1), channel_id=1, replica_groups=mesh['x'=4,'z'=8,'y'=4,'core'=2] {'x','y'}, dimensions={0} | all-to-all | bytes 524288 | tf_op jit(solution)/shard_map/all_to_all | solution.py:150
  18.6 0.7 broadcast_in_dim.6
  19.3 8.2 %all-to-all-start.1 = ((bf16[8,48,256]{2,1,0:T(8,128)(2,1)}), bf16[8,48,256]{2,1,0:T(8,128)(2,1)S(1)}, u32[]{:S(2)}, u32[]{:S(2)}) async-start(bf16[8,48,256]{2,1,0:T(8,128)(2,1)} %broadcast_in_dim.6), calls=%async_computation.1 | async-start | bytes 393216 | tf_op jit(solution)/shard_map/all_to_all | solution.py:157
  27.5 2.3 %collective-permute-start = (bf16[4,256,256]{2,1,0:T(8,128)(2,1)S(1)}, bf16[4,256,256]{2,1,0:T(8,128)(2,1)S(1)}, u32[]{:S(2)}, u32[]{:S(2)}) collective-permute-start(bf16[4,256,256]{2,1,0:T(8,128)(2,1)S(1)} %get-tuple-element.11.m0), channel_id=1, source_target_pairs={{0,2},{1,3},{8,10},{9,11},{16,18},{17,19},{24,26},{25,27},{32,34},... | collective-permute-start | bytes 1572872 | tf_op jit(solution)/shard_map/ppermute | solution.py:152
  29.8 6.5 %all-to-all-done.1 = bf16[8,48,256]{2,1,0:T(8,128)(2,1)S(1)} async-done(((bf16[8,48,256]{2,1,0:T(8,128)(2,1)}), bf16[8,48,256]{2,1,0:T(8,128)(2,1)S(1)}, u32[]{:S(2)}, u32[]{:S(2)}) %all-to-all-start.1) | async-done | bytes 196640 | tf_op jit(solution)/shard_map/all_to_all | solution.py:157
  36.3 1.0 %broadcast_in_dim.8 = bf16[4,4,112,256]{3,2,1,0:T(8,128)(2,1)} broadcast(bf16[4,112,256]{2,1,0:T(8,128)(2,1)S(1)} %pad_maximum_fusion.2), dimensions={1,2,3} | broadcast | bytes 1146880 | tf_op jit(solution)/shard_map/broadcast_in_dim | solution.py:162
  37.3 3.6 %all-to-all-start.2 = ((bf16[16,112,256]{2,1,0:T(8,128)(2,1)}), bf16[16,112,256]{2,1,0:T(8,128)(2,1)S(1)}, u32[]{:S(2)}, u32[]{:S(2)}) async-start(bf16[16,112,256]{2,1,0:T(8,128)(2,1)} %bitcast.16), calls=%async_computation.2 | async-start | bytes 1835008 | tf_op jit(solution)/shard_map/all_to_all | solution.py:163
  40.9 4.4 %collective-permute-start.1 = (bf16[4,256,256]{2,1,0:T(8,128)(2,1)S(1)}, bf16[4,256,256]{2,1,0:T(8,128)(2,1)S(1)}, u32[]{:S(2)}, u32[]{:S(2)}) collective-permute-start(bf16[4,256,256]{2,1,0:T(8,128)(2,1)S(1)} %get-tuple-element.11.m0), channel_id=1, source_target_pairs={{0,6},{1,7},{8,14},{9,15},{16,22},{17,23},{24,30},{25,31},{32,38},... | collective-permute-start | bytes 1572872 | tf_op jit(solution)/shard_map/ppermute | solution.py:153
  45.4 1.5 %collective-permute-start.2 = (bf16[4,256,256]{2,1,0:T(8,128)(2,1)S(1)}, bf16[4,256,256]{2,1,0:T(8,128)(2,1)}, u32[]{:S(2)}, u32[]{:S(2)}) collective-permute-start(bf16[4,256,256]{2,1,0:T(8,128)(2,1)S(1)} %collective-permute-done), channel_id=1, source_target_pairs={{2,4},{3,5},{10,12},{11,13},{18,20},{19,21},{26,28},{27,29},{34,36... | collective-permute-start | bytes 1572872 | tf_op jit(solution)/shard_map/ppermute | solution.py:154
  46.8 17.6 %collective-permute-done.1 = bf16[4,256,256]{2,1,0:T(8,128)(2,1)S(1)} collective-permute-done((bf16[4,256,256]{2,1,0:T(8,128)(2,1)S(1)}, bf16[4,256,256]{2,1,0:T(8,128)(2,1)S(1)}, u32[]{:S(2)}, u32[]{:S(2)}) %collective-permute-start.1) | collective-permute-done | bytes 524320 | tf_op jit(solution)/shard_map/ppermute | solution.py:153
  64.4 0.8 %copy-done = bf16[4,256,256]{2,1,0:T(8,128)(2,1)} copy-done((bf16[4,256,256]{2,1,0:T(8,128)(2,1)}, bf16[4,256,256]{2,1,0:T(8,128)(2,1)S(1)}, u32[]{:S(2)}) %copy-start) | copy-done | bytes 524312
  65.2 1.3 %add_select_fusion = bf16[4,256,256]{2,1,0:T(8,128)(2,1)S(1)} fusion(bf16[4,256,256]{2,1,0:T(8,128)(2,1)S(1)} %get-tuple-element.11.m0, bf16[4,256,256]{2,1,0:T(8,128)(2,1)} %collective-permute-done.2, bf16[4,256,256]{2,1,0:T(8,128)(2,1)S(1)} %collective-permute-done, bf16[4,256,256]{2,1,0:T(8,128)(2,1)} %copy-done, pred[]{:T(512)S(6)} %eq.8), kind=kLoop, calls=%fused_computation.4 | loop fusion | flops 786432 | bytes 2621441 | tf_op jit(solution)/shard_map/select_n | solution.py:169
  66.5 1.0 %collective-permute-start.3 = (bf16[4,256,256]{2,1,0:T(8,128)(2,1)S(1)}, bf16[4,256,256]{2,1,0:T(8,128)(2,1)}, u32[]{:S(2)}, u32[]{:S(2)}) collective-permute-start(bf16[4,256,256]{2,1,0:T(8,128)(2,1)S(1)} %add_select_fusion), channel_id=1, source_target_pairs={{0,1},{1,0},{2,3},{3,2},{4,5},{5,4},{6,7},{7,6},{8,9},{9,8},{10,11... | collective-permute-start | bytes 1572872 | tf_op jit(solution)/shard_map/ppermute | solution.py:19
  67.5 0.1 collective-permute-start.4
  67.6 0.1 copy.9
  67.7 0.1 reshape.22
  67.8 0.1 pad_add_fusion.place
  67.9 1.3 %collective-permute-done.3 = bf16[4,256,256]{2,1,0:T(8,128)(2,1)} collective-permute-done((bf16[4,256,256]{2,1,0:T(8,128)(2,1)S(1)}, bf16[4,256,256]{2,1,0:T(8,128)(2,1)}, u32[]{:S(2)}, u32[]{:S(2)}) %collective-permute-start.3) | collective-permute-done | bytes 524320 | tf_op jit(solution)/shard_map/ppermute | solution.py:19
  69.2 1.1 %broadcast_select_fusion = (bf16[4,256,256]{2,1,0:T(8,128)(2,1)S(1)}, bf16[4,256,256]{2,1,0:T(8,128)(2,1)S(1)}) fusion(bf16[4,256,256]{2,1,0:T(8,128)(2,1)} %collective-permute-done.3, bf16[4,256,256]{2,1,0:T(8,128)(2,1)S(1)} %add_select_fusion, pred[]{:T(512)S(6)} %eq.7), kind=kLoop, calls=%fused_computation.5 | loop fusion | flops 524288 | bytes 2097153 | tf_op jit(solution)/shard_map/select_n | solution.py:172
  70.4 3.5 %finish.1 = (bf16[2,4,256,256]{3,2,1,0:T(8,128)(2,1)S(1)}, bf16[4,256,512]{2,1,0:T(8,128)(2,1)}) custom-call(s32[11]{0:T(128)S(1)} %pad_add_fusion.place, bf16[6,256,256]{2,1,0:T(8,128)(2,1)S(1)} %pad_maximum_fusion.rows0, bf16[4,256,256]{2,1,0:T(8,128)(2,1)S(1)} %get-tuple-element.12.rows1, bf16[16,112,256]{2,1,0:T(8,128)(2,1)S(1)} %all-to-all-done.2.got, ...), custom_call_target="tpu_custom_call" | custom-call | tf_op jit(solution)/shard_map/finish/pallas_call | solution.py:177
  73.9 2.0 %copy.11 = bf16[4,256,2,256]{3,2,1,0:T(2,128)(2,1)} copy(bf16[4,256,2,256]{3,1,0,2:T(8,128)(2,1)S(1)} %bitcast.34) | data formatting | bytes 2097152
  (21 shorter events, 0.3 us)
Async XLA Ops:
  0.6 0.7 copy-start.2
  19.3 16.9 %all-to-all-start.1 = ((bf16[8,48,256]{2,1,0:T(8,128)(2,1)}), bf16[8,48,256]{2,1,0:T(8,128)(2,1)S(1)}, u32[]{:S(2)}, u32[]{:S(2)}) async-start(bf16[8,48,256]{2,1,0:T(8,128)(2,1)} %broadcast_in_dim.6), calls=%async_computation.1 | async-start | bytes 393216 | tf_op jit(solution)/shard_map/all_to_all | solution.py:157
  27.5 17.9 %collective-permute-start = (bf16[4,256,256]{2,1,0:T(8,128)(2,1)S(1)}, bf16[4,256,256]{2,1,0:T(8,128)(2,1)S(1)}, u32[]{:S(2)}, u32[]{:S(2)}) collective-permute-start(bf16[4,256,256]{2,1,0:T(8,128)(2,1)S(1)} %get-tuple-element.11.m0), channel_id=1, source_target_pairs={{0,2},{1,3},{8,10},{9,11},{16,18},{17,19},{24,26},{25,27},{32,34},... | collective-permute-start | bytes 1572872 | tf_op jit(solution)/shard_map/ppermute | solution.py:152
  37.3 30.2 %all-to-all-start.2 = ((bf16[16,112,256]{2,1,0:T(8,128)(2,1)}), bf16[16,112,256]{2,1,0:T(8,128)(2,1)S(1)}, u32[]{:S(2)}, u32[]{:S(2)}) async-start(bf16[16,112,256]{2,1,0:T(8,128)(2,1)} %bitcast.16), calls=%async_computation.2 | async-start | bytes 1835008 | tf_op jit(solution)/shard_map/all_to_all | solution.py:163
  40.9 23.5 %collective-permute-start.1 = (bf16[4,256,256]{2,1,0:T(8,128)(2,1)S(1)}, bf16[4,256,256]{2,1,0:T(8,128)(2,1)S(1)}, u32[]{:S(2)}, u32[]{:S(2)}) collective-permute-start(bf16[4,256,256]{2,1,0:T(8,128)(2,1)S(1)} %get-tuple-element.11.m0), channel_id=1, source_target_pairs={{0,6},{1,7},{8,14},{9,15},{16,22},{17,23},{24,30},{25,31},{32,38},... | collective-permute-start | bytes 1572872 | tf_op jit(solution)/shard_map/ppermute | solution.py:153
  45.4 19.9 %collective-permute-start.2 = (bf16[4,256,256]{2,1,0:T(8,128)(2,1)S(1)}, bf16[4,256,256]{2,1,0:T(8,128)(2,1)}, u32[]{:S(2)}, u32[]{:S(2)}) collective-permute-start(bf16[4,256,256]{2,1,0:T(8,128)(2,1)S(1)} %collective-permute-done), channel_id=1, source_target_pairs={{2,4},{3,5},{10,12},{11,13},{18,20},{19,21},{26,28},{27,29},{34,36... | collective-permute-start | bytes 1572872 | tf_op jit(solution)/shard_map/ppermute | solution.py:154
  64.4 0.8 %copy-start = (bf16[4,256,256]{2,1,0:T(8,128)(2,1)}, bf16[4,256,256]{2,1,0:T(8,128)(2,1)S(1)}, u32[]{:S(2)}) copy-start(bf16[4,256,256]{2,1,0:T(8,128)(2,1)S(1)} %collective-permute-done.1) | copy-start | bytes 1572868
  66.5 2.7 %collective-permute-start.3 = (bf16[4,256,256]{2,1,0:T(8,128)(2,1)S(1)}, bf16[4,256,256]{2,1,0:T(8,128)(2,1)}, u32[]{:S(2)}, u32[]{:S(2)}) collective-permute-start(bf16[4,256,256]{2,1,0:T(8,128)(2,1)S(1)} %add_select_fusion), channel_id=1, source_target_pairs={{0,1},{1,0},{2,3},{3,2},{4,5},{5,4},{6,7},{7,6},{8,9},{9,8},{10,11... | collective-permute-start | bytes 1572872 | tf_op jit(solution)/shard_map/ppermute | solution.py:19
  67.5 2.9 %collective-permute-start.4 = (bf16[16,112,256]{2,1,0:T(8,128)(2,1)S(1)}, bf16[16,112,256]{2,1,0:T(8,128)(2,1)S(1)}, u32[]{:S(2)}, u32[]{:S(2)}) collective-permute-start(bf16[16,112,256]{2,1,0:T(8,128)(2,1)S(1)} %all-to-all-done.2.got), channel_id=1, source_target_pairs={{0,1},{1,0},{2,3},{3,2},{4,5},{5,4},{6,7},{7,6},{8,9},{9,8},{10,11... | collective-permute-start | bytes 2752520 | tf_op jit(solution)/shard_map/ppermute | solution.py:19
  67.9 2.4 %copy-start.1 = (bf16[2,256,256]{2,1,0:T(8,128)(2,1)S(1)}, bf16[2,256,256]{2,1,0:T(8,128)(2,1)}, u32[]{:S(2)}) copy-start(bf16[2,256,256]{2,1,0:T(8,128)(2,1)} %param.6) | copy-start | bytes 786436

commit v5 on v4

--- a/solution.py
+++ b/solution.py
@@ -151,7 +151,8 @@
 
     right = lax.ppermute(panel, "y", [(0, 1)])
     left = lax.ppermute(panel, "y", [(0, 3)])
-    far = lax.ppermute(right, "y", [(1, 2)])
+    near = right + left
+    far = lax.ppermute(near, ("y", "core"), [(2, 4), (7, 5)])
 
     send = jnp.concatenate([got[0, :RB], got[Y, :RB], got[0, RB:]], axis=0)
     got = lax.all_to_all(jnp.broadcast_to(send[None], (Z,) + send.shape), "z", 0, 0)
@@ -166,7 +167,7 @@
     place = jnp.stack([x * Z + z, y * K + k, k]).astype(jnp.int32)
     place = jnp.concatenate([place, fill.reshape(TR * TC)])
 
-    own = lax.select(y == 0, panel, right + left + far)
+    own = lax.select(y == 0, panel, near + far)
     other = swap(own)
     rows0 = jnp.concatenate([lax.select(k == 0, own, other), w])
     rows1 = lax.select(k == 0, other, own)

time: 76.5 us -> 71 us (0.928)
  the two profiles are of different devices: /device:TPU:1 before, /device:TPU:81 now
where the time goes in v5:
time: 71 us; the launch traced here: 70.4 us
  waiting for transfers between devices  23.6 us (33%)
  starting transfers between devices  20.5 us (29%)
  blocking collectives  12.5 us (18%)
  local copies, waits for them, and re-layouts  5.61 us (8%)
  other arithmetic  3.95 us (6%)
  Pallas kernels  3.48 us (5%)
  between operations  0.81 us (1%)
    ppermute x1, waiting for transfers between devices, body(): far = lax.ppermute(near, ('y', 'core'), [(2, 4), (7, 5)])  17.6 us
    all_to_all x1, blocking collectives, body(): got = lax.all_to_all(send, ('x', 'y'), 0, 0)  12.5 us
    all_to_all x1, starting transfers between devices, body(): lax.all_to_all(jnp.broadcast_to(send[None], (Z,) + send.shape), 'z', 0, 0)  7.55 us
    ppermute x2, starting transfers between devices, swap(): return lax.ppermute(v, 'core', [(0, 1), (1, 0)])  5.28 us
    all_to_all x1, starting transfers between devices, body(): got = lax.all_to_all(send, ('x', 'y'), 0, 0)  5.04 us
    all_to_all x1, waiting for transfers between devices, body(): lax.all_to_all(jnp.broadcast_to(send[None], (Z,) + send.shape), 'z', 0, 0)  4.64 us
    pallas_call x1, Pallas kernels, body(): pl.pallas_call(finish_kernel, in_specs=[smem] + [vmem] * 6 + [pl.BlockSpe...  3.48 us
    unnamed x7, local copies, waits for them, and re-layouts  2.82 us
  transfers between devices with their start and end apart: 7, of which 3 were waited for; matrix products, arithmetic and copies ran while one was open for 5% of the time, Pallas kernels for 0%

profile of v5, /device:TPU:81, one launch (start us, length us, event | category | flops | bytes accessed | tf_op | source)
XLA Modules:
  0.0 70.4 jit_solution(5195043561780108769)
XLA Ops:
  0.6 0.7 copy-done.1
  1.3 1.4 %bitcast_multiply_fusion = bf16[2,4,256,256]{3,2,1,0:T(8,128)(2,1)S(1)} fusion(bf16[4,256,2,256]{3,2,1,0:T(2,128)(2,1)} %param.4, bf16[2,4]{1,0:T(2,128)(2,1)S(1)} %bitcast.39), kind=kLoop, calls=%fused_computation | loop fusion | flops 524288 | bytes 2097168 | tf_op jit(solution)/shard_map/mul | solution.py:143
  2.8 0.9 %constant_dynamic-slice_fusion = bf16[1,256,256]{2,1,0:T(8,128)(2,1)S(1)} fusion(bf16[4,256,512]{2,1,0:T(8,128)(2,1)} %samples_far.1, s32[]{:T(128)S(6)} %select_n.24), kind=kLoop, calls=%fused_computation.20 | loop fusion | bytes 262148 | tf_op jit(solution)/shard_map/dynamic_slice | solution.py:148
  3.8 12.5 %all_to_all.15 = bf16[16,32,256]{2,1,0:T(8,128)(2,1)S(1)} all-to-all(bf16[16,32,256]{2,1,0:T(8,128)(2,1)S(1)} %pad_maximum_fusion.1), channel_id=1, replica_groups=mesh['x'=4,'z'=8,'y'=4,'core'=2] {'x','y'}, dimensions={0} | all-to-all | bytes 524288 | tf_op jit(solution)/shard_map/all_to_all | solution.py:150
  16.3 0.7 broadcast_in_dim.6
  17.0 7.6 %all-to-all-start.1 = ((bf16[8,48,256]{2,1,0:T(8,128)(2,1)}), bf16[8,48,256]{2,1,0:T(8,128)(2,1)S(1)}, u32[]{:S(2)}, u32[]{:S(2)}) async-start(bf16[8,48,256]{2,1,0:T(8,128)(2,1)} %broadcast_in_dim.6), calls=%async_computation.1 | async-start | bytes 393216 | tf_op jit(solution)/shard_map/all_to_all | solution.py:158
  24.5 0.7 collective-permute-start.1
  25.2 0.7 collective-permute-start
  25.9 4.6 %all-to-all-done.1 = bf16[8,48,256]{2,1,0:T(8,128)(2,1)S(1)} async-done(((bf16[8,48,256]{2,1,0:T(8,128)(2,1)}), bf16[8,48,256]{2,1,0:T(8,128)(2,1)S(1)}, u32[]{:S(2)}, u32[]{:S(2)}) %all-to-all-start.1) | async-done | bytes 196640 | tf_op jit(solution)/shard_map/all_to_all | solution.py:158
  30.6 1.0 %broadcast_in_dim.8 = bf16[4,4,112,256]{3,2,1,0:T(8,128)(2,1)} broadcast(bf16[4,112,256]{2,1,0:T(8,128)(2,1)S(1)} %pad_maximum_fusion.2), dimensions={1,2,3} | broadcast | bytes 1146880 | tf_op jit(solution)/shard_map/broadcast_in_dim | solution.py:163
  31.6 5.0 %all-to-all-start.2 = ((bf16[16,112,256]{2,1,0:T(8,128)(2,1)}), bf16[16,112,256]{2,1,0:T(8,128)(2,1)S(1)}, u32[]{:S(2)}, u32[]{:S(2)}) async-start(bf16[16,112,256]{2,1,0:T(8,128)(2,1)} %bitcast.16), calls=%async_computation.2 | async-start | bytes 1835008 | tf_op jit(solution)/shard_map/all_to_all | solution.py:164
  36.7 0.1 add.17
  36.8 1.3 %collective-permute-start.2 = (bf16[4,256,256]{2,1,0:T(8,128)(2,1)S(1)}, bf16[4,256,256]{2,1,0:T(8,128)(2,1)}, u32[]{:S(2)}, u32[]{:S(2)}) collective-permute-start(bf16[4,256,256]{2,1,0:T(8,128)(2,1)S(1)} %add.17), channel_id=1, source_target_pairs={{2,4},{7,5},{10,12},{15,13},{18,20},{23,21},{26,28},{31,29},{34,36... | collective-permute-start | bytes 1572872 | tf_op jit(solution)/shard_map/ppermute | solution.py:155
  38.1 17.6 %collective-permute-done.2 = bf16[4,256,256]{2,1,0:T(8,128)(2,1)} collective-permute-done((bf16[4,256,256]{2,1,0:T(8,128)(2,1)S(1)}, bf16[4,256,256]{2,1,0:T(8,128)(2,1)}, u32[]{:S(2)}, u32[]{:S(2)}) %collective-permute-start.2) | collective-permute-done | bytes 524320 | tf_op jit(solution)/shard_map/ppermute | solution.py:155
  55.7 1.1 %add_select_fusion = bf16[4,256,256]{2,1,0:T(8,128)(2,1)S(1)} fusion(bf16[4,256,256]{2,1,0:T(8,128)(2,1)S(1)} %get-tuple-element.11.m0, bf16[4,256,256]{2,1,0:T(8,128)(2,1)S(1)} %add.17, bf16[4,256,256]{2,1,0:T(8,128)(2,1)} %collective-permute-done.2, pred[]{:T(512)S(6)} %eq.8), kind=kLoop, calls=%fused_computation.4 | loop fusion | flops 524288 | bytes 2097153 | tf_op jit(solution)/shard_map/select_n | solution.py:170
  56.9 5.2 %collective-permute-start.3 = (bf16[4,256,256]{2,1,0:T(8,128)(2,1)S(1)}, bf16[4,256,256]{2,1,0:T(8,128)(2,1)}, u32[]{:S(2)}, u32[]{:S(2)}) collective-permute-start(bf16[4,256,256]{2,1,0:T(8,128)(2,1)S(1)} %add_select_fusion), channel_id=1, source_target_pairs={{0,1},{1,0},{2,3},{3,2},{4,5},{5,4},{6,7},{7,6},{8,9},{9,8},{10,11... | collective-permute-start | bytes 1572872 | tf_op jit(solution)/shard_map/ppermute | solution.py:19
  62.0 0.1 collective-permute-start.4
  62.1 0.1 copy.9
  62.2 0.1 reshape.22
  62.3 0.1 pad_add_fusion.place
  62.4 1.3 %collective-permute-done.3 = bf16[4,256,256]{2,1,0:T(8,128)(2,1)} collective-permute-done((bf16[4,256,256]{2,1,0:T(8,128)(2,1)S(1)}, bf16[4,256,256]{2,1,0:T(8,128)(2,1)}, u32[]{:S(2)}, u32[]{:S(2)}) %collective-permute-start.3) | collective-permute-done | bytes 524320 | tf_op jit(solution)/shard_map/ppermute | solution.py:19
  63.7 1.1 %broadcast_select_fusion = (bf16[4,256,256]{2,1,0:T(8,128)(2,1)S(1)}, bf16[4,256,256]{2,1,0:T(8,128)(2,1)S(1)}) fusion(bf16[4,256,256]{2,1,0:T(8,128)(2,1)} %collective-permute-done.3, bf16[4,256,256]{2,1,0:T(8,128)(2,1)S(1)} %add_select_fusion, pred[]{:T(512)S(6)} %eq.7), kind=kLoop, calls=%fused_computation.5 | loop fusion | flops 524288 | bytes 2097153 | tf_op jit(solution)/shard_map/select_n | solution.py:173
  64.9 3.5 %finish.1 = (bf16[2,4,256,256]{3,2,1,0:T(8,128)(2,1)S(1)}, bf16[4,256,512]{2,1,0:T(8,128)(2,1)}) custom-call(s32[11]{0:T(128)S(1)} %pad_add_fusion.place, bf16[6,256,256]{2,1,0:T(8,128)(2,1)S(1)} %pad_maximum_fusion.rows0, bf16[4,256,256]{2,1,0:T(8,128)(2,1)S(1)} %get-tuple-element.12.rows1, bf16[16,112,256]{2,1,0:T(8,128)(2,1)S(1)} %all-to-all-done.2.got, ...), custom_call_target="tpu_custom_call" | custom-call | tf_op jit(solution)/shard_map/finish/pallas_call | solution.py:178
  68.4 2.0 %copy.11 = bf16[4,256,2,256]{3,2,1,0:T(2,128)(2,1)} copy(bf16[4,256,2,256]{3,1,0,2:T(8,128)(2,1)S(1)} %bitcast.34) | data formatting | bytes 2097152
  (20 shorter events, 0.3 us)
Async XLA Ops:
  0.6 0.7 copy-start.1
  17.0 13.6 %all-to-all-start.1 = ((bf16[8,48,256]{2,1,0:T(8,128)(2,1)}), bf16[8,48,256]{2,1,0:T(8,128)(2,1)S(1)}, u32[]{:S(2)}, u32[]{:S(2)}) async-start(bf16[8,48,256]{2,1,0:T(8,128)(2,1)} %broadcast_in_dim.6), calls=%async_computation.1 | async-start | bytes 393216 | tf_op jit(solution)/shard_map/all_to_all | solution.py:158
  24.5 12.1 %collective-permute-start.1 = (bf16[4,256,256]{2,1,0:T(8,128)(2,1)S(1)}, bf16[4,256,256]{2,1,0:T(8,128)(2,1)S(1)}, u32[]{:S(2)}, u32[]{:S(2)}) collective-permute-start(bf16[4,256,256]{2,1,0:T(8,128)(2,1)S(1)} %get-tuple-element.11.m0), channel_id=1, source_target_pairs={{0,6},{1,7},{8,14},{9,15},{16,22},{17,23},{24,30},{25,31},{32,38},... | collective-permute-start | bytes 1572872 | tf_op jit(solution)/shard_map/ppermute | solution.py:153
  25.2 11.5 %collective-permute-start = (bf16[4,256,256]{2,1,0:T(8,128)(2,1)S(1)}, bf16[4,256,256]{2,1,0:T(8,128)(2,1)S(1)}, u32[]{:S(2)}, u32[]{:S(2)}) collective-permute-start(bf16[4,256,256]{2,1,0:T(8,128)(2,1)S(1)} %get-tuple-element.11.m0), channel_id=1, source_target_pairs={{0,2},{1,3},{8,10},{9,11},{16,18},{17,19},{24,26},{25,27},{32,34},... | collective-permute-start | bytes 1572872 | tf_op jit(solution)/shard_map/ppermute | solution.py:152
  31.6 30.4 %all-to-all-start.2 = ((bf16[16,112,256]{2,1,0:T(8,128)(2,1)}), bf16[16,112,256]{2,1,0:T(8,128)(2,1)S(1)}, u32[]{:S(2)}, u32[]{:S(2)}) async-start(bf16[16,112,256]{2,1,0:T(8,128)(2,1)} %bitcast.16), calls=%async_computation.2 | async-start | bytes 1835008 | tf_op jit(solution)/shard_map/all_to_all | solution.py:164
  36.8 18.9 %collective-permute-start.2 = (bf16[4,256,256]{2,1,0:T(8,128)(2,1)S(1)}, bf16[4,256,256]{2,1,0:T(8,128)(2,1)}, u32[]{:S(2)}, u32[]{:S(2)}) collective-permute-start(bf16[4,256,256]{2,1,0:T(8,128)(2,1)S(1)} %add.17), channel_id=1, source_target_pairs={{2,4},{7,5},{10,12},{15,13},{18,20},{23,21},{26,28},{31,29},{34,36... | collective-permute-start | bytes 1572872 | tf_op jit(solution)/shard_map/ppermute | solution.py:155
  56.9 6.8 %collective-permute-start.3 = (bf16[4,256,256]{2,1,0:T(8,128)(2,1)S(1)}, bf16[4,256,256]{2,1,0:T(8,128)(2,1)}, u32[]{:S(2)}, u32[]{:S(2)}) collective-permute-start(bf16[4,256,256]{2,1,0:T(8,128)(2,1)S(1)} %add_select_fusion), channel_id=1, source_target_pairs={{0,1},{1,0},{2,3},{3,2},{4,5},{5,4},{6,7},{7,6},{8,9},{9,8},{10,11... | collective-permute-start | bytes 1572872 | tf_op jit(solution)/shard_map/ppermute | solution.py:19
  62.0 2.9 %collective-permute-start.4 = (bf16[16,112,256]{2,1,0:T(8,128)(2,1)S(1)}, bf16[16,112,256]{2,1,0:T(8,128)(2,1)S(1)}, u32[]{:S(2)}, u32[]{:S(2)}) collective-permute-start(bf16[16,112,256]{2,1,0:T(8,128)(2,1)S(1)} %all-to-all-done.2.got), channel_id=1, source_target_pairs={{0,1},{1,0},{2,3},{3,2},{4,5},{5,4},{6,7},{7,6},{8,9},{9,8},{10,11... | collective-permute-start | bytes 2752520 | tf_op jit(solution)/shard_map/ppermute | solution.py:19
  62.4 2.4 %copy-start = (bf16[2,256,256]{2,1,0:T(8,128)(2,1)S(1)}, bf16[2,256,256]{2,1,0:T(8,128)(2,1)}, u32[]{:S(2)}) copy-start(bf16[2,256,256]{2,1,0:T(8,128)(2,1)} %param.6) | copy-start | bytes 786436

commit v6 on v5

--- a/solution.py
+++ b/solution.py
@@ -35,10 +35,11 @@
     return jnp.where(cond, value, jnp.zeros_like(value))
 
 
-def finish(k, place, f0, f1, g0, g1, m0, m1, samples, slab, solved, lrow, lcol, ys, obuf, sem, arrival):
+def finish(ends, place, f0, f1, g0, g1, m0, m1, samples, slab, solved, lrow, lcol, ys, obuf, sem, arrival):
     row_pos = place[0]
     col_pos = place[1]
     w = (f0[TR], f0[TR + 1])
+    e0, e1 = ends
     m = (m0, m1)
 
     def tile(ref, at):
@@ -47,10 +48,10 @@
     def from_second(tile_second, first):
         return (tile_second.astype(F32) - mmt(first, l0_one)).astype(BF16)
 
-    l0_one = mm(tile(g0, 4), w[0]).astype(BF16)
-    first_col = [mm(tile(g0, 2 * k + b), w[0]).astype(BF16) for b in range(TC)]
+    l0_one = mm(tile(g0, e0), w[0]).astype(BF16)
+    first_col = [mm(tile(g0, b), w[0]).astype(BF16) for b in range(TC)]
     first_col[0] = keep(col_pos >= 1, first_col[0])
-    y0 = tmm(w[0], jnp.concatenate([tile(g0, 5), tile(g1, 5)], axis=1)).astype(BF16)
+    y0 = tmm(w[0], jnp.concatenate([tile(g0, e0 + 1), tile(g1, e1 + 1)], axis=1)).astype(BF16)
     first_row = mm(f0[0:TR].reshape(TR * T, T), w[0]).astype(BF16)
     first_row = [first_row[a * T : (a + 1) * T] for a in range(TR)]
     first_row[0] = keep(row_pos >= 1, first_row[0])
@@ -60,9 +61,9 @@
     for a in range(TR):
         lrow[a * T : (a + 1) * T, 0:T] = first_row[a]
 
-    second_col = [from_second(tile(g1, 2 * k + b), first_col[b]) for b in range(TC)]
+    second_col = [from_second(tile(g1, b), first_col[b]) for b in range(TC)]
     second_row = [from_second(f1[a], first_row[a]) for a in range(TR)]
-    r1 = jnp.concatenate([tile(g0, 6), tile(g1, 6)], axis=1).astype(F32) - mm(l0_one, y0)
+    r1 = jnp.concatenate([tile(g0, e0 + 2), tile(g1, e1 + 2)], axis=1).astype(F32) - mm(l0_one, y0)
     slab[0, 0] = second_row[0]
     for b in range(TC):
         third = mm(second_col[b], w[1]).astype(BF16)
@@ -128,11 +129,11 @@
 
     @pl.when(place[2] == 0)
     def _():
-        finish(0, place, rows0, rows1, got, got_o, *rest)
+        finish((4, 2), place, rows0, rows1, got, got_o, *rest)
 
     @pl.when(place[2] == 1)
     def _():
-        finish(1, place, rows0, rows1, got_o, got, *rest)
+        finish((2, 4), place, rows0, rows1, got_o, got, *rest)
 
 
 def body(front, fill, w, samples):
@@ -140,12 +141,13 @@
     z = lax.axis_index("z")
     y = lax.axis_index("y")
     k = lax.axis_index("core")
-    tiles = front.transpose(2, 0, 1, 3) * fill.astype(BF16).transpose(2, 0, 1, 3)
+    piece = lax.dynamic_slice(samples, (0, 0, k * T), (1, T, T))
+    piece, pattern = lax.optimization_barrier((piece, fill))
+    tiles = front.transpose(2, 0, 1, 3) * pattern.astype(BF16).transpose(2, 0, 1, 3)
     tiles = lax.optimization_barrier(tiles)
 
     panel = lax.optimization_barrier(tiles[0])
 
-    piece = lax.dynamic_slice(samples, (0, 0, k * T), (1, T, T))
     send = jnp.concatenate([panel[0].reshape(Q, RB, T), piece.reshape(Q, RB, T)], axis=1)
     got = lax.all_to_all(send, ("x", "y"), 0, 0)
 
@@ -159,6 +161,8 @@
 
     pairs = got.reshape(Y, 2, 3 * RB, T)[:, :, : 2 * RB, :].reshape(Y, 4 * RB, T)
     common = jnp.concatenate([got[1, :RB], got[0, 2 * RB :], got[1, 2 * RB :]], axis=0)
+    pairs = pairs.reshape(Y, 2, 2 * RB, T)
+    pairs = lax.select(k == 0, pairs, pairs[:, ::-1]).reshape(Y, 4 * RB, T)
     send = jnp.concatenate([pairs, jnp.broadcast_to(common[None], (Y,) + common.shape)], axis=1)
     send = jnp.broadcast_to(send[None], (X,) + send.shape).reshape(Q, 7 * RB, T)
     got = lax.all_to_all(send, ("x", "y"), 0, 0)
@@ -171,7 +175,7 @@
     other = swap(own)
     rows0 = jnp.concatenate([lax.select(k == 0, own, other), w])
     rows1 = lax.select(k == 0, other, own)
-    got_o = swap(got)
+    got_o = swap(got[:, 2 * RB :])
 
     vmem = pl.BlockSpec(memory_space=pltpu.VMEM)
     smem = pl.BlockSpec(memory_space=pltpu.SMEM)

time: 71 us -> 66.8 us (0.941)
  the two profiles are of different devices: /device:TPU:81 before, /device:TPU:1 now
where the time goes in v6:
time: 66.8 us; the launch traced here: 66.2 us
  starting transfers between devices  35.2 us (53%)
  waiting for transfers between devices  16.2 us (24%)
  local copies, waits for them, and re-layouts  5.82 us (9%)
  other arithmetic  4.74 us (7%)
  Pallas kernels  3.48 us (5%)
  between operations  0.84 us (1%)
    all_to_all x2, starting transfers between devices, body(): got = lax.all_to_all(send, ('x', 'y'), 0, 0)  11.2 us
    all_to_all x2, waiting for transfers between devices, body(): got = lax.all_to_all(send, ('x', 'y'), 0, 0)  8.6 us
    ppermute x2, starting transfers between devices, swap(): return lax.ppermute(v, 'core', [(0, 1), (1, 0)])  8.49 us
    all_to_all x1, starting transfers between devices, body(): lax.all_to_all(jnp.broadcast_to(send[None], (Z,) + send.shape), 'z', 0, 0)  8.19 us
    all_to_all x1, waiting for transfers between devices, body(): lax.all_to_all(jnp.broadcast_to(send[None], (Z,) + send.shape), 'z', 0, 0)  7.15 us
    ppermute x1, starting transfers between devices, body(): left = lax.ppermute(panel, 'y', [(0, 3)])  4.5 us
    pallas_call x1, Pallas kernels, body(): pl.pallas_call(finish_kernel, in_specs=[smem] + [vmem] * 6 + [pl.BlockSpe...  3.48 us
    unnamed x7, local copies, waits for them, and re-layouts  2.15 us
  transfers between devices with their start and end apart: 8, of which 4 were waited for; matrix products, arithmetic and copies ran while one was open for 8% of the time, Pallas kernels for 0%

profile of v6, /device:TPU:1, one launch (start us, length us, event | category | flops | bytes accessed | tf_op | source)
XLA Modules:
  0.0 66.2 jit_solution(3121426136907760352)
XLA Ops:
  0.6 0.9 %constant_dynamic-slice_fusion = bf16[1,256,256]{2,1,0:T(8,128)(2,1)S(1)} fusion(bf16[4,256,512]{2,1,0:T(8,128)(2,1)} %samples_far.1, s32[]{:T(128)S(6)} %select_n.27), kind=kLoop, calls=%fused_computation.21 | loop fusion | bytes 262148 | tf_op jit(solution)/shard_map/dynamic_slice | solution.py:144
  1.6 1.4 %bitcast_multiply_fusion = bf16[2,4,256,256]{3,2,1,0:T(8,128)(2,1)S(1)} fusion(bf16[4,256,2,256]{3,2,1,0:T(2,128)(2,1)} %param.4, bf16[2,4]{1,0:T(2,128)(2,1)S(1)} %bitcast.39), kind=kLoop, calls=%fused_computation | loop fusion | flops 524288 | bytes 2097168 | tf_op jit(solution)/shard_map/mul | solution.py:146
  3.1 0.7 %pad_maximum_fusion.1 = bf16[16,32,256]{2,1,0:T(8,128)(2,1)} fusion(bf16[16,16,256]{2,1,0:T(8,128)(2,1)S(1)} %bitcast.37, bf16[16,16,256]{2,1,0:T(8,128)(2,1)S(1)} %bitcast.38), kind=kLoop, calls=%fused_computation.7 | loop fusion | flops 524288 | bytes 524288 | tf_op jit(solution)/shard_map/concatenate | solution.py:151
  3.8 7.6 %all-to-all-start = ((bf16[16,32,256]{2,1,0:T(8,128)(2,1)}), bf16[16,32,256]{2,1,0:T(8,128)(2,1)S(1)}, u32[]{:S(2)}, u32[]{:S(2)}) async-start(bf16[16,32,256]{2,1,0:T(8,128)(2,1)} %pad_maximum_fusion.1), calls=%async_computation | async-start | bytes 524288 | tf_op jit(solution)/shard_map/all_to_all | solution.py:152
  11.4 4.5 %collective-permute-start.1 = (bf16[4,256,256]{2,1,0:T(8,128)(2,1)S(1)}, bf16[4,256,256]{2,1,0:T(8,128)(2,1)S(1)}, u32[]{:S(2)}, u32[]{:S(2)}) collective-permute-start(bf16[4,256,256]{2,1,0:T(8,128)(2,1)S(1)} %get-tuple-element.15.m0), channel_id=1, source_target_pairs={{0,6},{1,7},{8,14},{9,15},{16,22},{17,23},{24,30},{25,31},{32,38},... | collective-permute-start | bytes 1572872 | tf_op jit(solution)/shard_map/ppermute | solution.py:155
  15.9 1.3 %collective-permute-start = (bf16[4,256,256]{2,1,0:T(8,128)(2,1)S(1)}, bf16[4,256,256]{2,1,0:T(8,128)(2,1)S(1)}, u32[]{:S(2)}, u32[]{:S(2)}) collective-permute-start(bf16[4,256,256]{2,1,0:T(8,128)(2,1)S(1)} %get-tuple-element.15.m0), channel_id=1, source_target_pairs={{0,2},{1,3},{8,10},{9,11},{16,18},{17,19},{24,26},{25,27},{32,34},... | collective-permute-start | bytes 1572872 | tf_op jit(solution)/shard_map/ppermute | solution.py:154
  17.2 1.6 %all-to-all-done = bf16[16,32,256]{2,1,0:T(8,128)(2,1)S(1)} async-done(((bf16[16,32,256]{2,1,0:T(8,128)(2,1)}), bf16[16,32,256]{2,1,0:T(8,128)(2,1)S(1)}, u32[]{:S(2)}, u32[]{:S(2)}) %all-to-all-start) | async-done | bytes 262176 | tf_op jit(solution)/shard_map/all_to_all | solution.py:152
  18.9 0.7 %broadcast_in_dim.6 = bf16[8,48,256]{2,1,0:T(8,128)(2,1)} broadcast(bf16[48,256]{1,0:T(8,128)(2,1)S(1)} %pad_maximum_fusion.3), dimensions={1,2} | broadcast | bytes 221184 | tf_op jit(solution)/shard_map/broadcast_in_dim | solution.py:160
  19.6 8.2 %all-to-all-start.1 = ((bf16[8,48,256]{2,1,0:T(8,128)(2,1)}), bf16[8,48,256]{2,1,0:T(8,128)(2,1)S(1)}, u32[]{:S(2)}, u32[]{:S(2)}) async-start(bf16[8,48,256]{2,1,0:T(8,128)(2,1)} %broadcast_in_dim.6), calls=%async_computation.1 | async-start | bytes 393216 | tf_op jit(solution)/shard_map/all_to_all | solution.py:160
  27.8 0.1 add.18
  27.9 1.5 %collective-permute-start.2 = (bf16[4,256,256]{2,1,0:T(8,128)(2,1)S(1)}, bf16[4,256,256]{2,1,0:T(8,128)(2,1)}, u32[]{:S(2)}, u32[]{:S(2)}) collective-permute-start(bf16[4,256,256]{2,1,0:T(8,128)(2,1)S(1)} %add.18), channel_id=1, source_target_pairs={{2,4},{7,5},{10,12},{15,13},{18,20},{23,21},{26,28},{31,29},{34,36... | collective-permute-start | bytes 1572872 | tf_op jit(solution)/shard_map/ppermute | solution.py:157
  29.4 7.1 %all-to-all-done.1 = bf16[8,48,256]{2,1,0:T(8,128)(2,1)S(1)} async-done(((bf16[8,48,256]{2,1,0:T(8,128)(2,1)}), bf16[8,48,256]{2,1,0:T(8,128)(2,1)S(1)}, u32[]{:S(2)}, u32[]{:S(2)}) %all-to-all-start.1) | async-done | bytes 196640 | tf_op jit(solution)/shard_map/all_to_all | solution.py:160
  36.6 1.0 %broadcast_in_dim.8 = bf16[4,4,112,256]{3,2,1,0:T(8,128)(2,1)} broadcast(bf16[4,112,256]{2,1,0:T(8,128)(2,1)S(1)} %pad_maximum_fusion.2), dimensions={1,2,3} | broadcast | bytes 1146880 | tf_op jit(solution)/shard_map/broadcast_in_dim | solution.py:167
  37.6 3.6 %all-to-all-start.2 = ((bf16[16,112,256]{2,1,0:T(8,128)(2,1)}), bf16[16,112,256]{2,1,0:T(8,128)(2,1)S(1)}, u32[]{:S(2)}, u32[]{:S(2)}) async-start(bf16[16,112,256]{2,1,0:T(8,128)(2,1)} %bitcast.16), calls=%async_computation.2 | async-start | bytes 1835008 | tf_op jit(solution)/shard_map/all_to_all | solution.py:168
  41.3 1.1 %add_select_fusion = bf16[4,256,256]{2,1,0:T(8,128)(2,1)S(1)} fusion(bf16[4,256,256]{2,1,0:T(8,128)(2,1)S(1)} %get-tuple-element.15.m0, bf16[4,256,256]{2,1,0:T(8,128)(2,1)S(1)} %add.18, bf16[4,256,256]{2,1,0:T(8,128)(2,1)} %collective-permute-done.2, pred[]{:T(512)S(6)} %eq.9), kind=kLoop, calls=%fused_computation.4 | loop fusion | flops 524288 | bytes 2097153 | tf_op jit(solution)/shard_map/select_n | solution.py:174
  42.4 3.4 %collective-permute-start.3 = (bf16[4,256,256]{2,1,0:T(8,128)(2,1)S(1)}, bf16[4,256,256]{2,1,0:T(8,128)(2,1)}, u32[]{:S(2)}, u32[]{:S(2)}) collective-permute-start(bf16[4,256,256]{2,1,0:T(8,128)(2,1)S(1)} %add_select_fusion), channel_id=1, source_target_pairs={{0,1},{1,0},{2,3},{3,2},{4,5},{5,4},{6,7},{7,6},{8,9},{9,8},{10,11... | collective-permute-start | bytes 1572872 | tf_op jit(solution)/shard_map/ppermute | solution.py:19
  45.8 7.0 %all-to-all-done.2.got = bf16[16,112,256]{2,1,0:T(8,128)(2,1)S(1)} async-done(((bf16[16,112,256]{2,1,0:T(8,128)(2,1)}), bf16[16,112,256]{2,1,0:T(8,128)(2,1)S(1)}, u32[]{:S(2)}, u32[]{:S(2)}) %all-to-all-start.2) | async-done | bytes 917536 | tf_op jit(solution)/shard_map/all_to_all | solution.py:168
  52.8 0.9 %slice.53 = bf16[16,80,256]{2,1,0:T(8,128)(2,1)} slice(bf16[16,112,256]{2,1,0:T(8,128)(2,1)S(1)} %all-to-all-done.2.got), slice={[0:16], [32:112], [0:256]} | slice | bytes 1310720 | tf_op jit(solution)/shard_map/slice | solution.py:178
  53.7 5.1 %collective-permute-start.4 = (bf16[16,80,256]{2,1,0:T(8,128)(2,1)}, bf16[16,80,256]{2,1,0:T(8,128)(2,1)S(1)}, u32[]{:S(2)}, u32[]{:S(2)}) collective-permute-start(bf16[16,80,256]{2,1,0:T(8,128)(2,1)} %slice.53), channel_id=1, source_target_pairs={{0,1},{1,0},{2,3},{3,2},{4,5},{5,4},{6,7},{7,6},{8,9},{9,8},{10,11... | collective-permute-start | bytes 1966088 | tf_op jit(solution)/shard_map/ppermute | solution.py:19
  58.7 0.1 copy.9
  59.0 1.2 %broadcast_select_fusion = (bf16[4,256,256]{2,1,0:T(8,128)(2,1)S(1)}, bf16[4,256,256]{2,1,0:T(8,128)(2,1)S(1)}) fusion(bf16[4,256,256]{2,1,0:T(8,128)(2,1)} %collective-permute-done.3, bf16[4,256,256]{2,1,0:T(8,128)(2,1)S(1)} %add_select_fusion, pred[]{:T(512)S(6)} %eq.8), kind=kLoop, calls=%fused_computation.5 | loop fusion | flops 524288 | bytes 2097153 | tf_op jit(solution)/shard_map/select_n | solution.py:177
  60.3 0.4 collective-permute-done.4.got_o
  60.7 3.5 %finish.1 = (bf16[2,4,256,256]{3,2,1,0:T(8,128)(2,1)S(1)}, bf16[4,256,512]{2,1,0:T(8,128)(2,1)}) custom-call(s32[11]{0:T(128)S(1)} %pad_add_fusion.place, bf16[6,256,256]{2,1,0:T(8,128)(2,1)S(1)} %pad_maximum_fusion.rows0, bf16[4,256,256]{2,1,0:T(8,128)(2,1)S(1)} %get-tuple-element.16.rows1, bf16[16,112,256]{2,1,0:T(8,128)(2,1)S(1)} %all-to-all-done.2.got, ...), custom_call_target="tpu_custom_call" | custom-call | tf_op jit(solution)/shard_map/finish/pallas_call | solution.py:182
  64.2 2.0 %copy.11 = bf16[4,256,2,256]{3,2,1,0:T(2,128)(2,1)} copy(bf16[4,256,2,256]{3,1,0,2:T(8,128)(2,1)S(1)} %bitcast.34) | data formatting | bytes 2097152
  (23 shorter events, 0.4 us)
Async XLA Ops:
  0.6 0.9 %copy-start.1 = (s32[4,1,2,1]{0,3,2,1:T(1,128)S(1)}, s32[4,1,2,1]{0,3,2,1:T(1,128)}, u32[]{:S(2)}) copy-start(s32[4,1,2,1]{0,3,2,1:T(1,128)} %param.5) | copy-start | bytes 100
  3.8 15.0 %all-to-all-start = ((bf16[16,32,256]{2,1,0:T(8,128)(2,1)}), bf16[16,32,256]{2,1,0:T(8,128)(2,1)S(1)}, u32[]{:S(2)}, u32[]{:S(2)}) async-start(bf16[16,32,256]{2,1,0:T(8,128)(2,1)} %pad_maximum_fusion.1), calls=%async_computation | async-start | bytes 524288 | tf_op jit(solution)/shard_map/all_to_all | solution.py:152
  11.4 16.3 %collective-permute-start.1 = (bf16[4,256,256]{2,1,0:T(8,128)(2,1)S(1)}, bf16[4,256,256]{2,1,0:T(8,128)(2,1)S(1)}, u32[]{:S(2)}, u32[]{:S(2)}) collective-permute-start(bf16[4,256,256]{2,1,0:T(8,128)(2,1)S(1)} %get-tuple-element.15.m0), channel_id=1, source_target_pairs={{0,6},{1,7},{8,14},{9,15},{16,22},{17,23},{24,30},{25,31},{32,38},... | collective-permute-start | bytes 1572872 | tf_op jit(solution)/shard_map/ppermute | solution.py:155
  15.9 11.8 %collective-permute-start = (bf16[4,256,256]{2,1,0:T(8,128)(2,1)S(1)}, bf16[4,256,256]{2,1,0:T(8,128)(2,1)S(1)}, u32[]{:S(2)}, u32[]{:S(2)}) collective-permute-start(bf16[4,256,256]{2,1,0:T(8,128)(2,1)S(1)} %get-tuple-element.15.m0), channel_id=1, source_target_pairs={{0,2},{1,3},{8,10},{9,11},{16,18},{17,19},{24,26},{25,27},{32,34},... | collective-permute-start | bytes 1572872 | tf_op jit(solution)/shard_map/ppermute | solution.py:154
  19.6 16.9 %all-to-all-start.1 = ((bf16[8,48,256]{2,1,0:T(8,128)(2,1)}), bf16[8,48,256]{2,1,0:T(8,128)(2,1)S(1)}, u32[]{:S(2)}, u32[]{:S(2)}) async-start(bf16[8,48,256]{2,1,0:T(8,128)(2,1)} %broadcast_in_dim.6), calls=%async_computation.1 | async-start | bytes 393216 | tf_op jit(solution)/shard_map/all_to_all | solution.py:160
  27.9 13.4 %collective-permute-start.2 = (bf16[4,256,256]{2,1,0:T(8,128)(2,1)S(1)}, bf16[4,256,256]{2,1,0:T(8,128)(2,1)}, u32[]{:S(2)}, u32[]{:S(2)}) collective-permute-start(bf16[4,256,256]{2,1,0:T(8,128)(2,1)S(1)} %add.18), channel_id=1, source_target_pairs={{2,4},{7,5},{10,12},{15,13},{18,20},{23,21},{26,28},{31,29},{34,36... | collective-permute-start | bytes 1572872 | tf_op jit(solution)/shard_map/ppermute | solution.py:157
  37.6 15.2 %all-to-all-start.2 = ((bf16[16,112,256]{2,1,0:T(8,128)(2,1)}), bf16[16,112,256]{2,1,0:T(8,128)(2,1)S(1)}, u32[]{:S(2)}, u32[]{:S(2)}) async-start(bf16[16,112,256]{2,1,0:T(8,128)(2,1)} %bitcast.16), calls=%async_computation.2 | async-start | bytes 1835008 | tf_op jit(solution)/shard_map/all_to_all | solution.py:168
  42.4 16.6 %collective-permute-start.3 = (bf16[4,256,256]{2,1,0:T(8,128)(2,1)S(1)}, bf16[4,256,256]{2,1,0:T(8,128)(2,1)}, u32[]{:S(2)}, u32[]{:S(2)}) collective-permute-start(bf16[4,256,256]{2,1,0:T(8,128)(2,1)S(1)} %add_select_fusion), channel_id=1, source_target_pairs={{0,1},{1,0},{2,3},{3,2},{4,5},{5,4},{6,7},{7,6},{8,9},{9,8},{10,11... | collective-permute-start | bytes 1572872 | tf_op jit(solution)/shard_map/ppermute | solution.py:19
  53.7 7.0 %collective-permute-start.4 = (bf16[16,80,256]{2,1,0:T(8,128)(2,1)}, bf16[16,80,256]{2,1,0:T(8,128)(2,1)S(1)}, u32[]{:S(2)}, u32[]{:S(2)}) collective-permute-start(bf16[16,80,256]{2,1,0:T(8,128)(2,1)} %slice.53), channel_id=1, source_target_pairs={{0,1},{1,0},{2,3},{3,2},{4,5},{5,4},{6,7},{7,6},{8,9},{9,8},{10,11... | collective-permute-start | bytes 1966088 | tf_op jit(solution)/shard_map/ppermute | solution.py:19
  59.0 1.2 %copy-start = (bf16[2,256,256]{2,1,0:T(8,128)(2,1)S(1)}, bf16[2,256,256]{2,1,0:T(8,128)(2,1)}, u32[]{:S(2)}) copy-start(bf16[2,256,256]{2,1,0:T(8,128)(2,1)} %param.6) | copy-start | bytes 786436

commit v7 on v6

--- a/solution.py
+++ b/solution.py
@@ -151,10 +151,9 @@
     send = jnp.concatenate([panel[0].reshape(Q, RB, T), piece.reshape(Q, RB, T)], axis=1)
     got = lax.all_to_all(send, ("x", "y"), 0, 0)
 
-    right = lax.ppermute(panel, "y", [(0, 1)])
-    left = lax.ppermute(panel, "y", [(0, 3)])
-    near = right + left
-    far = lax.ppermute(near, ("y", "core"), [(2, 4), (7, 5)])
+    near = lax.ppermute(panel, ("y", "core"), [(0, 2), (1, 7)])
+    relay = lax.select(y == 0, panel, near)
+    far = lax.ppermute(relay, ("y", "core"), [(2, 4), (7, 5), (0, 6), (1, 3)])
 
     send = jnp.concatenate([got[0, :RB], got[Y, :RB], got[0, RB:]], axis=0)
     got = lax.all_to_all(jnp.broadcast_to(send[None], (Z,) + send.shape), "z", 0, 0)

time: 66.8 us -> 66.8 us (level)
    all_to_all x1, waiting for transfers between devices: 7.15 us -> 5.61 us  [body(): lax.all_to_all(jnp.broadcast_to(send[None], (Z,) + send.shape), 'z', 0, 0)]
    all_to_all x2, waiting for transfers between devices: 8.6 us -> 9.93 us  [body(): got = lax.all_to_all(send, ('x', 'y'), 0, 0)]
    ppermute x3 -> x2, starting transfers between devices: 7.28 us -> 7.58 us  [the longest x1 4.5 us: body(): near = lax.ppermute(panel, ('y', 'core'), [(0, 2), (1, 7)])]
  transfers between devices with their start and end apart: 8 -> 7, of which waited for: 4 -> 4; matrix products, arithmetic and copies ran while one was open for 8% -> 8% of each run, Pallas kernels for 0% -> 0%
where the time goes in v7:
time: 66.8 us; the launch traced here: 66.2 us
  starting transfers between devices  35.5 us (53%)
  waiting for transfers between devices  16 us (24%)
  local copies, waits for them, and re-layouts  5.82 us (9%)
  other arithmetic  4.67 us (7%)
  Pallas kernels  3.48 us (5%)
  between operations  0.81 us (1%)
    all_to_all x2, starting transfers between devices, body(): got = lax.all_to_all(send, ('x', 'y'), 0, 0)  11.2 us
    all_to_all x2, waiting for transfers between devices, body(): got = lax.all_to_all(send, ('x', 'y'), 0, 0)  9.93 us
    ppermute x2, starting transfers between devices, swap(): return lax.ppermute(v, 'core', [(0, 1), (1, 0)])  8.49 us
    all_to_all x1, starting transfers between devices, body(): lax.all_to_all(jnp.broadcast_to(send[None], (Z,) + send.shape), 'z', 0, 0)  8.19 us
    all_to_all x1, waiting for transfers between devices, body(): lax.all_to_all(jnp.broadcast_to(send[None], (Z,) + send.shape), 'z', 0, 0)  5.61 us
    ppermute x1, starting transfers between devices, body(): near = lax.ppermute(panel, ('y', 'core'), [(0, 2), (1, 7)])  4.5 us
    pallas_call x1, Pallas kernels, body(): pl.pallas_call(finish_kernel, in_specs=[smem] + [vmem] * 6 + [pl.BlockSpe...  3.48 us
    ppermute x1, starting transfers between devices, body(): far = lax.ppermute(relay, ('y', 'core'), [(2, 4), (7, 5), (0, 6), (1, 3)])  3.08 us
  transfers between devices with their start and end apart: 7, of which 4 were waited for; matrix products, arithmetic and copies ran while one was open for 8% of the time, Pallas kernels for 0%

profile of v7, /device:TPU:1, one launch (start us, length us, event | category | flops | bytes accessed | tf_op | source)
XLA Modules:
  0.0 66.2 jit_solution(3739678497548712635)
XLA Ops:
  0.6 0.9 %constant_dynamic-slice_fusion = bf16[1,256,256]{2,1,0:T(8,128)(2,1)S(1)} fusion(bf16[4,256,512]{2,1,0:T(8,128)(2,1)} %samples_far.1, s32[]{:T(128)S(6)} %select_n.31), kind=kLoop, calls=%fused_computation.22 | loop fusion | bytes 262148 | tf_op jit(solution)/shard_map/dynamic_slice | solution.py:144
  1.6 1.4 %bitcast_multiply_fusion = bf16[2,4,256,256]{3,2,1,0:T(8,128)(2,1)S(1)} fusion(bf16[4,256,2,256]{3,2,1,0:T(2,128)(2,1)} %param.4, bf16[2,4]{1,0:T(2,128)(2,1)S(1)} %bitcast.39), kind=kLoop, calls=%fused_computation | loop fusion | flops 524288 | bytes 2097168 | tf_op jit(solution)/shard_map/mul | solution.py:146
  3.1 0.7 %pad_maximum_fusion.1 = bf16[16,32,256]{2,1,0:T(8,128)(2,1)} fusion(bf16[16,16,256]{2,1,0:T(8,128)(2,1)S(1)} %bitcast.37, bf16[16,16,256]{2,1,0:T(8,128)(2,1)S(1)} %bitcast.38), kind=kLoop, calls=%fused_computation.8 | loop fusion | flops 524288 | bytes 524288 | tf_op jit(solution)/shard_map/concatenate | solution.py:151
  3.8 7.6 %all-to-all-start = ((bf16[16,32,256]{2,1,0:T(8,128)(2,1)}), bf16[16,32,256]{2,1,0:T(8,128)(2,1)S(1)}, u32[]{:S(2)}, u32[]{:S(2)}) async-start(bf16[16,32,256]{2,1,0:T(8,128)(2,1)} %pad_maximum_fusion.1), calls=%async_computation | async-start | bytes 524288 | tf_op jit(solution)/shard_map/all_to_all | solution.py:152
  11.4 4.5 %collective-permute-start = (bf16[4,256,256]{2,1,0:T(8,128)(2,1)S(1)}, bf16[4,256,256]{2,1,0:T(8,128)(2,1)S(1)}, u32[]{:S(2)}, u32[]{:S(2)}) collective-permute-start(bf16[4,256,256]{2,1,0:T(8,128)(2,1)S(1)} %get-tuple-element.15.m0), channel_id=1, source_target_pairs={{0,2},{1,7},{8,10},{9,15},{16,18},{17,23},{24,26},{25,31},{32,34},... | collective-permute-start | bytes 1572872 | tf_op jit(solution)/shard_map/ppermute | solution.py:154
  15.9 2.9 %all-to-all-done = bf16[16,32,256]{2,1,0:T(8,128)(2,1)S(1)} async-done(((bf16[16,32,256]{2,1,0:T(8,128)(2,1)}), bf16[16,32,256]{2,1,0:T(8,128)(2,1)S(1)}, u32[]{:S(2)}, u32[]{:S(2)}) %all-to-all-start) | async-done | bytes 262176 | tf_op jit(solution)/shard_map/all_to_all | solution.py:152
  18.9 0.7 %broadcast_in_dim.6 = bf16[8,48,256]{2,1,0:T(8,128)(2,1)} broadcast(bf16[48,256]{1,0:T(8,128)(2,1)S(1)} %pad_maximum_fusion.3), dimensions={1,2} | broadcast | bytes 221184 | tf_op jit(solution)/shard_map/broadcast_in_dim | solution.py:159
  19.6 8.2 %all-to-all-start.1 = ((bf16[8,48,256]{2,1,0:T(8,128)(2,1)}), bf16[8,48,256]{2,1,0:T(8,128)(2,1)S(1)}, u32[]{:S(2)}, u32[]{:S(2)}) async-start(bf16[8,48,256]{2,1,0:T(8,128)(2,1)} %broadcast_in_dim.6), calls=%async_computation.1 | async-start | bytes 393216 | tf_op jit(solution)/shard_map/all_to_all | solution.py:159
  27.8 3.1 %collective-permute-start.1 = (bf16[4,256,256]{2,1,0:T(8,128)(2,1)S(1)}, bf16[4,256,256]{2,1,0:T(8,128)(2,1)}, u32[]{:S(2)}, u32[]{:S(2)}) collective-permute-start(bf16[4,256,256]{2,1,0:T(8,128)(2,1)S(1)} %broadcast_select_fusion), channel_id=1, source_target_pairs={{2,4},{7,5},{0,6},{1,3},{10,12},{15,13},{8,14},{9,11},{18,20},{23,... | collective-permute-start | bytes 1572872 | tf_op jit(solution)/shard_map/ppermute | solution.py:156
  30.9 5.6 %all-to-all-done.1 = bf16[8,48,256]{2,1,0:T(8,128)(2,1)S(1)} async-done(((bf16[8,48,256]{2,1,0:T(8,128)(2,1)}), bf16[8,48,256]{2,1,0:T(8,128)(2,1)S(1)}, u32[]{:S(2)}, u32[]{:S(2)}) %all-to-all-start.1) | async-done | bytes 196640 | tf_op jit(solution)/shard_map/all_to_all | solution.py:159
  36.6 1.0 %broadcast_in_dim.8 = bf16[4,4,112,256]{3,2,1,0:T(8,128)(2,1)} broadcast(bf16[4,112,256]{2,1,0:T(8,128)(2,1)S(1)} %pad_maximum_fusion.2), dimensions={1,2,3} | broadcast | bytes 1146880 | tf_op jit(solution)/shard_map/broadcast_in_dim | solution.py:166
  37.6 3.6 %all-to-all-start.2 = ((bf16[16,112,256]{2,1,0:T(8,128)(2,1)}), bf16[16,112,256]{2,1,0:T(8,128)(2,1)S(1)}, u32[]{:S(2)}, u32[]{:S(2)}) async-start(bf16[16,112,256]{2,1,0:T(8,128)(2,1)} %bitcast.16), calls=%async_computation.2 | async-start | bytes 1835008 | tf_op jit(solution)/shard_map/all_to_all | solution.py:167
  41.3 1.1 %add_select_fusion = bf16[4,256,256]{2,1,0:T(8,128)(2,1)S(1)} fusion(bf16[4,256,256]{2,1,0:T(8,128)(2,1)S(1)} %get-tuple-element.15.m0, bf16[4,256,256]{2,1,0:T(8,128)(2,1)S(1)} %collective-permute-done, bf16[4,256,256]{2,1,0:T(8,128)(2,1)} %collective-permute-done.1, pred[]{:T(512)S(6)} %eq.10), kind=kLoop, calls=%fused_computation.4 | loop fusion | flops 524288 | bytes 2097153 | tf_op jit(solution)/shard_map/select_n | solution.py:173
  42.4 3.4 %collective-permute-start.2 = (bf16[4,256,256]{2,1,0:T(8,128)(2,1)S(1)}, bf16[4,256,256]{2,1,0:T(8,128)(2,1)}, u32[]{:S(2)}, u32[]{:S(2)}) collective-permute-start(bf16[4,256,256]{2,1,0:T(8,128)(2,1)S(1)} %add_select_fusion), channel_id=1, source_target_pairs={{0,1},{1,0},{2,3},{3,2},{4,5},{5,4},{6,7},{7,6},{8,9},{9,8},{10,11... | collective-permute-start | bytes 1572872 | tf_op jit(solution)/shard_map/ppermute | solution.py:19
  45.8 7.0 %all-to-all-done.2.got = bf16[16,112,256]{2,1,0:T(8,128)(2,1)S(1)} async-done(((bf16[16,112,256]{2,1,0:T(8,128)(2,1)}), bf16[16,112,256]{2,1,0:T(8,128)(2,1)S(1)}, u32[]{:S(2)}, u32[]{:S(2)}) %all-to-all-start.2) | async-done | bytes 917536 | tf_op jit(solution)/shard_map/all_to_all | solution.py:167
  52.8 0.9 %slice.53 = bf16[16,80,256]{2,1,0:T(8,128)(2,1)} slice(bf16[16,112,256]{2,1,0:T(8,128)(2,1)S(1)} %all-to-all-done.2.got), slice={[0:16], [32:112], [0:256]} | slice | bytes 1310720 | tf_op jit(solution)/shard_map/slice | solution.py:177
  53.7 5.1 %collective-permute-start.3 = (bf16[16,80,256]{2,1,0:T(8,128)(2,1)}, bf16[16,80,256]{2,1,0:T(8,128)(2,1)S(1)}, u32[]{:S(2)}, u32[]{:S(2)}) collective-permute-start(bf16[16,80,256]{2,1,0:T(8,128)(2,1)} %slice.53), channel_id=1, source_target_pairs={{0,1},{1,0},{2,3},{3,2},{4,5},{5,4},{6,7},{7,6},{8,9},{9,8},{10,11... | collective-permute-start | bytes 1966088 | tf_op jit(solution)/shard_map/ppermute | solution.py:19
  58.7 0.1 copy.9
  58.8 0.1 reshape.22
  58.9 0.1 pad_add_fusion.place
  59.0 1.2 %broadcast_select_fusion.1 = (bf16[4,256,256]{2,1,0:T(8,128)(2,1)S(1)}, bf16[4,256,256]{2,1,0:T(8,128)(2,1)S(1)}) fusion(bf16[4,256,256]{2,1,0:T(8,128)(2,1)} %collective-permute-done.2, bf16[4,256,256]{2,1,0:T(8,128)(2,1)S(1)} %add_select_fusion, pred[]{:T(512)S(6)} %eq.4), kind=kLoop, calls=%fused_computation.6 | loop fusion | flops 524288 | bytes 2097153 | tf_op jit(solution)/shard_map/select_n | solution.py:176
  60.3 0.4 collective-permute-done.3.got_o
  60.7 3.5 %finish.1 = (bf16[2,4,256,256]{3,2,1,0:T(8,128)(2,1)S(1)}, bf16[4,256,512]{2,1,0:T(8,128)(2,1)}) custom-call(s32[11]{0:T(128)S(1)} %pad_add_fusion.place, bf16[6,256,256]{2,1,0:T(8,128)(2,1)S(1)} %pad_maximum_fusion.rows0, bf16[4,256,256]{2,1,0:T(8,128)(2,1)S(1)} %get-tuple-element.16.rows1, bf16[16,112,256]{2,1,0:T(8,128)(2,1)S(1)} %all-to-all-done.2.got, ...), custom_call_target="tpu_custom_call" | custom-call | tf_op jit(solution)/shard_map/finish/pallas_call | solution.py:181
  64.2 2.0 %copy.11 = bf16[4,256,2,256]{3,2,1,0:T(2,128)(2,1)} copy(bf16[4,256,2,256]{3,1,0,2:T(8,128)(2,1)S(1)} %bitcast.34) | data formatting | bytes 2097152
  (21 shorter events, 0.3 us)
Async XLA Ops:
  0.6 0.9 %copy-start.1 = (s32[4,1,2,1]{0,3,2,1:T(1,128)S(1)}, s32[4,1,2,1]{0,3,2,1:T(1,128)}, u32[]{:S(2)}) copy-start(s32[4,1,2,1]{0,3,2,1:T(1,128)} %param.5) | copy-start | bytes 100
  3.8 15.0 %all-to-all-start = ((bf16[16,32,256]{2,1,0:T(8,128)(2,1)}), bf16[16,32,256]{2,1,0:T(8,128)(2,1)S(1)}, u32[]{:S(2)}, u32[]{:S(2)}) async-start(bf16[16,32,256]{2,1,0:T(8,128)(2,1)} %pad_maximum_fusion.1), calls=%async_computation | async-start | bytes 524288 | tf_op jit(solution)/shard_map/all_to_all | solution.py:152
  11.4 16.3 %collective-permute-start = (bf16[4,256,256]{2,1,0:T(8,128)(2,1)S(1)}, bf16[4,256,256]{2,1,0:T(8,128)(2,1)S(1)}, u32[]{:S(2)}, u32[]{:S(2)}) collective-permute-start(bf16[4,256,256]{2,1,0:T(8,128)(2,1)S(1)} %get-tuple-element.15.m0), channel_id=1, source_target_pairs={{0,2},{1,7},{8,10},{9,15},{16,18},{17,23},{24,26},{25,31},{32,34},... | collective-permute-start | bytes 1572872 | tf_op jit(solution)/shard_map/ppermute | solution.py:154
  19.6 16.9 %all-to-all-start.1 = ((bf16[8,48,256]{2,1,0:T(8,128)(2,1)}), bf16[8,48,256]{2,1,0:T(8,128)(2,1)S(1)}, u32[]{:S(2)}, u32[]{:S(2)}) async-start(bf16[8,48,256]{2,1,0:T(8,128)(2,1)} %broadcast_in_dim.6), calls=%async_computation.1 | async-start | bytes 393216 | tf_op jit(solution)/shard_map/all_to_all | solution.py:159
  27.8 13.4 %collective-permute-start.1 = (bf16[4,256,256]{2,1,0:T(8,128)(2,1)S(1)}, bf16[4,256,256]{2,1,0:T(8,128)(2,1)}, u32[]{:S(2)}, u32[]{:S(2)}) collective-permute-start(bf16[4,256,256]{2,1,0:T(8,128)(2,1)S(1)} %broadcast_select_fusion), channel_id=1, source_target_pairs={{2,4},{7,5},{0,6},{1,3},{10,12},{15,13},{8,14},{9,11},{18,20},{23,... | collective-permute-start | bytes 1572872 | tf_op jit(solution)/shard_map/ppermute | solution.py:156
  37.6 15.2 %all-to-all-start.2 = ((bf16[16,112,256]{2,1,0:T(8,128)(2,1)}), bf16[16,112,256]{2,1,0:T(8,128)(2,1)S(1)}, u32[]{:S(2)}, u32[]{:S(2)}) async-start(bf16[16,112,256]{2,1,0:T(8,128)(2,1)} %bitcast.16), calls=%async_computation.2 | async-start | bytes 1835008 | tf_op jit(solution)/shard_map/all_to_all | solution.py:167
  42.4 16.6 %collective-permute-start.2 = (bf16[4,256,256]{2,1,0:T(8,128)(2,1)S(1)}, bf16[4,256,256]{2,1,0:T(8,128)(2,1)}, u32[]{:S(2)}, u32[]{:S(2)}) collective-permute-start(bf16[4,256,256]{2,1,0:T(8,128)(2,1)S(1)} %add_select_fusion), channel_id=1, source_target_pairs={{0,1},{1,0},{2,3},{3,2},{4,5},{5,4},{6,7},{7,6},{8,9},{9,8},{10,11... | collective-permute-start | bytes 1572872 | tf_op jit(solution)/shard_map/ppermute | solution.py:19
  53.7 7.0 %collective-permute-start.3 = (bf16[16,80,256]{2,1,0:T(8,128)(2,1)}, bf16[16,80,256]{2,1,0:T(8,128)(2,1)S(1)}, u32[]{:S(2)}, u32[]{:S(2)}) collective-permute-start(bf16[16,80,256]{2,1,0:T(8,128)(2,1)} %slice.53), channel_id=1, source_target_pairs={{0,1},{1,0},{2,3},{3,2},{4,5},{5,4},{6,7},{7,6},{8,9},{9,8},{10,11... | collective-permute-start | bytes 1966088 | tf_op jit(solution)/shard_map/ppermute | solution.py:19
  59.0 1.2 %copy-start = (bf16[2,256,256]{2,1,0:T(8,128)(2,1)S(1)}, bf16[2,256,256]{2,1,0:T(8,128)(2,1)}, u32[]{:S(2)}) copy-start(bf16[2,256,256]{2,1,0:T(8,128)(2,1)} %param.6) | copy-start | bytes 786436

commit v8 on v7

--- a/solution.py
+++ b/solution.py
@@ -76,15 +76,11 @@
     arrival.wait()
     for a in range(TR):
         rows = lrow[a * T : (a + 1) * T, :]
-        obuf[a] = (samples[a].astype(F32) - mm(rows, ys[...])).astype(BF16)
-
-    @pl.when(row_pos == 0)
-    def _():
-        obuf[0] = ys[0:T, :]
-
-    @pl.when(row_pos == 1)
-    def _():
-        obuf[0] = ys[T : 2 * T, :]
+        solved_tile = (samples[a].astype(F32) - mm(rows, ys[...])).astype(BF16)
+        if a == 0:
+            solved_tile = lax.select(row_pos == 0, ys[0:T, :], solved_tile)
+            solved_tile = lax.select(row_pos == 1, ys[T : 2 * T, :], solved_tile)
+        obuf[a] = solved_tile
 
     out = pltpu.make_async_copy(obuf, solved, sem)
     out.start()

time: 66.8 us -> 66.8 us (level)
  no operation moved by 1% of the time
where the time goes in v8:
time: 66.8 us; the launch traced here: 66.2 us
  starting transfers between devices  35.5 us (53%)
  waiting for transfers between devices  16 us (24%)
  local copies, waits for them, and re-layouts  5.82 us (9%)
  other arithmetic  4.67 us (7%)
  Pallas kernels  3.47 us (5%)
  between operations  0.81 us (1%)
    all_to_all x2, starting transfers between devices, body(): got = lax.all_to_all(send, ('x', 'y'), 0, 0)  11.2 us
    all_to_all x2, waiting for transfers between devices, body(): got = lax.all_to_all(send, ('x', 'y'), 0, 0)  9.93 us
    ppermute x2, starting transfers between devices, swap(): return lax.ppermute(v, 'core', [(0, 1), (1, 0)])  8.49 us
    all_to_all x1, starting transfers between devices, body(): lax.all_to_all(jnp.broadcast_to(send[None], (Z,) + send.shape), 'z', 0, 0)  8.19 us
    all_to_all x1, waiting for transfers between devices, body(): lax.all_to_all(jnp.broadcast_to(send[None], (Z,) + send.shape), 'z', 0, 0)  5.61 us
    ppermute x1, starting transfers between devices, body(): near = lax.ppermute(panel, ('y', 'core'), [(0, 2), (1, 7)])  4.5 us
    pallas_call x1, Pallas kernels, body(): pl.pallas_call(finish_kernel, in_specs=[smem] + [vmem] * 6 + [pl.BlockSpe...  3.47 us
    ppermute x1, starting transfers between devices, body(): far = lax.ppermute(relay, ('y', 'core'), [(2, 4), (7, 5), (0, 6), (1, 3)])  3.08 us
  transfers between devices with their start and end apart: 7, of which 4 were waited for; matrix products, arithmetic and copies ran while one was open for 8% of the time, Pallas kernels for 0%

profile of v8, /device:TPU:1, one launch (start us, length us, event | category | flops | bytes accessed | tf_op | source)
XLA Modules:
  0.0 66.2 jit_solution(3864706567526044484)
XLA Ops:
  0.6 0.9 %constant_dynamic-slice_fusion = bf16[1,256,256]{2,1,0:T(8,128)(2,1)S(1)} fusion(bf16[4,256,512]{2,1,0:T(8,128)(2,1)} %samples_far.1, s32[]{:T(128)S(6)} %select_n.31), kind=kLoop, calls=%fused_computation.22 | loop fusion | bytes 262148 | tf_op jit(solution)/shard_map/dynamic_slice | solution.py:140
  1.6 1.4 %bitcast_multiply_fusion = bf16[2,4,256,256]{3,2,1,0:T(8,128)(2,1)S(1)} fusion(bf16[4,256,2,256]{3,2,1,0:T(2,128)(2,1)} %param.4, bf16[2,4]{1,0:T(2,128)(2,1)S(1)} %bitcast.39), kind=kLoop, calls=%fused_computation | loop fusion | flops 524288 | bytes 2097168 | tf_op jit(solution)/shard_map/mul | solution.py:142
  3.1 0.7 %pad_maximum_fusion.1 = bf16[16,32,256]{2,1,0:T(8,128)(2,1)} fusion(bf16[16,16,256]{2,1,0:T(8,128)(2,1)S(1)} %bitcast.37, bf16[16,16,256]{2,1,0:T(8,128)(2,1)S(1)} %bitcast.38), kind=kLoop, calls=%fused_computation.8 | loop fusion | flops 524288 | bytes 524288 | tf_op jit(solution)/shard_map/concatenate | solution.py:147
  3.8 7.6 %all-to-all-start = ((bf16[16,32,256]{2,1,0:T(8,128)(2,1)}), bf16[16,32,256]{2,1,0:T(8,128)(2,1)S(1)}, u32[]{:S(2)}, u32[]{:S(2)}) async-start(bf16[16,32,256]{2,1,0:T(8,128)(2,1)} %pad_maximum_fusion.1), calls=%async_computation | async-start | bytes 524288 | tf_op jit(solution)/shard_map/all_to_all | solution.py:148
  11.4 4.5 %collective-permute-start = (bf16[4,256,256]{2,1,0:T(8,128)(2,1)S(1)}, bf16[4,256,256]{2,1,0:T(8,128)(2,1)S(1)}, u32[]{:S(2)}, u32[]{:S(2)}) collective-permute-start(bf16[4,256,256]{2,1,0:T(8,128)(2,1)S(1)} %get-tuple-element.15.m0), channel_id=1, source_target_pairs={{0,2},{1,7},{8,10},{9,15},{16,18},{17,23},{24,26},{25,31},{32,34},... | collective-permute-start | bytes 1572872 | tf_op jit(solution)/shard_map/ppermute | solution.py:150
  15.9 2.9 %all-to-all-done = bf16[16,32,256]{2,1,0:T(8,128)(2,1)S(1)} async-done(((bf16[16,32,256]{2,1,0:T(8,128)(2,1)}), bf16[16,32,256]{2,1,0:T(8,128)(2,1)S(1)}, u32[]{:S(2)}, u32[]{:S(2)}) %all-to-all-start) | async-done | bytes 262176 | tf_op jit(solution)/shard_map/all_to_all | solution.py:148
  18.9 0.7 %broadcast_in_dim.6 = bf16[8,48,256]{2,1,0:T(8,128)(2,1)} broadcast(bf16[48,256]{1,0:T(8,128)(2,1)S(1)} %pad_maximum_fusion.3), dimensions={1,2} | broadcast | bytes 221184 | tf_op jit(solution)/shard_map/broadcast_in_dim | solution.py:155
  19.6 8.2 %all-to-all-start.1 = ((bf16[8,48,256]{2,1,0:T(8,128)(2,1)}), bf16[8,48,256]{2,1,0:T(8,128)(2,1)S(1)}, u32[]{:S(2)}, u32[]{:S(2)}) async-start(bf16[8,48,256]{2,1,0:T(8,128)(2,1)} %broadcast_in_dim.6), calls=%async_computation.1 | async-start | bytes 393216 | tf_op jit(solution)/shard_map/all_to_all | solution.py:155
  27.8 3.1 %collective-permute-start.1 = (bf16[4,256,256]{2,1,0:T(8,128)(2,1)S(1)}, bf16[4,256,256]{2,1,0:T(8,128)(2,1)}, u32[]{:S(2)}, u32[]{:S(2)}) collective-permute-start(bf16[4,256,256]{2,1,0:T(8,128)(2,1)S(1)} %broadcast_select_fusion), channel_id=1, source_target_pairs={{2,4},{7,5},{0,6},{1,3},{10,12},{15,13},{8,14},{9,11},{18,20},{23,... | collective-permute-start | bytes 1572872 | tf_op jit(solution)/shard_map/ppermute | solution.py:152
  30.9 5.6 %all-to-all-done.1 = bf16[8,48,256]{2,1,0:T(8,128)(2,1)S(1)} async-done(((bf16[8,48,256]{2,1,0:T(8,128)(2,1)}), bf16[8,48,256]{2,1,0:T(8,128)(2,1)S(1)}, u32[]{:S(2)}, u32[]{:S(2)}) %all-to-all-start.1) | async-done | bytes 196640 | tf_op jit(solution)/shard_map/all_to_all | solution.py:155
  36.6 1.0 %broadcast_in_dim.8 = bf16[4,4,112,256]{3,2,1,0:T(8,128)(2,1)} broadcast(bf16[4,112,256]{2,1,0:T(8,128)(2,1)S(1)} %pad_maximum_fusion.2), dimensions={1,2,3} | broadcast | bytes 1146880 | tf_op jit(solution)/shard_map/broadcast_in_dim | solution.py:162
  37.6 3.6 %all-to-all-start.2 = ((bf16[16,112,256]{2,1,0:T(8,128)(2,1)}), bf16[16,112,256]{2,1,0:T(8,128)(2,1)S(1)}, u32[]{:S(2)}, u32[]{:S(2)}) async-start(bf16[16,112,256]{2,1,0:T(8,128)(2,1)} %bitcast.16), calls=%async_computation.2 | async-start | bytes 1835008 | tf_op jit(solution)/shard_map/all_to_all | solution.py:163
  41.3 1.1 %add_select_fusion = bf16[4,256,256]{2,1,0:T(8,128)(2,1)S(1)} fusion(bf16[4,256,256]{2,1,0:T(8,128)(2,1)S(1)} %get-tuple-element.15.m0, bf16[4,256,256]{2,1,0:T(8,128)(2,1)S(1)} %collective-permute-done, bf16[4,256,256]{2,1,0:T(8,128)(2,1)} %collective-permute-done.1, pred[]{:T(512)S(6)} %eq.10), kind=kLoop, calls=%fused_computation.4 | loop fusion | flops 524288 | bytes 2097153 | tf_op jit(solution)/shard_map/select_n | solution.py:169
  42.4 3.4 %collective-permute-start.2 = (bf16[4,256,256]{2,1,0:T(8,128)(2,1)S(1)}, bf16[4,256,256]{2,1,0:T(8,128)(2,1)}, u32[]{:S(2)}, u32[]{:S(2)}) collective-permute-start(bf16[4,256,256]{2,1,0:T(8,128)(2,1)S(1)} %add_select_fusion), channel_id=1, source_target_pairs={{0,1},{1,0},{2,3},{3,2},{4,5},{5,4},{6,7},{7,6},{8,9},{9,8},{10,11... | collective-permute-start | bytes 1572872 | tf_op jit(solution)/shard_map/ppermute | solution.py:19
  45.8 7.0 %all-to-all-done.2.got = bf16[16,112,256]{2,1,0:T(8,128)(2,1)S(1)} async-done(((bf16[16,112,256]{2,1,0:T(8,128)(2,1)}), bf16[16,112,256]{2,1,0:T(8,128)(2,1)S(1)}, u32[]{:S(2)}, u32[]{:S(2)}) %all-to-all-start.2) | async-done | bytes 917536 | tf_op jit(solution)/shard_map/all_to_all | solution.py:163
  52.8 0.9 %slice.53 = bf16[16,80,256]{2,1,0:T(8,128)(2,1)} slice(bf16[16,112,256]{2,1,0:T(8,128)(2,1)S(1)} %all-to-all-done.2.got), slice={[0:16], [32:112], [0:256]} | slice | bytes 1310720 | tf_op jit(solution)/shard_map/slice | solution.py:173
  53.7 5.1 %collective-permute-start.3 = (bf16[16,80,256]{2,1,0:T(8,128)(2,1)}, bf16[16,80,256]{2,1,0:T(8,128)(2,1)S(1)}, u32[]{:S(2)}, u32[]{:S(2)}) collective-permute-start(bf16[16,80,256]{2,1,0:T(8,128)(2,1)} %slice.53), channel_id=1, source_target_pairs={{0,1},{1,0},{2,3},{3,2},{4,5},{5,4},{6,7},{7,6},{8,9},{9,8},{10,11... | collective-permute-start | bytes 1966088 | tf_op jit(solution)/shard_map/ppermute | solution.py:19
  58.7 0.1 copy.9
  58.8 0.1 reshape.22
  58.9 0.1 pad_add_fusion.place
  59.0 1.2 %broadcast_select_fusion.1 = (bf16[4,256,256]{2,1,0:T(8,128)(2,1)S(1)}, bf16[4,256,256]{2,1,0:T(8,128)(2,1)S(1)}) fusion(bf16[4,256,256]{2,1,0:T(8,128)(2,1)} %collective-permute-done.2, bf16[4,256,256]{2,1,0:T(8,128)(2,1)S(1)} %add_select_fusion, pred[]{:T(512)S(6)} %eq.4), kind=kLoop, calls=%fused_computation.6 | loop fusion | flops 524288 | bytes 2097153 | tf_op jit(solution)/shard_map/select_n | solution.py:172
  60.3 0.4 collective-permute-done.3.got_o
  60.7 3.5 %finish.1 = (bf16[2,4,256,256]{3,2,1,0:T(8,128)(2,1)S(1)}, bf16[4,256,512]{2,1,0:T(8,128)(2,1)}) custom-call(s32[11]{0:T(128)S(1)} %pad_add_fusion.place, bf16[6,256,256]{2,1,0:T(8,128)(2,1)S(1)} %pad_maximum_fusion.rows0, bf16[4,256,256]{2,1,0:T(8,128)(2,1)S(1)} %get-tuple-element.16.rows1, bf16[16,112,256]{2,1,0:T(8,128)(2,1)S(1)} %all-to-all-done.2.got, ...), custom_call_target="tpu_custom_call" | custom-call | tf_op jit(solution)/shard_map/finish/pallas_call | solution.py:177
  64.2 2.0 %copy.11 = bf16[4,256,2,256]{3,2,1,0:T(2,128)(2,1)} copy(bf16[4,256,2,256]{3,1,0,2:T(8,128)(2,1)S(1)} %bitcast.34) | data formatting | bytes 2097152
  (21 shorter events, 0.3 us)
Async XLA Ops:
  0.6 0.9 %copy-start.1 = (s32[4,1,2,1]{0,3,2,1:T(1,128)S(1)}, s32[4,1,2,1]{0,3,2,1:T(1,128)}, u32[]{:S(2)}) copy-start(s32[4,1,2,1]{0,3,2,1:T(1,128)} %param.5) | copy-start | bytes 100
  3.8 15.0 %all-to-all-start = ((bf16[16,32,256]{2,1,0:T(8,128)(2,1)}), bf16[16,32,256]{2,1,0:T(8,128)(2,1)S(1)}, u32[]{:S(2)}, u32[]{:S(2)}) async-start(bf16[16,32,256]{2,1,0:T(8,128)(2,1)} %pad_maximum_fusion.1), calls=%async_computation | async-start | bytes 524288 | tf_op jit(solution)/shard_map/all_to_all | solution.py:148
  11.4 16.3 %collective-permute-start = (bf16[4,256,256]{2,1,0:T(8,128)(2,1)S(1)}, bf16[4,256,256]{2,1,0:T(8,128)(2,1)S(1)}, u32[]{:S(2)}, u32[]{:S(2)}) collective-permute-start(bf16[4,256,256]{2,1,0:T(8,128)(2,1)S(1)} %get-tuple-element.15.m0), channel_id=1, source_target_pairs={{0,2},{1,7},{8,10},{9,15},{16,18},{17,23},{24,26},{25,31},{32,34},... | collective-permute-start | bytes 1572872 | tf_op jit(solution)/shard_map/ppermute | solution.py:150
  19.6 16.9 %all-to-all-start.1 = ((bf16[8,48,256]{2,1,0:T(8,128)(2,1)}), bf16[8,48,256]{2,1,0:T(8,128)(2,1)S(1)}, u32[]{:S(2)}, u32[]{:S(2)}) async-start(bf16[8,48,256]{2,1,0:T(8,128)(2,1)} %broadcast_in_dim.6), calls=%async_computation.1 | async-start | bytes 393216 | tf_op jit(solution)/shard_map/all_to_all | solution.py:155
  27.8 13.4 %collective-permute-start.1 = (bf16[4,256,256]{2,1,0:T(8,128)(2,1)S(1)}, bf16[4,256,256]{2,1,0:T(8,128)(2,1)}, u32[]{:S(2)}, u32[]{:S(2)}) collective-permute-start(bf16[4,256,256]{2,1,0:T(8,128)(2,1)S(1)} %broadcast_select_fusion), channel_id=1, source_target_pairs={{2,4},{7,5},{0,6},{1,3},{10,12},{15,13},{8,14},{9,11},{18,20},{23,... | collective-permute-start | bytes 1572872 | tf_op jit(solution)/shard_map/ppermute | solution.py:152
  37.6 15.2 %all-to-all-start.2 = ((bf16[16,112,256]{2,1,0:T(8,128)(2,1)}), bf16[16,112,256]{2,1,0:T(8,128)(2,1)S(1)}, u32[]{:S(2)}, u32[]{:S(2)}) async-start(bf16[16,112,256]{2,1,0:T(8,128)(2,1)} %bitcast.16), calls=%async_computation.2 | async-start | bytes 1835008 | tf_op jit(solution)/shard_map/all_to_all | solution.py:163
  42.4 16.6 %collective-permute-start.2 = (bf16[4,256,256]{2,1,0:T(8,128)(2,1)S(1)}, bf16[4,256,256]{2,1,0:T(8,128)(2,1)}, u32[]{:S(2)}, u32[]{:S(2)}) collective-permute-start(bf16[4,256,256]{2,1,0:T(8,128)(2,1)S(1)} %add_select_fusion), channel_id=1, source_target_pairs={{0,1},{1,0},{2,3},{3,2},{4,5},{5,4},{6,7},{7,6},{8,9},{9,8},{10,11... | collective-permute-start | bytes 1572872 | tf_op jit(solution)/shard_map/ppermute | solution.py:19
  53.7 7.0 %collective-permute-start.3 = (bf16[16,80,256]{2,1,0:T(8,128)(2,1)}, bf16[16,80,256]{2,1,0:T(8,128)(2,1)S(1)}, u32[]{:S(2)}, u32[]{:S(2)}) collective-permute-start(bf16[16,80,256]{2,1,0:T(8,128)(2,1)} %slice.53), channel_id=1, source_target_pairs={{0,1},{1,0},{2,3},{3,2},{4,5},{5,4},{6,7},{7,6},{8,9},{9,8},{10,11... | collective-permute-start | bytes 1966088 | tf_op jit(solution)/shard_map/ppermute | solution.py:19
  59.0 1.2 %copy-start = (bf16[2,256,256]{2,1,0:T(8,128)(2,1)S(1)}, bf16[2,256,256]{2,1,0:T(8,128)(2,1)}, u32[]{:S(2)}) copy-start(bf16[2,256,256]{2,1,0:T(8,128)(2,1)} %param.6) | copy-start | bytes 786436

commit v9 on v8

--- a/solution.py
+++ b/solution.py
@@ -35,7 +35,7 @@
     return jnp.where(cond, value, jnp.zeros_like(value))
 
 
-def finish(ends, place, f0, f1, g0, g1, m0, m1, samples, slab, solved, lrow, lcol, ys, obuf, sem, arrival):
+def finish(ends, place, f0, lrow, lead, g0, g1, m0, m1, samples, slab, solved, lcol, ys, obuf, sem, arrival):
     row_pos = place[0]
     col_pos = place[1]
     w = (f0[TR], f0[TR + 1])
@@ -48,30 +48,20 @@
     def from_second(tile_second, first):
         return (tile_second.astype(F32) - mmt(first, l0_one)).astype(BF16)
 
-    l0_one = mm(tile(g0, e0), w[0]).astype(BF16)
+    l0_one = lead[0]
+    slab[0, 0] = lead[1]
     first_col = [mm(tile(g0, b), w[0]).astype(BF16) for b in range(TC)]
     first_col[0] = keep(col_pos >= 1, first_col[0])
-    y0 = tmm(w[0], jnp.concatenate([tile(g0, e0 + 1), tile(g1, e1 + 1)], axis=1)).astype(BF16)
-    first_row = mm(f0[0:TR].reshape(TR * T, T), w[0]).astype(BF16)
-    first_row = [first_row[a * T : (a + 1) * T] for a in range(TR)]
-    first_row[0] = keep(row_pos >= 1, first_row[0])
+    y0 = tmm(w[0], jnp.concatenate([tile(g0, e0), tile(g1, e1)], axis=1)).astype(BF16)
     ys[0:T, :] = y0
     for b in range(TC):
         lcol[b * T : (b + 1) * T, 0:T] = first_col[b]
-    for a in range(TR):
-        lrow[a * T : (a + 1) * T, 0:T] = first_row[a]
-
+    r1 = jnp.concatenate([tile(g0, e0 + 1), tile(g1, e1 + 1)], axis=1).astype(F32) - mm(l0_one, y0)
     second_col = [from_second(tile(g1, b), first_col[b]) for b in range(TC)]
-    second_row = [from_second(f1[a], first_row[a]) for a in range(TR)]
-    r1 = jnp.concatenate([tile(g0, e0 + 2), tile(g1, e1 + 2)], axis=1).astype(F32) - mm(l0_one, y0)
-    slab[0, 0] = second_row[0]
+    ys[T : 2 * T, :] = tmm(w[1], r1.astype(BF16)).astype(BF16)
     for b in range(TC):
         third = mm(second_col[b], w[1]).astype(BF16)
         lcol[b * T : (b + 1) * T, T : 2 * T] = keep(col_pos >= 2, third) if b == 0 else third
-    for a in range(TR):
-        third = mm(second_row[a], w[1]).astype(BF16)
-        lrow[a * T : (a + 1) * T, T : 2 * T] = keep(row_pos >= 2, third) if a == 0 else third
-    ys[T : 2 * T, :] = tmm(w[1], r1.astype(BF16)).astype(BF16)
 
     arrival.wait()
     for a in range(TR):
@@ -117,7 +107,25 @@
     out.wait()
 
 
-def finish_kernel(place, rows0, rows1, got, got_o, m0, m1, samples_far, *rest):
+def head_kernel(place, rows0, rows1, one, lrow, lead):
+    row_pos = place[0]
+    w = (rows0[TR], rows0[TR + 1])
+    l0_one = mm(one[...], w[0]).astype(BF16)
+    lead[0] = l0_one
+    first = mm(rows0[0:TR].reshape(TR * T, T), w[0]).astype(BF16)
+    for a in range(TR):
+        rows = slice(a * T, (a + 1) * T)
+        left = keep(row_pos >= 1, first[rows]) if a == 0 else first[rows]
+        second = (rows1[a].astype(F32) - mmt(left, l0_one)).astype(BF16)
+        third = mm(second, w[1]).astype(BF16)
+        if a == 0:
+            lead[1] = second
+            third = keep(row_pos >= 2, third)
+        lrow[rows, 0:T] = left
+        lrow[rows, T : 2 * T] = third
+
+
+def finish_kernel(place, rows0, lrow, lead, got, got_o, m0, m1, samples_far, *rest):
     *rest, samples, samples_sem = rest
     arrival = pltpu.make_async_copy(samples_far, samples, samples_sem)
     arrival.start()
@@ -125,11 +133,11 @@
 
     @pl.when(place[2] == 0)
     def _():
-        finish((4, 2), place, rows0, rows1, got, got_o, *rest)
+        finish((5, 2), place, rows0, lrow, lead, got, got_o, *rest)
 
     @pl.when(place[2] == 1)
     def _():
-        finish((2, 4), place, rows0, rows1, got_o, got, *rest)
+        finish((2, 5), place, rows0, lrow, lead, got_o, got, *rest)
 
 
 def body(front, fill, w, samples):
@@ -155,10 +163,12 @@
     got = lax.all_to_all(jnp.broadcast_to(send[None], (Z,) + send.shape), "z", 0, 0)
 
     pairs = got.reshape(Y, 2, 3 * RB, T)[:, :, : 2 * RB, :].reshape(Y, 4 * RB, T)
-    common = jnp.concatenate([got[1, :RB], got[0, 2 * RB :], got[1, 2 * RB :]], axis=0)
+    tile_one = jnp.broadcast_to(got[1:2, :RB], (Y, RB, T))
+    samp = jnp.concatenate([got[0, 2 * RB :], got[1, 2 * RB :]], axis=0)
+    samp = jnp.broadcast_to(samp[None], (Y,) + samp.shape)
     pairs = pairs.reshape(Y, 2, 2 * RB, T)
-    pairs = lax.select(k == 0, pairs, pairs[:, ::-1]).reshape(Y, 4 * RB, T)
-    send = jnp.concatenate([pairs, jnp.broadcast_to(common[None], (Y,) + common.shape)], axis=1)
+    pairs = lax.select(k == 0, pairs, pairs[:, ::-1])
+    send = jnp.concatenate([pairs[:, 0], tile_one, pairs[:, 1], samp], axis=1)
     send = jnp.broadcast_to(send[None], (X,) + send.shape).reshape(Q, 7 * RB, T)
     got = lax.all_to_all(send, ("x", "y"), 0, 0)
 
@@ -170,20 +180,32 @@
     other = swap(own)
     rows0 = jnp.concatenate([lax.select(k == 0, own, other), w])
     rows1 = lax.select(k == 0, other, own)
-    got_o = swap(got[:, 2 * RB :])
+    one = got[:, 2 * RB : 3 * RB]
+    one = lax.select(k == 0, one, swap(one)).reshape(T, T)
+    got_o = swap(got[:, 3 * RB :])
 
     vmem = pl.BlockSpec(memory_space=pltpu.VMEM)
     smem = pl.BlockSpec(memory_space=pltpu.SMEM)
+    lrow, lead = pl.pallas_call(
+        head_kernel,
+        in_specs=[smem] + [vmem] * 3,
+        out_specs=[vmem, vmem],
+        out_shape=[
+            jax.ShapeDtypeStruct((TR * T, 2 * T), BF16),
+            jax.ShapeDtypeStruct((2, T, T), BF16),
+        ],
+        compiler_params=pltpu.CompilerParams(vmem_limit_bytes=16 * 1024 * 1024),
+        name="head",
+    )(place, rows0, rows1, one)
     slab, solved = pl.pallas_call(
         finish_kernel,
-        in_specs=[smem] + [vmem] * 6 + [pl.BlockSpec(memory_space=pltpu.HBM)],
+        in_specs=[smem] + [vmem] * 7 + [pl.BlockSpec(memory_space=pltpu.HBM)],
         out_specs=[vmem, pl.BlockSpec(memory_space=pl.ANY)],
         out_shape=[
             jax.ShapeDtypeStruct((TC, TR, T, T), BF16),
             jax.ShapeDtypeStruct((TR, T, 2 * T), BF16),
         ],
         scratch_shapes=[
-            pltpu.VMEM((TR * T, 2 * T), BF16),
             pltpu.VMEM((TC * T, 2 * T), BF16),
             pltpu.VMEM((2 * T, 2 * T), BF16),
             pltpu.VMEM((TR, T, 2 * T), BF16),
@@ -196,7 +218,8 @@
     )(
         place,
         rows0,
-        rows1,
+        lrow,
+        lead,
         got,
         got_o,
         panel,

time: 66.8 us -> 66.6 us (level)
  Pallas kernels: 3.47 us -> 4.91 us
  other arithmetic: 4.67 us -> 3.37 us
    pallas_call x1 -> x2, Pallas kernels: 3.47 us -> 4.91 us  [the longest x1 3.53 us: body(): pl.pallas_call(finish_kernel, in_specs=[smem] + [vmem] * 7 + [pl.BlockSpe...]
    select_n x1, other arithmetic: 1.16 us -> 0.07 us  [body(): rows1 = lax.select(k == 0, other, own)]
    select_n x1, other arithmetic: 1.12 us -> 0.08 us  [body(): own = lax.select(y == 0, panel, near + far)]
    slice x1 -> x2, local copies, waits for them, and re-layouts: 0.88 us -> 0.06 us  [the longest x1 0.05 us: body(): got_o = swap(got[:, 3 * RB:])]
    select_n x1, other arithmetic: 0.06 us -> 0.87 us  [body(): relay = lax.select(y == 0, panel, near)]
    ppermute x1, starting transfers between devices: 3.08 us -> 2.3 us  [body(): far = lax.ppermute(relay, ('y', 'core'), [(2, 4), (7, 5), (0, 6), (1, 3)])]
    all_to_all x2, waiting for transfers between devices: 9.93 us -> 10.7 us  [body(): got = lax.all_to_all(send, ('x', 'y'), 0, 0)]
    unnamed x7, local copies, waits for them, and re-layouts: 2.15 us -> 2.9 us
  transfers between devices with their start and end apart: 7 -> 8, of which waited for: 4 -> 3; matrix products, arithmetic and copies ran while one was open for 8% -> 5% of each run, Pallas kernels for 0% -> 2%
where the time goes in v9:
time: 66.6 us; the launch traced here: 66.1 us
  starting transfers between devices  34.9 us (52%)
  waiting for transfers between devices  16.3 us (24%)
  local copies, waits for them, and re-layouts  5.76 us (9%)
  Pallas kernels  4.91 us (7%)
  other arithmetic  3.37 us (5%)
  between operations  0.88 us (1%)
    all_to_all x2, starting transfers between devices, body(): got = lax.all_to_all(send, ('x', 'y'), 0, 0)  11.2 us
    all_to_all x2, waiting for transfers between devices, body(): got = lax.all_to_all(send, ('x', 'y'), 0, 0)  10.7 us
    ppermute x3, starting transfers between devices, swap(): return lax.ppermute(v, 'core', [(0, 1), (1, 0)])  8.68 us
    all_to_all x1, starting transfers between devices, body(): lax.all_to_all(jnp.broadcast_to(send[None], (Z,) + send.shape), 'z', 0, 0)  8.19 us
    all_to_all x1, waiting for transfers between devices, body(): lax.all_to_all(jnp.broadcast_to(send[None], (Z,) + send.shape), 'z', 0, 0)  5.58 us
    ppermute x1, starting transfers between devices, body(): near = lax.ppermute(panel, ('y', 'core'), [(0, 2), (1, 7)])  4.5 us
    pallas_call x1, Pallas kernels, body(): pl.pallas_call(finish_kernel, in_specs=[smem] + [vmem] * 7 + [pl.BlockSpe...  3.53 us
    unnamed x7, local copies, waits for them, and re-layouts  2.9 us
  transfers between devices with their start and end apart: 8, of which 3 were waited for; matrix products, arithmetic and copies ran while one was open for 5% of the time, Pallas kernels for 2%

profile of v9, /device:TPU:1, one launch (start us, length us, event | category | flops | bytes accessed | tf_op | source)
XLA Modules:
  0.0 66.1 jit_solution(14682724069245927949)
XLA Ops:
  0.6 0.9 %constant_dynamic-slice_fusion = bf16[1,256,256]{2,1,0:T(8,128)(2,1)S(1)} fusion(bf16[4,256,512]{2,1,0:T(8,128)(2,1)} %samples_far.1, s32[]{:T(128)S(6)} %select_n.37), kind=kLoop, calls=%fused_computation.25 | loop fusion | bytes 262148 | tf_op jit(solution)/shard_map/dynamic_slice | solution.py:148
  1.6 1.4 %bitcast_multiply_fusion = bf16[2,4,256,256]{3,2,1,0:T(8,128)(2,1)S(1)} fusion(bf16[4,256,2,256]{3,2,1,0:T(2,128)(2,1)} %param.4, bf16[2,4]{1,0:T(2,128)(2,1)S(1)} %bitcast.45), kind=kLoop, calls=%fused_computation | loop fusion | flops 524288 | bytes 2097168 | tf_op jit(solution)/shard_map/mul | solution.py:150
  3.1 0.7 %pad_maximum_fusion.1 = bf16[16,32,256]{2,1,0:T(8,128)(2,1)} fusion(bf16[16,16,256]{2,1,0:T(8,128)(2,1)S(1)} %bitcast.43, bf16[16,16,256]{2,1,0:T(8,128)(2,1)S(1)} %bitcast.44), kind=kLoop, calls=%fused_computation.8 | loop fusion | flops 524288 | bytes 524288 | tf_op jit(solution)/shard_map/concatenate | solution.py:155
  3.8 7.6 %all-to-all-start = ((bf16[16,32,256]{2,1,0:T(8,128)(2,1)}), bf16[16,32,256]{2,1,0:T(8,128)(2,1)S(1)}, u32[]{:S(2)}, u32[]{:S(2)}) async-start(bf16[16,32,256]{2,1,0:T(8,128)(2,1)} %pad_maximum_fusion.1), calls=%async_computation | async-start | bytes 524288 | tf_op jit(solution)/shard_map/all_to_all | solution.py:156
  11.4 4.5 %collective-permute-start = (bf16[4,256,256]{2,1,0:T(8,128)(2,1)S(1)}, bf16[4,256,256]{2,1,0:T(8,128)(2,1)S(1)}, u32[]{:S(2)}, u32[]{:S(2)}) collective-permute-start(bf16[4,256,256]{2,1,0:T(8,128)(2,1)S(1)} %get-tuple-element.19.m0), channel_id=1, source_target_pairs={{0,2},{1,7},{8,10},{9,15},{16,18},{17,23},{24,26},{25,31},{32,34},... | collective-permute-start | bytes 1572872 | tf_op jit(solution)/shard_map/ppermute | solution.py:158
  15.9 2.9 %all-to-all-done = bf16[16,32,256]{2,1,0:T(8,128)(2,1)S(1)} async-done(((bf16[16,32,256]{2,1,0:T(8,128)(2,1)}), bf16[16,32,256]{2,1,0:T(8,128)(2,1)S(1)}, u32[]{:S(2)}, u32[]{:S(2)}) %all-to-all-start) | async-done | bytes 262176 | tf_op jit(solution)/shard_map/all_to_all | solution.py:156
  18.9 0.7 %broadcast_in_dim.10 = bf16[8,48,256]{2,1,0:T(8,128)(2,1)} broadcast(bf16[48,256]{1,0:T(8,128)(2,1)S(1)} %pad_maximum_fusion.3), dimensions={1,2} | broadcast | bytes 221184 | tf_op jit(solution)/shard_map/broadcast_in_dim | solution.py:163
  19.6 8.2 %all-to-all-start.1 = ((bf16[8,48,256]{2,1,0:T(8,128)(2,1)}), bf16[8,48,256]{2,1,0:T(8,128)(2,1)S(1)}, u32[]{:S(2)}, u32[]{:S(2)}) async-start(bf16[8,48,256]{2,1,0:T(8,128)(2,1)} %broadcast_in_dim.10), calls=%async_computation.1 | async-start | bytes 393216 | tf_op jit(solution)/shard_map/all_to_all | solution.py:163
  27.8 0.9 %broadcast_select_fusion = bf16[4,256,256]{2,1,0:T(8,128)(2,1)} fusion(bf16[4,256,256]{2,1,0:T(8,128)(2,1)S(1)} %get-tuple-element.19.m0, bf16[4,256,256]{2,1,0:T(8,128)(2,1)S(1)} %collective-permute-done, pred[]{:T(512)S(6)} %eq.5), kind=kLoop, calls=%fused_computation.5 | loop fusion | flops 262144 | bytes 1572865 | tf_op jit(solution)/shard_map/select_n | solution.py:159
  28.6 2.3 %collective-permute-start.1 = (bf16[4,256,256]{2,1,0:T(8,128)(2,1)}, bf16[4,256,256]{2,1,0:T(8,128)(2,1)S(1)}, u32[]{:S(2)}, u32[]{:S(2)}) collective-permute-start(bf16[4,256,256]{2,1,0:T(8,128)(2,1)} %broadcast_select_fusion), channel_id=1, source_target_pairs={{2,4},{7,5},{0,6},{1,3},{10,12},{15,13},{8,14},{9,11},{18,20},{23,... | collective-permute-start | bytes 1572872 | tf_op jit(solution)/shard_map/ppermute | solution.py:160
  30.9 5.6 %all-to-all-done.1 = bf16[8,48,256]{2,1,0:T(8,128)(2,1)S(1)} async-done(((bf16[8,48,256]{2,1,0:T(8,128)(2,1)}), bf16[8,48,256]{2,1,0:T(8,128)(2,1)S(1)}, u32[]{:S(2)}, u32[]{:S(2)}) %all-to-all-start.1) | async-done | bytes 196640 | tf_op jit(solution)/shard_map/all_to_all | solution.py:163
  36.6 1.0 %broadcast_in_dim.14 = bf16[4,4,112,256]{3,2,1,0:T(8,128)(2,1)} broadcast(bf16[4,112,256]{2,1,0:T(8,128)(2,1)S(1)} %pad_maximum_fusion.2), dimensions={1,2,3} | broadcast | bytes 1146880 | tf_op jit(solution)/shard_map/broadcast_in_dim | solution.py:172
  37.6 3.6 %all-to-all-start.2 = ((bf16[16,112,256]{2,1,0:T(8,128)(2,1)}), bf16[16,112,256]{2,1,0:T(8,128)(2,1)S(1)}, u32[]{:S(2)}, u32[]{:S(2)}) async-start(bf16[16,112,256]{2,1,0:T(8,128)(2,1)} %bitcast.17), calls=%async_computation.2 | async-start | bytes 1835008 | tf_op jit(solution)/shard_map/all_to_all | solution.py:173
  41.3 0.1 add_select_fusion
  41.4 3.4 %collective-permute-start.2 = (bf16[4,256,256]{2,1,0:T(8,128)(2,1)S(1)}, bf16[4,256,256]{2,1,0:T(8,128)(2,1)S(1)}, u32[]{:S(2)}, u32[]{:S(2)}) collective-permute-start(bf16[4,256,256]{2,1,0:T(8,128)(2,1)S(1)} %add_select_fusion), channel_id=1, source_target_pairs={{0,1},{1,0},{2,3},{3,2},{4,5},{5,4},{6,7},{7,6},{8,9},{9,8},{10,11... | collective-permute-start | bytes 1572872 | tf_op jit(solution)/shard_map/ppermute | solution.py:19
  44.8 0.1 copy.9
  44.9 0.1 reshape.22
  45.0 7.8 %all-to-all-done.2.got = bf16[16,112,256]{2,1,0:T(8,128)(2,1)S(1)} async-done(((bf16[16,112,256]{2,1,0:T(8,128)(2,1)}), bf16[16,112,256]{2,1,0:T(8,128)(2,1)S(1)}, u32[]{:S(2)}, u32[]{:S(2)}) %all-to-all-start.2) | async-done | bytes 917536 | tf_op jit(solution)/shard_map/all_to_all | solution.py:173
  52.8 5.2 %collective-permute-start.3 = (bf16[16,16,256]{2,1,0:T(8,128)(2,1)S(1)}, bf16[16,16,256]{2,1,0:T(8,128)(2,1)S(1)}, u32[]{:S(2)}, u32[]{:S(2)}) collective-permute-start(bf16[16,16,256]{2,1,0:T(8,128)(2,1)S(1)} %slice.67), channel_id=1, source_target_pairs={{0,1},{1,0},{2,3},{3,2},{4,5},{5,4},{6,7},{7,6},{8,9},{9,8},{10,11... | collective-permute-start | bytes 393224 | tf_op jit(solution)/shard_map/ppermute | solution.py:19
  58.1 0.1 collective-permute-start.4
  58.3 0.7 %copy-done = bf16[2,256,256]{2,1,0:T(8,128)(2,1)S(1)} copy-done((bf16[2,256,256]{2,1,0:T(8,128)(2,1)S(1)}, bf16[2,256,256]{2,1,0:T(8,128)(2,1)}, u32[]{:S(2)}) %copy-start) | copy-done | bytes 262168
  59.1 1.4 %head.1 = (bf16[1024,512]{1,0:T(8,128)(2,1)S(1)}, bf16[2,256,256]{2,1,0:T(8,128)(2,1)S(1)}) custom-call(s32[11]{0:T(128)S(1)} %pad_add_fusion.place, bf16[6,256,256]{2,1,0:T(8,128)(2,1)S(1)} %pad_maximum_fusion.rows0, bf16[4,256,256]{2,1,0:T(8,128)(2,1)S(1)} %get-tuple-element.20.rows1, bf16[256,256]{1,0:T(8,128)(2,1)S(1)} %bitcast.41), custom_call_target="tpu_custom_call" | custom-call | tf_op jit(solution)/shard_map/head/pallas_call | solution.py:189
  60.5 3.5 %finish.1 = (bf16[2,4,256,256]{3,2,1,0:T(8,128)(2,1)S(1)}, bf16[4,256,512]{2,1,0:T(8,128)(2,1)}) custom-call(s32[11]{0:T(128)S(1)} %pad_add_fusion.place, bf16[6,256,256]{2,1,0:T(8,128)(2,1)S(1)} %pad_maximum_fusion.rows0, bf16[1024,512]{1,0:T(8,128)(2,1)S(1)} %get-tuple-element.10.lrow, bf16[2,256,256]{2,1,0:T(8,128)(2,1)S(1)} %get-tuple-element.11.lead, ...), custom_call_target="tpu_custom_call" | custom-call | tf_op jit(solution)/shard_map/finish/pallas_call | solution.py:200
  64.0 2.0 %copy.12 = bf16[4,256,2,256]{3,2,1,0:T(2,128)(2,1)} copy(bf16[4,256,2,256]{3,1,0,2:T(8,128)(2,1)S(1)} %bitcast.40) | data formatting | bytes 2097152
  (28 shorter events, 0.5 us)
Async XLA Ops:
  0.6 0.9 %copy-start.1 = (s32[4,1,2,1]{0,3,2,1:T(1,128)S(1)}, s32[4,1,2,1]{0,3,2,1:T(1,128)}, u32[]{:S(2)}) copy-start(s32[4,1,2,1]{0,3,2,1:T(1,128)} %param.5) | copy-start | bytes 100
  3.8 15.0 %all-to-all-start = ((bf16[16,32,256]{2,1,0:T(8,128)(2,1)}), bf16[16,32,256]{2,1,0:T(8,128)(2,1)S(1)}, u32[]{:S(2)}, u32[]{:S(2)}) async-start(bf16[16,32,256]{2,1,0:T(8,128)(2,1)} %pad_maximum_fusion.1), calls=%async_computation | async-start | bytes 524288 | tf_op jit(solution)/shard_map/all_to_all | solution.py:156
  11.4 16.3 %collective-permute-start = (bf16[4,256,256]{2,1,0:T(8,128)(2,1)S(1)}, bf16[4,256,256]{2,1,0:T(8,128)(2,1)S(1)}, u32[]{:S(2)}, u32[]{:S(2)}) collective-permute-start(bf16[4,256,256]{2,1,0:T(8,128)(2,1)S(1)} %get-tuple-element.19.m0), channel_id=1, source_target_pairs={{0,2},{1,7},{8,10},{9,15},{16,18},{17,23},{24,26},{25,31},{32,34},... | collective-permute-start | bytes 1572872 | tf_op jit(solution)/shard_map/ppermute | solution.py:158
  19.6 16.9 %all-to-all-start.1 = ((bf16[8,48,256]{2,1,0:T(8,128)(2,1)}), bf16[8,48,256]{2,1,0:T(8,128)(2,1)S(1)}, u32[]{:S(2)}, u32[]{:S(2)}) async-start(bf16[8,48,256]{2,1,0:T(8,128)(2,1)} %broadcast_in_dim.10), calls=%async_computation.1 | async-start | bytes 393216 | tf_op jit(solution)/shard_map/all_to_all | solution.py:163
  28.6 12.7 %collective-permute-start.1 = (bf16[4,256,256]{2,1,0:T(8,128)(2,1)}, bf16[4,256,256]{2,1,0:T(8,128)(2,1)S(1)}, u32[]{:S(2)}, u32[]{:S(2)}) collective-permute-start(bf16[4,256,256]{2,1,0:T(8,128)(2,1)} %broadcast_select_fusion), channel_id=1, source_target_pairs={{2,4},{7,5},{0,6},{1,3},{10,12},{15,13},{8,14},{9,11},{18,20},{23,... | collective-permute-start | bytes 1572872 | tf_op jit(solution)/shard_map/ppermute | solution.py:160
  37.6 15.2 %all-to-all-start.2 = ((bf16[16,112,256]{2,1,0:T(8,128)(2,1)}), bf16[16,112,256]{2,1,0:T(8,128)(2,1)S(1)}, u32[]{:S(2)}, u32[]{:S(2)}) async-start(bf16[16,112,256]{2,1,0:T(8,128)(2,1)} %bitcast.17), calls=%async_computation.2 | async-start | bytes 1835008 | tf_op jit(solution)/shard_map/all_to_all | solution.py:173
  41.4 16.8 %collective-permute-start.2 = (bf16[4,256,256]{2,1,0:T(8,128)(2,1)S(1)}, bf16[4,256,256]{2,1,0:T(8,128)(2,1)S(1)}, u32[]{:S(2)}, u32[]{:S(2)}) collective-permute-start(bf16[4,256,256]{2,1,0:T(8,128)(2,1)S(1)} %add_select_fusion), channel_id=1, source_target_pairs={{0,1},{1,0},{2,3},{3,2},{4,5},{5,4},{6,7},{7,6},{8,9},{9,8},{10,11... | collective-permute-start | bytes 1572872 | tf_op jit(solution)/shard_map/ppermute | solution.py:19
  52.8 6.3 %collective-permute-start.3 = (bf16[16,16,256]{2,1,0:T(8,128)(2,1)S(1)}, bf16[16,16,256]{2,1,0:T(8,128)(2,1)S(1)}, u32[]{:S(2)}, u32[]{:S(2)}) collective-permute-start(bf16[16,16,256]{2,1,0:T(8,128)(2,1)S(1)} %slice.67), channel_id=1, source_target_pairs={{0,1},{1,0},{2,3},{3,2},{4,5},{5,4},{6,7},{7,6},{8,9},{9,8},{10,11... | collective-permute-start | bytes 393224 | tf_op jit(solution)/shard_map/ppermute | solution.py:19
  58.0 1.0 %copy-start = (bf16[2,256,256]{2,1,0:T(8,128)(2,1)S(1)}, bf16[2,256,256]{2,1,0:T(8,128)(2,1)}, u32[]{:S(2)}) copy-start(bf16[2,256,256]{2,1,0:T(8,128)(2,1)} %param.6) | copy-start | bytes 786436
  58.1 2.4 %collective-permute-start.4 = (bf16[16,64,256]{2,1,0:T(8,128)(2,1)S(1)}, bf16[16,64,256]{2,1,0:T(8,128)(2,1)S(1)}, u32[]{:S(2)}, u32[]{:S(2)}) collective-permute-start(bf16[16,64,256]{2,1,0:T(8,128)(2,1)S(1)} %slice.68), channel_id=1, source_target_pairs={{0,1},{1,0},{2,3},{3,2},{4,5},{5,4},{6,7},{7,6},{8,9},{9,8},{10,11... | collective-permute-start | bytes 1572872 | tf_op jit(solution)/shard_map/ppermute | solution.py:19

commit v10 on v9

--- a/solution.py
+++ b/solution.py
@@ -35,7 +35,7 @@
     return jnp.where(cond, value, jnp.zeros_like(value))
 
 
-def finish(ends, place, f0, lrow, lead, g0, g1, m0, m1, samples, slab, solved, lcol, ys, obuf, sem, arrival):
+def finish(ends, place, f0, lrow, lead, g0, g1, m0, m1, samples, slab, solved, lcol, ys, obuf, sem):
     row_pos = place[0]
     col_pos = place[1]
     w = (f0[TR], f0[TR + 1])
@@ -63,7 +63,6 @@
         third = mm(second_col[b], w[1]).astype(BF16)
         lcol[b * T : (b + 1) * T, T : 2 * T] = keep(col_pos >= 2, third) if b == 0 else third
 
-    arrival.wait()
     for a in range(TR):
         rows = lrow[a * T : (a + 1) * T, :]
         solved_tile = (samples[a].astype(F32) - mm(rows, ys[...])).astype(BF16)
@@ -107,7 +106,9 @@
     out.wait()
 
 
-def head_kernel(place, rows0, rows1, one, lrow, lead):
+def head_kernel(place, rows0, rows1, one, samples_far, lrow, lead, samples, sem):
+    arrival = pltpu.make_async_copy(samples_far, samples, sem)
+    arrival.start()
     row_pos = place[0]
     w = (rows0[TR], rows0[TR + 1])
     l0_one = mm(one[...], w[0]).astype(BF16)
@@ -123,14 +124,10 @@
             third = keep(row_pos >= 2, third)
         lrow[rows, 0:T] = left
         lrow[rows, T : 2 * T] = third
-
-
-def finish_kernel(place, rows0, lrow, lead, got, got_o, m0, m1, samples_far, *rest):
-    *rest, samples, samples_sem = rest
-    arrival = pltpu.make_async_copy(samples_far, samples, samples_sem)
-    arrival.start()
-    rest = (m0, m1, samples, *rest, arrival)
-
+    arrival.wait()
+
+
+def finish_kernel(place, rows0, lrow, lead, got, got_o, *rest):
     @pl.when(place[2] == 0)
     def _():
         finish((5, 2), place, rows0, lrow, lead, got, got_o, *rest)
@@ -186,20 +183,22 @@
 
     vmem = pl.BlockSpec(memory_space=pltpu.VMEM)
     smem = pl.BlockSpec(memory_space=pltpu.SMEM)
-    lrow, lead = pl.pallas_call(
+    lrow, lead, samples_near = pl.pallas_call(
         head_kernel,
-        in_specs=[smem] + [vmem] * 3,
-        out_specs=[vmem, vmem],
+        in_specs=[smem] + [vmem] * 3 + [pl.BlockSpec(memory_space=pltpu.HBM)],
+        out_specs=[vmem, vmem, vmem],
         out_shape=[
             jax.ShapeDtypeStruct((TR * T, 2 * T), BF16),
             jax.ShapeDtypeStruct((2, T, T), BF16),
+            jax.ShapeDtypeStruct((TR, T, 2 * T), BF16),
         ],
+        scratch_shapes=[pltpu.SemaphoreType.DMA],
         compiler_params=pltpu.CompilerParams(vmem_limit_bytes=16 * 1024 * 1024),
         name="head",
-    )(place, rows0, rows1, one)
+    )(place, rows0, rows1, one, pltpu.with_memory_space_constraint(samples, pltpu.HBM))
     slab, solved = pl.pallas_call(
         finish_kernel,
-        in_specs=[smem] + [vmem] * 7 + [pl.BlockSpec(memory_space=pltpu.HBM)],
+        in_specs=[smem] + [vmem] * 8,
         out_specs=[vmem, pl.BlockSpec(memory_space=pl.ANY)],
         out_shape=[
             jax.ShapeDtypeStruct((TC, TR, T, T), BF16),
@@ -208,8 +207,6 @@
         scratch_shapes=[
             pltpu.VMEM((TC * T, 2 * T), BF16),
             pltpu.VMEM((2 * T, 2 * T), BF16),
-            pltpu.VMEM((TR, T, 2 * T), BF16),
-            pltpu.SemaphoreType.DMA,
             pltpu.VMEM((TR, T, 2 * T), BF16),
             pltpu.SemaphoreType.DMA,
         ],
@@ -224,7 +221,7 @@
         got_o,
         panel,
         rest,
-        pltpu.with_memory_space_constraint(samples, pltpu.HBM),
+        samples_near,
     )
     return slab.transpose(1, 2, 0, 3), solved
 

time: 66.6 us -> 66.5 us (level)
  transfers between devices with their start and end apart: 8 -> 8, of which waited for: 3 -> 3; matrix products, arithmetic and copies ran while one was open for 5% -> 5% of each run, Pallas kernels for 2% -> 3%
where the time goes in v10:
time: 66.5 us; the launch traced here: 65.9 us
  starting transfers between devices  34.9 us (52%)
  waiting for transfers between devices  16.3 us (25%)
  local copies, waits for them, and re-layouts  5.76 us (9%)
  Pallas kernels  4.75 us (7%)
  other arithmetic  3.37 us (5%)
  between operations  0.88 us (1%)
    all_to_all x2, starting transfers between devices, body(): got = lax.all_to_all(send, ('x', 'y'), 0, 0)  11.2 us
    all_to_all x2, waiting for transfers between devices, body(): got = lax.all_to_all(send, ('x', 'y'), 0, 0)  10.7 us
    ppermute x3, starting transfers between devices, swap(): return lax.ppermute(v, 'core', [(0, 1), (1, 0)])  8.68 us
    all_to_all x1, starting transfers between devices, body(): lax.all_to_all(jnp.broadcast_to(send[None], (Z,) + send.shape), 'z', 0, 0)  8.19 us
    all_to_all x1, waiting for transfers between devices, body(): lax.all_to_all(jnp.broadcast_to(send[None], (Z,) + send.shape), 'z', 0, 0)  5.58 us
    ppermute x1, starting transfers between devices, body(): near = lax.ppermute(panel, ('y', 'core'), [(0, 2), (1, 7)])  4.5 us
    pallas_call x1, Pallas kernels, body(): pl.pallas_call(finish_kernel, in_specs=[smem] + [vmem] * 8, out_specs=[vm...  2.97 us
    unnamed x7, local copies, waits for them, and re-layouts  2.9 us
  transfers between devices with their start and end apart: 8, of which 3 were waited for; matrix products, arithmetic and copies ran while one was open for 5% of the time, Pallas kernels for 3%

profile of v10, /device:TPU:1, one launch (start us, length us, event | category | flops | bytes accessed | tf_op | source)
XLA Modules:
  0.0 65.9 jit_solution(10385679482038001084)
XLA Ops:
  0.6 0.9 %constant_dynamic-slice_fusion = bf16[1,256,256]{2,1,0:T(8,128)(2,1)S(1)} fusion(bf16[4,256,512]{2,1,0:T(8,128)(2,1)} %samples_far.1, s32[]{:T(128)S(6)} %select_n.37), kind=kLoop, calls=%fused_computation.25 | loop fusion | bytes 262148 | tf_op jit(solution)/shard_map/dynamic_slice | solution.py:145
  1.6 1.4 %bitcast_multiply_fusion = bf16[2,4,256,256]{3,2,1,0:T(8,128)(2,1)S(1)} fusion(bf16[4,256,2,256]{3,2,1,0:T(2,128)(2,1)} %param.4, bf16[2,4]{1,0:T(2,128)(2,1)S(1)} %bitcast.45), kind=kLoop, calls=%fused_computation | loop fusion | flops 524288 | bytes 2097168 | tf_op jit(solution)/shard_map/mul | solution.py:147
  3.1 0.7 %pad_maximum_fusion.1 = bf16[16,32,256]{2,1,0:T(8,128)(2,1)} fusion(bf16[16,16,256]{2,1,0:T(8,128)(2,1)S(1)} %bitcast.43, bf16[16,16,256]{2,1,0:T(8,128)(2,1)S(1)} %bitcast.44), kind=kLoop, calls=%fused_computation.8 | loop fusion | flops 524288 | bytes 524288 | tf_op jit(solution)/shard_map/concatenate | solution.py:152
  3.8 7.6 %all-to-all-start = ((bf16[16,32,256]{2,1,0:T(8,128)(2,1)}), bf16[16,32,256]{2,1,0:T(8,128)(2,1)S(1)}, u32[]{:S(2)}, u32[]{:S(2)}) async-start(bf16[16,32,256]{2,1,0:T(8,128)(2,1)} %pad_maximum_fusion.1), calls=%async_computation | async-start | bytes 524288 | tf_op jit(solution)/shard_map/all_to_all | solution.py:153
  11.4 4.5 %collective-permute-start = (bf16[4,256,256]{2,1,0:T(8,128)(2,1)S(1)}, bf16[4,256,256]{2,1,0:T(8,128)(2,1)S(1)}, u32[]{:S(2)}, u32[]{:S(2)}) collective-permute-start(bf16[4,256,256]{2,1,0:T(8,128)(2,1)S(1)} %get-tuple-element.21.rest_0_), channel_id=1, source_target_pairs={{0,2},{1,7},{8,10},{9,15},{16,18},{17,23},{24,26},{25,31},{32,34},... | collective-permute-start | bytes 1572872 | tf_op jit(solution)/shard_map/ppermute | solution.py:155
  15.9 2.9 %all-to-all-done = bf16[16,32,256]{2,1,0:T(8,128)(2,1)S(1)} async-done(((bf16[16,32,256]{2,1,0:T(8,128)(2,1)}), bf16[16,32,256]{2,1,0:T(8,128)(2,1)S(1)}, u32[]{:S(2)}, u32[]{:S(2)}) %all-to-all-start) | async-done | bytes 262176 | tf_op jit(solution)/shard_map/all_to_all | solution.py:153
  18.9 0.7 %broadcast_in_dim.10 = bf16[8,48,256]{2,1,0:T(8,128)(2,1)} broadcast(bf16[48,256]{1,0:T(8,128)(2,1)S(1)} %pad_maximum_fusion.3), dimensions={1,2} | broadcast | bytes 221184 | tf_op jit(solution)/shard_map/broadcast_in_dim | solution.py:160
  19.6 8.2 %all-to-all-start.1 = ((bf16[8,48,256]{2,1,0:T(8,128)(2,1)}), bf16[8,48,256]{2,1,0:T(8,128)(2,1)S(1)}, u32[]{:S(2)}, u32[]{:S(2)}) async-start(bf16[8,48,256]{2,1,0:T(8,128)(2,1)} %broadcast_in_dim.10), calls=%async_computation.1 | async-start | bytes 393216 | tf_op jit(solution)/shard_map/all_to_all | solution.py:160
  27.8 0.9 %broadcast_select_fusion = bf16[4,256,256]{2,1,0:T(8,128)(2,1)} fusion(bf16[4,256,256]{2,1,0:T(8,128)(2,1)S(1)} %get-tuple-element.21.rest_0_, bf16[4,256,256]{2,1,0:T(8,128)(2,1)S(1)} %collective-permute-done, pred[]{:T(512)S(6)} %eq.5), kind=kLoop, calls=%fused_computation.5 | loop fusion | flops 262144 | bytes 1572865 | tf_op jit(solution)/shard_map/select_n | solution.py:156
  28.6 2.3 %collective-permute-start.1 = (bf16[4,256,256]{2,1,0:T(8,128)(2,1)}, bf16[4,256,256]{2,1,0:T(8,128)(2,1)S(1)}, u32[]{:S(2)}, u32[]{:S(2)}) collective-permute-start(bf16[4,256,256]{2,1,0:T(8,128)(2,1)} %broadcast_select_fusion), channel_id=1, source_target_pairs={{2,4},{7,5},{0,6},{1,3},{10,12},{15,13},{8,14},{9,11},{18,20},{23,... | collective-permute-start | bytes 1572872 | tf_op jit(solution)/shard_map/ppermute | solution.py:157
  30.9 5.6 %all-to-all-done.1 = bf16[8,48,256]{2,1,0:T(8,128)(2,1)S(1)} async-done(((bf16[8,48,256]{2,1,0:T(8,128)(2,1)}), bf16[8,48,256]{2,1,0:T(8,128)(2,1)S(1)}, u32[]{:S(2)}, u32[]{:S(2)}) %all-to-all-start.1) | async-done | bytes 196640 | tf_op jit(solution)/shard_map/all_to_all | solution.py:160
  36.6 1.0 %broadcast_in_dim.14 = bf16[4,4,112,256]{3,2,1,0:T(8,128)(2,1)} broadcast(bf16[4,112,256]{2,1,0:T(8,128)(2,1)S(1)} %pad_maximum_fusion.2), dimensions={1,2,3} | broadcast | bytes 1146880 | tf_op jit(solution)/shard_map/broadcast_in_dim | solution.py:169
  37.6 3.6 %all-to-all-start.2 = ((bf16[16,112,256]{2,1,0:T(8,128)(2,1)}), bf16[16,112,256]{2,1,0:T(8,128)(2,1)S(1)}, u32[]{:S(2)}, u32[]{:S(2)}) async-start(bf16[16,112,256]{2,1,0:T(8,128)(2,1)} %bitcast.17), calls=%async_computation.2 | async-start | bytes 1835008 | tf_op jit(solution)/shard_map/all_to_all | solution.py:170
  41.3 0.1 add_select_fusion
  41.4 3.4 %collective-permute-start.2 = (bf16[4,256,256]{2,1,0:T(8,128)(2,1)S(1)}, bf16[4,256,256]{2,1,0:T(8,128)(2,1)S(1)}, u32[]{:S(2)}, u32[]{:S(2)}) collective-permute-start(bf16[4,256,256]{2,1,0:T(8,128)(2,1)S(1)} %add_select_fusion), channel_id=1, source_target_pairs={{0,1},{1,0},{2,3},{3,2},{4,5},{5,4},{6,7},{7,6},{8,9},{9,8},{10,11... | collective-permute-start | bytes 1572872 | tf_op jit(solution)/shard_map/ppermute | solution.py:19
  44.8 0.1 copy.9
  44.9 0.1 reshape.22
  45.0 7.8 %all-to-all-done.2.got = bf16[16,112,256]{2,1,0:T(8,128)(2,1)S(1)} async-done(((bf16[16,112,256]{2,1,0:T(8,128)(2,1)}), bf16[16,112,256]{2,1,0:T(8,128)(2,1)S(1)}, u32[]{:S(2)}, u32[]{:S(2)}) %all-to-all-start.2) | async-done | bytes 917536 | tf_op jit(solution)/shard_map/all_to_all | solution.py:170
  52.8 5.2 %collective-permute-start.3 = (bf16[16,16,256]{2,1,0:T(8,128)(2,1)S(1)}, bf16[16,16,256]{2,1,0:T(8,128)(2,1)S(1)}, u32[]{:S(2)}, u32[]{:S(2)}) collective-permute-start(bf16[16,16,256]{2,1,0:T(8,128)(2,1)S(1)} %slice.67), channel_id=1, source_target_pairs={{0,1},{1,0},{2,3},{3,2},{4,5},{5,4},{6,7},{7,6},{8,9},{9,8},{10,11... | collective-permute-start | bytes 393224 | tf_op jit(solution)/shard_map/ppermute | solution.py:19
  58.1 0.1 collective-permute-start.4
  58.3 0.7 %copy-done = bf16[2,256,256]{2,1,0:T(8,128)(2,1)S(1)} copy-done((bf16[2,256,256]{2,1,0:T(8,128)(2,1)S(1)}, bf16[2,256,256]{2,1,0:T(8,128)(2,1)}, u32[]{:S(2)}) %copy-start) | copy-done | bytes 262168
  59.1 1.8 %head.1 = (bf16[1024,512]{1,0:T(8,128)(2,1)S(1)}, bf16[2,256,256]{2,1,0:T(8,128)(2,1)S(1)}, bf16[4,256,512]{2,1,0:T(8,128)(2,1)S(1)}) custom-call(s32[11]{0:T(128)S(1)} %pad_add_fusion.place, bf16[6,256,256]{2,1,0:T(8,128)(2,1)S(1)} %pad_maximum_fusion.rows0, bf16[4,256,256]{2,1,0:T(8,128)(2,1)S(1)} %get-tuple-element.22.rows1, ...), custom_call_target="tpu_custom_call" | custom-call | tf_op jit(solution)/shard_map/head/pallas_call | solution.py:186
  60.9 3.0 %finish.1 = (bf16[2,4,256,256]{3,2,1,0:T(8,128)(2,1)S(1)}, bf16[4,256,512]{2,1,0:T(8,128)(2,1)}) custom-call(s32[11]{0:T(128)S(1)} %pad_add_fusion.place, bf16[6,256,256]{2,1,0:T(8,128)(2,1)S(1)} %pad_maximum_fusion.rows0, bf16[1024,512]{1,0:T(8,128)(2,1)S(1)} %get-tuple-element.11.lrow, bf16[2,256,256]{2,1,0:T(8,128)(2,1)S(1)} %get-tuple-element.12.lead, ...), custom_call_target="tpu_custom_call" | custom-call | tf_op jit(solution)/shard_map/finish/pallas_call | solution.py:199
  63.9 2.0 %copy.12 = bf16[4,256,2,256]{3,2,1,0:T(2,128)(2,1)} copy(bf16[4,256,2,256]{3,1,0,2:T(8,128)(2,1)S(1)} %bitcast.40) | data formatting | bytes 2097152
  (28 shorter events, 0.5 us)
Async XLA Ops:
  0.6 0.9 %copy-start.1 = (s32[4,1,2,1]{0,3,2,1:T(1,128)S(1)}, s32[4,1,2,1]{0,3,2,1:T(1,128)}, u32[]{:S(2)}) copy-start(s32[4,1,2,1]{0,3,2,1:T(1,128)} %param.5) | copy-start | bytes 100
  3.8 15.0 %all-to-all-start = ((bf16[16,32,256]{2,1,0:T(8,128)(2,1)}), bf16[16,32,256]{2,1,0:T(8,128)(2,1)S(1)}, u32[]{:S(2)}, u32[]{:S(2)}) async-start(bf16[16,32,256]{2,1,0:T(8,128)(2,1)} %pad_maximum_fusion.1), calls=%async_computation | async-start | bytes 524288 | tf_op jit(solution)/shard_map/all_to_all | solution.py:153
  11.4 16.3 %collective-permute-start = (bf16[4,256,256]{2,1,0:T(8,128)(2,1)S(1)}, bf16[4,256,256]{2,1,0:T(8,128)(2,1)S(1)}, u32[]{:S(2)}, u32[]{:S(2)}) collective-permute-start(bf16[4,256,256]{2,1,0:T(8,128)(2,1)S(1)} %get-tuple-element.21.rest_0_), channel_id=1, source_target_pairs={{0,2},{1,7},{8,10},{9,15},{16,18},{17,23},{24,26},{25,31},{32,34},... | collective-permute-start | bytes 1572872 | tf_op jit(solution)/shard_map/ppermute | solution.py:155
  19.6 16.9 %all-to-all-start.1 = ((bf16[8,48,256]{2,1,0:T(8,128)(2,1)}), bf16[8,48,256]{2,1,0:T(8,128)(2,1)S(1)}, u32[]{:S(2)}, u32[]{:S(2)}) async-start(bf16[8,48,256]{2,1,0:T(8,128)(2,1)} %broadcast_in_dim.10), calls=%async_computation.1 | async-start | bytes 393216 | tf_op jit(solution)/shard_map/all_to_all | solution.py:160
  28.6 12.7 %collective-permute-start.1 = (bf16[4,256,256]{2,1,0:T(8,128)(2,1)}, bf16[4,256,256]{2,1,0:T(8,128)(2,1)S(1)}, u32[]{:S(2)}, u32[]{:S(2)}) collective-permute-start(bf16[4,256,256]{2,1,0:T(8,128)(2,1)} %broadcast_select_fusion), channel_id=1, source_target_pairs={{2,4},{7,5},{0,6},{1,3},{10,12},{15,13},{8,14},{9,11},{18,20},{23,... | collective-permute-start | bytes 1572872 | tf_op jit(solution)/shard_map/ppermute | solution.py:157
  37.6 15.2 %all-to-all-start.2 = ((bf16[16,112,256]{2,1,0:T(8,128)(2,1)}), bf16[16,112,256]{2,1,0:T(8,128)(2,1)S(1)}, u32[]{:S(2)}, u32[]{:S(2)}) async-start(bf16[16,112,256]{2,1,0:T(8,128)(2,1)} %bitcast.17), calls=%async_computation.2 | async-start | bytes 1835008 | tf_op jit(solution)/shard_map/all_to_all | solution.py:170
  41.4 16.8 %collective-permute-start.2 = (bf16[4,256,256]{2,1,0:T(8,128)(2,1)S(1)}, bf16[4,256,256]{2,1,0:T(8,128)(2,1)S(1)}, u32[]{:S(2)}, u32[]{:S(2)}) collective-permute-start(bf16[4,256,256]{2,1,0:T(8,128)(2,1)S(1)} %add_select_fusion), channel_id=1, source_target_pairs={{0,1},{1,0},{2,3},{3,2},{4,5},{5,4},{6,7},{7,6},{8,9},{9,8},{10,11... | collective-permute-start | bytes 1572872 | tf_op jit(solution)/shard_map/ppermute | solution.py:19
  52.8 6.3 %collective-permute-start.3 = (bf16[16,16,256]{2,1,0:T(8,128)(2,1)S(1)}, bf16[16,16,256]{2,1,0:T(8,128)(2,1)S(1)}, u32[]{:S(2)}, u32[]{:S(2)}) collective-permute-start(bf16[16,16,256]{2,1,0:T(8,128)(2,1)S(1)} %slice.67), channel_id=1, source_target_pairs={{0,1},{1,0},{2,3},{3,2},{4,5},{5,4},{6,7},{7,6},{8,9},{9,8},{10,11... | collective-permute-start | bytes 393224 | tf_op jit(solution)/shard_map/ppermute | solution.py:19
  58.0 1.0 %copy-start = (bf16[2,256,256]{2,1,0:T(8,128)(2,1)S(1)}, bf16[2,256,256]{2,1,0:T(8,128)(2,1)}, u32[]{:S(2)}) copy-start(bf16[2,256,256]{2,1,0:T(8,128)(2,1)} %param.6) | copy-start | bytes 786436
  58.1 2.9 %collective-permute-start.4 = (bf16[16,64,256]{2,1,0:T(8,128)(2,1)S(1)}, bf16[16,64,256]{2,1,0:T(8,128)(2,1)S(1)}, u32[]{:S(2)}, u32[]{:S(2)}) collective-permute-start(bf16[16,64,256]{2,1,0:T(8,128)(2,1)S(1)} %slice.68), channel_id=1, source_target_pairs={{0,1},{1,0},{2,3},{3,2},{4,5},{5,4},{6,7},{7,6},{8,9},{9,8},{10,11... | collective-permute-start | bytes 1572872 | tf_op jit(solution)/shard_map/ppermute | solution.py:19
